TPU v7x, 32 devices: a whole 2x2x4 slice. The times are simulated.
32 devices in a mesh: seq: 16 (over z, y, x), head: 2 (over core).
Axes of the slice: x: 2, y: 2, z: 4, core: 2. Of those that a mesh axis runs over, the one named last changes fastest.
Arguments:
- query_rows: bfloat16 [16384, 2048], P('seq', 'head'), may hold values from -6 to 6
- key_rows: bfloat16 [16384, 2048], P('seq', 'head'), may hold values from -6 to 6
- value_rows: bfloat16 [16384, 2048], P('seq', 'head'), may hold values from -16 to 16
- level_codes: int32 [16, 20, 16], P('seq', None, 'head'), may hold values from 1 to 8
- norm_gain: float32 [2048], P('head'), may hold values from 0.1 to 1.9
- upstream: bfloat16 [16384, 2048], P('seq', 'head'), may hold values from -6 to 6
Outputs:
- normed: bfloat16 [16384, 2048], P('seq', 'head')
- query_gradient: bfloat16 [16384, 2048], P('seq', 'head')
- key_gradient: bfloat16 [16384, 2048], P('seq', 'head')
- value_gradient: bfloat16 [16384, 2048], P('seq', 'head')
All inputs are finite; a program needn't handle non-finite values.
Results may differ from a plain program's by a relative error of at most 0.0059.
Values sent between devices are 32-bit elements; how exact they have to be, the bound alone decides.
No kernel may reach another device: no remote copies, remote signals or barrier semaphores. Data moves between devices by JAX's collectives and lax.ppermute only.
A program may use at most 128 MiB of HBM per device.

v0:
```python
import functools
import math

import jax
import jax.numpy as jnp
from jax import lax
from jax.experimental import pallas as pl
from jax.experimental.pallas import tpu as pltpu
from jax.sharding import PartitionSpec as P


D = 128
GROUP = 1024
CHUNK = 128
F32 = jnp.float32
BF16 = jnp.bfloat16


def dot(a, b, ca, cb):
    return lax.dot_general(a, b, (((ca,), (cb,)), ((), ())), preferred_element_type=F32)


def level_scale(level_codes):
    levels = jnp.arange(level_codes.shape[1], dtype=F32)
    factor = jnp.where(levels > 0, jnp.exp2(-(levels - 1.0) * 0.5), 1.0) * 0.25
    return level_codes.astype(F32) * factor[None, :, None] * D ** (-0.5)


def log2(n):
    return n.bit_length() - 1


def weight(codes, g, level, h):
    factor = (2.0 ** (-(level - 1) / 2) if level else 1.0) / 4 / math.sqrt(D)
    return codes[g, level, h].astype(F32) * factor


def tile_weights(codes, g, h, transposed=False):
    rows = lax.broadcasted_iota(jnp.int32, (CHUNK, CHUNK), 0)
    cols = lax.broadcasted_iota(jnp.int32, (CHUNK, CHUNK), 1)
    apart = rows ^ cols
    w = jnp.full((CHUNK, CHUNK), weight(codes, g, 0, h), F32)
    for level in range(1, log2(CHUNK) + 1):
        w = jnp.where(apart >= (1 << (level - 1)), weight(codes, g, level, h), w)
    return jnp.where(rows <= cols if transposed else rows >= cols, w, 0.0)


def chunk_maps(states, codes, h, reverse=False):
    count = len(states)
    per_group = GROUP // CHUNK
    first = log2(CHUNK) + 1
    maps = [None] * count

    def add(a, b):
        return b if a is None else a + b

    if not reverse:
        blocks = list(states)
        for bit in range(log2(count)):
            for i in range(count):
                if (i >> bit) & 1:
                    maps[i] = add(maps[i], weight(codes, i // per_group, first + bit, h) * blocks[(i >> bit) ^ 1])
            blocks = [blocks[2 * a] + blocks[2 * a + 1] for a in range(len(blocks) // 2)]
    else:
        for bit in range(log2(count)):
            size = 1 << bit
            for block in range(1, count >> bit, 2):
                total = None
                for i in range(block * size, (block + 1) * size):
                    total = add(total, weight(codes, i // per_group, first + bit, h) * states[i])
                for i in range((block - 1) * size, block * size):
                    maps[i] = add(maps[i], total)
    return maps


def bf16_map(m):
    return jnp.zeros((D, D), BF16) if m is None else m.astype(BF16)


def chunk_rows(tokens):
    return [slice(i * CHUNK, (i + 1) * CHUNK) for i in range(tokens // CHUNK)]


def col(h):
    return pl.ds(pl.multiple_of(h * D, D), D)


def cat(a, b, axis):
    return jnp.concatenate([a, b], axis)


def state_kernel(parts, each, far, pref, codes, k_hbm, v_hbm, *refs):
    outs, (k, v, state, sems) = refs[:parts], refs[parts:]
    width = each * D
    copies = []
    for n in range(parts):
        cols = slice(n * width, (n + 1) * width)
        pair = [
            pltpu.make_async_copy(k_hbm.at[:, cols], k.at[n], sems.at[0, n]),
            pltpu.make_async_copy(v_hbm.at[:, cols], v.at[n], sems.at[1, n]),
        ]
        for c in pair:
            c.start()
        copies.append(pair)
    first, bits = far
    p = pref[0]
    for m, out in enumerate(outs):
        row = width
        for level in range(bits):
            for i in range(each):
                out[row : row + 1, :] = jnp.full((1, D), weight(codes, 0, first + level, (m ^ p) * each + i), F32)
                row += 1
        if row < out.shape[0]:
            out[row:, :] = jnp.zeros((out.shape[0] - row, D), F32)
    for n in range(parts):
        for c in copies[n]:
            c.wait()
        for i in range(each):
            cols = slice(i * D, (i + 1) * D)
            state[n, cols, :] = dot(k[n, :, cols], v[n, :, cols], 0, 0)
    for m, out in enumerate(outs):
        out[:width, :] = state[m ^ p]


def inside_kernel(pair, codes, q, k, v, part, maps, att_t, *tiles):
    rows = chunk_rows(q.shape[0])
    per_group = GROUP // CHUNK

    @pl.loop(0, q.shape[1] // D // pair)
    def _(step):
        heads = [step * pair + n for n in range(pair)]
        for n, h in enumerate(heads):
            c = col(h)
            for i, r in enumerate(rows):
                if i % per_group == 0:
                    w = tile_weights(codes, i // per_group, h)
                tiles[n][r, :] = (w * dot(q[r, c], k[r, c], 1, 1)).astype(BF16)
            for i, r in enumerate(rows):
                if i % per_group == 0:
                    w = tile_weights(codes, i // per_group, h, transposed=True)
                att_t[r, c] = (w * dot(k[r, c], q[r, c], 1, 1)).astype(BF16)
            reads = chunk_maps([dot(k[r, c], v[r, c], 0, 0) for r in rows], codes, h)
            for i in range(len(rows)):
                maps[h, i] = bf16_map(reads[i])
        for n, h in enumerate(heads):
            c = col(h)
            for i, r in enumerate(rows):
                part[r, c] = dot(cat(tiles[n][r, :], q[r, c], 1), cat(v[r, c], maps[h, i], 0), 1, 0)


def scale_kernel(u, gain, scaled):
    @pl.loop(0, u.shape[0] // CHUNK)
    def _(i):
        r = pl.ds(pl.multiple_of(i * CHUNK, CHUNK), CHUNK)
        scaled[r, :] = u[r, :].astype(F32) * gain[...]


def sort_pieces(pieces, each, p, out):
    for m, piece in enumerate(pieces):
        for g in range(piece.shape[0]):
            for i in range(each):
                out[(m ^ p) * each + i, g] = piece[g, i * D : (i + 1) * D, :].astype(out.dtype)


def attend_kernel(pieces, each, pref, q, part, scaled, *refs):
    far, (att, stats, maps) = refs[:pieces], refs[pieces:]
    sort_pieces(far, each, pref[0], maps)
    heads = q.shape[1] // D

    @pl.loop(0, q.shape[0] // CHUNK)
    def _(step):
        r = pl.ds(pl.multiple_of(step * CHUNK, CHUNK), CHUNK)
        g = (step * CHUNK) // GROUP
        squares = dots = None
        for h in range(heads):
            c = slice(h * D, (h + 1) * D)
            a = part[r, c] + dot(q[r, c], maps[h, g], 1, 0)
            att[r, c] = a
            squares = a * a if h == 0 else squares + a * a
            dots = scaled[r, c] * a if h == 0 else dots + scaled[r, c] * a
        stats[0:1, r] = jnp.sum(squares.T, axis=0, keepdims=True)
        stats[1:2, r] = jnp.sum(dots.T, axis=0, keepdims=True)


def token_factors(stats, features, inv_s, beta_s):
    @pl.loop(0, stats.shape[1] // CHUNK)
    def _(step):
        r = pl.ds(pl.multiple_of(step * CHUNK, CHUNK), CHUNK)
        inv = lax.rsqrt(stats[0:1, r] / features + 1e-06)
        inv_s[r, :] = jnp.broadcast_to(inv, (CHUNK, CHUNK)).T
        if beta_s is not None:
            beta = inv * inv * inv * stats[1:2, r] / features
            beta_s[r, :] = jnp.broadcast_to(beta, (CHUNK, CHUNK)).T


def grad_kernel(pieces, each, features, pref, q, att, scaled, stats, grad, *refs):
    outs, (inv, beta, sums) = refs[:pieces], refs[pieces:]
    token_factors(stats, features, inv, beta)
    groups = q.shape[0] // GROUP

    @pl.loop(0, q.shape[1] // D)
    def _(h):
        c = col(h)
        for r in chunk_rows(q.shape[0]):
            grad[r, c] = (inv[r, :] * scaled[r, c] - att[r, c] * beta[r, :]).astype(BF16)
        for g in range(groups):
            r = slice(g * GROUP, (g + 1) * GROUP)
            sums[h, g] = dot(q[r, c], grad[r, c], 0, 0)

    for m, out in enumerate(outs):
        for g in range(groups):
            for i in range(each):
                out[g, i * D : (i + 1) * D, :] = sums[(m ^ pref[0]) * each + i, g]


def query_kernel(pieces, each, features, pref, codes, k, v, grad, maps, att, stats, gain, *refs):
    far, (dq, normed, reach, inv, tiles, outer) = refs[:pieces], refs[pieces:]
    h = pl.program_id(0)

    @pl.when(h == 0)
    def _():
        token_factors(stats, features, inv, None)
        sort_pieces(far, each, pref[0], reach)

    c = col(h)
    rows = chunk_rows(k.shape[0])
    per_group = GROUP // CHUNK
    for i, r in enumerate(rows):
        if i % per_group == 0:
            w = tile_weights(codes, i // per_group, h)
        to = (maps[h, i].astype(F32) + reach[h, i // per_group]).astype(BF16)
        y = dot(grad[r, c], cat(v[r, c], to, 0), 1, 1)
        tiles[r, :] = (w * y[:, :D]).astype(BF16)
        outer[r, :] = y[:, D:]
    for r in rows:
        normed[r, :] = (att[r, c] * inv[r, :] * gain[:, c]).astype(BF16)
    for r in rows:
        dq[r, :] = (dot(tiles[r, :], k[r, c], 1, 0) + outer[r, :]).astype(BF16)


def key_kernel(codes, q, v, grad, key_in, readers, tiles, outer):
    rows = chunk_rows(q.shape[0])
    per_group = GROUP // CHUNK

    @pl.loop(0, q.shape[1] // D)
    def _(h):
        c = col(h)
        sums = chunk_maps([dot(q[r, c], grad[r, c], 0, 0) for r in rows], codes, h, reverse=True)
        for i in range(len(rows)):
            readers[h, i] = bf16_map(sums[i])
        for i, r in enumerate(rows):
            if i % per_group == 0:
                w = tile_weights(codes, i // per_group, h, transposed=True)
            y = dot(v[r, c], cat(grad[r, c], readers[h, i], 0), 1, 1)
            tiles[r, :] = (w * y[:, :D]).astype(BF16)
            outer[r, :] = y[:, D:]
        for r in rows:
            key_in[r, c] = dot(tiles[r, :], q[r, c], 1, 0) + outer[r, :]


def value_kernel(k, grad, att_t, readers, value_in):
    rows = chunk_rows(k.shape[0])

    @pl.loop(0, k.shape[1] // D)
    def _(h):
        c = col(h)
        for i, r in enumerate(rows):
            value_in[r, c] = dot(cat(att_t[r, c], k[r, c], 1), cat(grad[r, c], readers[h, i], 0), 1, 0)


def outer_kernel(pieces, each, pref, k, v, key_in, value_in, *refs):
    far, (dk, dv, maps) = refs[:pieces], refs[pieces:]
    step = pl.program_id(0)

    @pl.when(step == 0)
    def _():
        for m, piece in enumerate(far):
            for i in range(each):
                maps[(m ^ pref[0]) * each + i] = piece[i * D : (i + 1) * D, :].astype(BF16)

    r = pl.ds(pl.multiple_of(step * CHUNK, CHUNK), CHUNK)
    for h in range(k.shape[1] // D):
        c = slice(h * D, (h + 1) * D)
        dk[:, c] = (key_in[r, c] + dot(v[r, c], maps[h], 1, 1)).astype(BF16)
        dv[:, c] = (value_in[r, c] + dot(k[r, c], maps[h], 1, 0)).astype(BF16)


def exchange(x, axis, distance):
    count = lax.axis_size(axis)
    return lax.ppermute(x, axis, [(i, i ^ distance) for i in range(count)])


def sum_over(x, axis):
    count = lax.axis_size(axis)
    if count == 2:
        return x + exchange(x, axis, 1)
    return lax.psum(x, axis)


class Far:
    def __init__(self, groups, heads):
        self.count = lax.axis_size("seq")
        self.me = lax.axis_index("seq")
        self.inner = min(4, self.count)
        self.inner_bits = log2(self.inner)
        self.bits = log2(self.count)
        self.groups = groups
        self.rows = heads * D // self.inner
        self.seg = math.gcd(D, self.rows)
        self.segs = self.rows // self.seg
        used = groups * self.bits * self.segs
        self.extra = -(-used // 8) * 8
        self.p = self.me % self.inner
        self.outer = self.me // self.inner
        self.fast = self.rows % D == 0 and groups == 1

    def take(self, ext, m):
        used = self.groups * self.bits * self.segs
        return ext[m][:used].reshape(self.groups, self.bits, self.segs, 1, D)

    def forward(self, sends):
        got = [sends[0]] + [exchange(sends[m], "seq", m) for m in range(1, self.inner)]
        state = [x[: self.rows].reshape(self.segs, self.seg, D) for x in got]
        ext = [x[self.rows :] for x in got]
        total = functools.reduce(lambda a, b: a + b, state)
        outer = []
        for bit in range(self.bits - self.inner_bits):
            came = exchange(total.reshape(self.rows, D), "seq", self.inner << bit).reshape(total.shape)
            outer.append(came)
            total = total + came
        back = []
        for m in range(self.inner):
            w = self.take(ext, m)
            acc = jnp.zeros((self.groups, self.segs, self.seg, D), F32)
            for other in range(self.inner):
                if other != m:
                    reads = ((self.p ^ other) < (self.p ^ m)).astype(F32)
                    acc = acc + (w[:, (m ^ other).bit_length() - 1] * reads) * state[other][None]
            for bit, came in enumerate(outer):
                reads = ((self.outer >> bit) & 1).astype(F32)
                acc = acc + (w[:, self.inner_bits + bit] * reads) * came[None]
            back.append(acc.reshape(self.groups, self.rows, D))
        return [back[0]] + [exchange(back[m], "seq", m) for m in range(1, self.inner)], ext

    def backward(self, sends, ext):
        got = [sends[0]] + [exchange(sends[m], "seq", m) for m in range(1, self.inner)]
        grads = [x.reshape(self.groups, self.segs, self.seg, D) for x in got]
        weights = [self.take(ext, m) for m in range(self.inner)]

        def read_at(m, level):
            return jnp.sum(weights[m][:, level] * grads[m], axis=0)

        total = None
        for bit in reversed(range(self.bits - self.inner_bits)):
            reads = ((self.outer >> bit) & 1).astype(F32)
            send = reads * functools.reduce(
                lambda a, b: a + b, [read_at(m, self.inner_bits + bit) for m in range(self.inner)]
            )
            if total is not None:
                send = send + total
            came = exchange(send.reshape(self.rows, D), "seq", self.inner << bit).reshape(send.shape)
            total = came if total is None else total + came
        back = []
        for m in range(self.inner):
            acc = total if total is not None else jnp.zeros((self.segs, self.seg, D), F32)
            for other in range(self.inner):
                if other != m:
                    reads = ((self.p ^ other) > (self.p ^ m)).astype(F32)
                    acc = acc + reads * read_at(other, (m ^ other).bit_length() - 1)
            back.append(acc.reshape(self.rows, D))
        return [back[0]] + [exchange(back[m], "seq", m) for m in range(1, self.inner)]

    def gather_pieces(self, pieces):
        stacked = jnp.stack(pieces, 0)
        order = self.p ^ jnp.arange(self.inner)
        return jnp.moveaxis(jnp.take(stacked, order, axis=0), 0, -3).reshape(pieces[0].shape[:-2] + (self.inner * self.rows, D))

    def split_pieces(self, whole):
        parts = whole.reshape(whole.shape[:-2] + (self.inner, self.rows, D))
        return [lax.dynamic_index_in_dim(parts, self.p ^ m, parts.ndim - 3, keepdims=False) for m in range(self.inner)]


def local(query_rows, key_rows, value_rows, level_codes, norm_gain, upstream):
    tokens, width = query_rows.shape
    groups = tokens // GROUP
    heads = width // D
    features = width * lax.axis_size("head")
    chunks = tokens // CHUNK
    far = Far(groups, heads)
    first_far = log2(GROUP) + log2(groups) + 1
    pieces, each = (far.inner, heads // far.inner) if far.fast else (1, heads)
    pref = (far.p if far.fast else jnp.zeros_like(far.p)).astype(jnp.int32).reshape(1)
    gain = norm_gain.reshape(1, width)
    pair = 2 if heads % 2 == 0 else 1

    smem = pl.BlockSpec(memory_space=pltpu.SMEM)
    vmem = pl.BlockSpec(memory_space=pltpu.VMEM)
    wide = jax.ShapeDtypeStruct((tokens, width), F32)
    narrow = jax.ShapeDtypeStruct((tokens, width), BF16)
    tile16 = pltpu.VMEM((tokens, D), BF16)
    tile32 = pltpu.VMEM((tokens, D), F32)
    unit = tokens * D * D * heads

    def call(kernel, units, ins, outs, scratch=(), limit=12, **kw):
        kw.setdefault("out_specs", [vmem] * len(outs))
        return pl.pallas_call(
            kernel,
            in_specs=ins,
            out_shape=outs,
            scratch_shapes=list(scratch),
            compiler_params=pltpu.CompilerParams(vmem_limit_bytes=limit << 20),
            cost_estimate=pl.CostEstimate(flops=2 * units * unit, bytes_accessed=tokens * width * 8, transcendentals=0),
            **kw,
        )

    if far.fast:
        sends = call(
            functools.partial(state_kernel, pieces, each, (first_far, far.bits)),
            1,
            [smem, smem] + [pl.BlockSpec(memory_space=pltpu.HBM)] * 2,
            [jax.ShapeDtypeStruct((far.rows + far.extra, D), F32)] * pieces,
            [pltpu.VMEM((pieces, tokens, each * D), BF16)] * 2
            + [pltpu.VMEM((pieces, each * D, D), F32), pltpu.SemaphoreType.DMA((2, pieces))],
            limit=58,
        )(pref, level_codes, key_rows, value_rows)
    else:
        state = jnp.einsum(
            "she,shf->hef",
            key_rows.reshape(tokens, heads, D),
            value_rows.reshape(tokens, heads, D),
            preferred_element_type=F32,
        ).reshape(heads * D, D)
        lam = level_scale(level_codes)
        per_row = jnp.repeat(lam[:, first_far : first_far + far.bits, :], D // far.seg, axis=2)
        sends = []
        for m, piece in enumerate(far.split_pieces(state)):
            w = lax.dynamic_slice_in_dim(per_row, (far.p ^ m) * far.segs, far.segs, 2).reshape(-1, 1)
            w = jnp.pad(w, ((0, far.extra - w.shape[0]), (0, 0)))
            sends.append(jnp.concatenate([piece, jnp.broadcast_to(w, (far.extra, D))], 0))

    part, maps, att_t = call(
        functools.partial(inside_kernel, pair),
        5,
        [smem, vmem, vmem, vmem],
        [wide, jax.ShapeDtypeStruct((heads, chunks, D, D), BF16), narrow],
        [tile16] * pair,
    )(level_codes, query_rows, key_rows, value_rows)
    scaled = call(scale_kernel, 1, [vmem, vmem], [wide])(upstream, gain)[0]

    far_maps, ext = far.forward(sends)
    if not far.fast:
        far_maps = [far.gather_pieces(far_maps)]

    att, stats = call(
        functools.partial(attend_kernel, pieces, each),
        1,
        [smem] + [vmem] * (3 + pieces),
        [wide, jax.ShapeDtypeStruct((2, tokens), F32)],
        [pltpu.VMEM((heads, groups, D, D), BF16)],
    )(pref, query_rows, part, scaled, *far_maps)

    stats = sum_over(stats, "head")

    grad, *map_grads = call(
        functools.partial(grad_kernel, pieces, each, features),
        1,
        [smem] + [vmem] * 4,
        [narrow] + [jax.ShapeDtypeStruct((groups, each * D, D), F32)] * pieces,
        [tile32, tile32, pltpu.VMEM((heads, groups, D, D), F32)],
    )(pref, query_rows, att, scaled, stats)

    if not far.fast:
        map_grads = far.split_pieces(map_grads[0])

    query_gradient, normed = call(
        functools.partial(query_kernel, pieces, each, features),
        3,
        [smem, smem] + [vmem] * (7 + pieces),
        [narrow, narrow],
        [pltpu.VMEM((heads, groups, D, D), F32), tile32, tile16, tile32],
        grid=(heads,),
        out_specs=[pl.BlockSpec((tokens, D), lambda h: (0, h))] * 2,
    )(pref, level_codes, key_rows, value_rows, grad, maps, att, stats, gain, *far_maps)
    key_in, readers = call(
        key_kernel, 4, [smem] + [vmem] * 3, [wide, jax.ShapeDtypeStruct((heads, chunks, D, D), BF16)], [tile16, tile32]
    )(level_codes, query_rows, value_rows, grad)
    value_in = call(value_kernel, 2, [vmem] * 4, [wide])(key_rows, grad, att_t, readers)[0]

    state_grads = far.backward(map_grads, ext)
    if not far.fast:
        state_grads = [far.gather_pieces(state_grads)]

    key_gradient, value_gradient = call(
        functools.partial(outer_kernel, pieces, each),
        2,
        [smem] + [vmem] * (4 + pieces),
        [narrow, narrow],
        [pltpu.VMEM((heads, D, D), BF16)],
        grid=(tokens // CHUNK,),
        out_specs=[pl.BlockSpec((CHUNK, width), lambda i: (i, 0))] * 2,
    )(pref, key_rows, value_rows, key_in, value_in, *state_grads)
    return (normed, query_gradient, key_gradient, value_gradient)


def solution(mesh):
    return jax.shard_map(
        local,
        mesh=mesh,
        in_specs=(
            P("seq", "head"),
            P("seq", "head"),
            P("seq", "head"),
            P("seq", None, "head"),
            P("head"),
            P("seq", "head"),
        ),
        out_specs=(P("seq", "head"), P("seq", "head"), P("seq", "head"), P("seq", "head")),
        check_vma=False,
    )
```

profile of v0, /device:TPU:0, one launch (start us, length us, event | category | flops | bytes accessed | tf_op | source)
XLA Modules:
  0.0 107.5 jit_solution(10576236413129459362)
XLA Ops:
  2.0 4.3 %shard_map.95 = (f32[264,128]{1,0:T(8,128)}, f32[264,128]{1,0:T(8,128)}, f32[264,128]{1,0:T(8,128)}, f32[264,128]{1,0:T(8,128)}) custom-call(s32[1]{0:T(128)} %bitcast.pref, s32[1,20,8]{2,1,0:T(8,128)} %copy.18.codes, bf16[1024,1024]{1,0:T(8,128)(2,1)} %k.7, bf16[1024,1024]{1,0:T(8,128)(2,1)} %v.7), custom_call_target="tpu_custom_call" | custom-call | flops 268435456 | bytes 8388608 | tf_op jit(solution)/shard_map/pallas_call | solution.py:417
  6.3 3.0 %collective-permute-start = (f32[264,128]{1,0:T(8,128)}, f32[264,128]{1,0:T(8,128)S(1)}, u32[]{:S(2)}, u32[]{:S(2)}) collective-permute-start(f32[264,128]{1,0:T(8,128)} %get-tuple-element.26), channel_id=1, source_target_pairs={{0,2},{2,0},{4,6},{6,4},{8,10},{10,8},{12,14},{14,12},{16,18},{18,... | collective-permute-start | bytes 405512 | tf_op jit(solution)/shard_map/ppermute | solution.py:290
  11.6 2.1 %collective-permute-done = f32[264,128]{1,0:T(8,128)S(1)} collective-permute-done((f32[264,128]{1,0:T(8,128)}, f32[264,128]{1,0:T(8,128)S(1)}, u32[]{:S(2)}, u32[]{:S(2)}) %collective-permute-start) | collective-permute-done | bytes 135200 | tf_op jit(solution)/shard_map/ppermute | solution.py:290
  13.7 3.9 %collective-permute-done.1 = f32[264,128]{1,0:T(8,128)S(1)} collective-permute-done((f32[264,128]{1,0:T(8,128)}, f32[264,128]{1,0:T(8,128)S(1)}, u32[]{:S(2)}, u32[]{:S(2)}) %collective-permute-start.1) | collective-permute-done | bytes 135200 | tf_op jit(solution)/shard_map/ppermute | solution.py:290
  18.5 1.6 %collective-permute-start.3 = (f32[256,128]{1,0:T(8,128)S(1)}, f32[256,128]{1,0:T(8,128)S(1)}, u32[]{:S(2)}, u32[]{:S(2)}) collective-permute-start(f32[256,128]{1,0:T(8,128)S(1)} %add_add_fusion), channel_id=1, source_target_pairs={{0,8},{2,10},{4,12},{6,14},{8,0},{10,2},{12,4},{14,6},{16,24},{18,... | collective-permute-start | bytes 393224 | tf_op jit(solution)/shard_map/ppermute | solution.py:290
  20.2 3.4 %collective-permute-done.3 = f32[256,128]{1,0:T(8,128)S(1)} collective-permute-done((f32[256,128]{1,0:T(8,128)S(1)}, f32[256,128]{1,0:T(8,128)S(1)}, u32[]{:S(2)}, u32[]{:S(2)}) %collective-permute-start.3) | collective-permute-done | bytes 131104 | tf_op jit(solution)/shard_map/ppermute | solution.py:290
  23.5 2.7 %collective-permute-start.4 = (f32[256,128]{1,0:T(8,128)S(1)}, f32[256,128]{1,0:T(8,128)S(1)}, u32[]{:S(2)}, u32[]{:S(2)}) collective-permute-start(f32[256,128]{1,0:T(8,128)S(1)} %add.237), channel_id=1, source_target_pairs={{0,16},{2,18},{4,20},{6,22},{8,24},{10,26},{12,28},{14,30},{16,0},... | collective-permute-start | bytes 393224 | tf_op jit(solution)/shard_map/ppermute | solution.py:290
  26.2 4.7 %collective-permute-done.4 = f32[256,128]{1,0:T(8,128)S(1)} collective-permute-done((f32[256,128]{1,0:T(8,128)S(1)}, f32[256,128]{1,0:T(8,128)S(1)}, u32[]{:S(2)}, u32[]{:S(2)}) %collective-permute-start.4) | collective-permute-done | bytes 131104 | tf_op jit(solution)/shard_map/ppermute | solution.py:290
  37.6 2.0 %copy-done.3 = f32[1024,1024]{1,0:T(8,128)} copy-done((f32[1024,1024]{1,0:T(8,128)}, f32[1024,1024]{1,0:T(8,128)S(1)}, u32[]{:S(2)}) %copy-start.3) | copy-done | bytes 4194328
  39.6 1.6 %copy-done.1 = bf16[1024,1024]{1,0:T(8,128)(2,1)S(1)} copy-done((bf16[1024,1024]{1,0:T(8,128)(2,1)S(1)}, bf16[1024,1024]{1,0:T(8,128)(2,1)}, u32[]{:S(2)}) %copy-start.1) | copy-done | bytes 2097176
  42.8 6.1 %shard_map.93 = (f32[1024,1024]{1,0:T(8,128)S(1)}, bf16[8,8,128,128]{3,2,1,0:T(8,128)(2,1)S(1)}, bf16[1024,1024]{1,0:T(8,128)(2,1)S(1)}) custom-call(s32[1,20,8]{2,1,0:T(8,128)S(1)} %copy-done.8, bf16[1024,1024]{1,0:T(8,128)(2,1)S(1)} %copy-done.5, bf16[1024,1024]{1,0:T(8,128)(2,1)S(1)} %copy-done.1, bf16[1024,1024]{1,0:T(8,128)(2,1)S(1)} %copy-done), custom_call_target="tpu_custom_call" | custom-call | flops 1342177280 | bytes 8388608 | tf_op jit(solution)/shard_map/pallas_call | solution.py:441
  49.0 2.8 %shard_map.96 = (f32[1024,1024]{1,0:T(8,128)S(1)}, f32[2,1024]{1,0:T(2,128)S(1)}) custom-call(s32[1]{0:T(128)} %bitcast.pref, bf16[1024,1024]{1,0:T(8,128)(2,1)S(1)} %copy-done.6, f32[1024,1024]{1,0:T(8,128)S(1)} %get-tuple-element.24.part, f32[1024,1024]{1,0:T(8,128)S(1)} %copy-done.4, f32[1,256,128]{2,1,0:T(8,128)S(1)} %bitcast.330, ...), custom_call_target="tpu_custom_call" | custom-call | flops 268435456 | bytes 8388608 | tf_op jit(solution)/shard_map/pallas_call | solution.py:454
  53.1 4.8 %shard_map.97 = (bf16[1024,1024]{1,0:T(8,128)(2,1)S(1)}, f32[1,256,128]{2,1,0:T(8,128)S(1)}, f32[1,256,128]{2,1,0:T(8,128)S(1)}, f32[1,256,128]{2,1,0:T(8,128)S(1)}, f32[1,256,128]{2,1,0:T(8,128)S(1)}) custom-call(s32[1]{0:T(128)} %bitcast.pref, bf16[1024,1024]{1,0:T(8,128)(2,1)S(1)} %copy-done.6, f32[1024,1024]{1,0:T(8,128)S(1)} %get-tuple-element.29.att, ...), custom_call_target="tpu_custom_call" | custom-call | flops 268435456 | bytes 8388608 | tf_op jit(solution)/shard_map/pallas_call | solution.py:464
  61.4 2.9 %collective-permute-done.9 = f32[1,256,128]{2,1,0:T(8,128)S(1)} collective-permute-done((f32[1,256,128]{2,1,0:T(8,128)S(1)}, f32[1,256,128]{2,1,0:T(8,128)S(1)}, u32[]{:S(2)}, u32[]{:S(2)}) %collective-permute-start.9) | collective-permute-done | bytes 131104 | tf_op jit(solution)/shard_map/ppermute | solution.py:290
  64.3 1.6 %collective-permute-done.10 = f32[1,256,128]{2,1,0:T(8,128)S(1)} collective-permute-done((f32[1,256,128]{2,1,0:T(8,128)S(1)}, f32[1,256,128]{2,1,0:T(8,128)S(1)}, u32[]{:S(2)}, u32[]{:S(2)}) %collective-permute-start.10) | collective-permute-done | bytes 131104 | tf_op jit(solution)/shard_map/ppermute | solution.py:290
  65.9 1.8 %collective-permute-done.11 = f32[1,256,128]{2,1,0:T(8,128)S(1)} collective-permute-done((f32[1,256,128]{2,1,0:T(8,128)S(1)}, f32[1,256,128]{2,1,0:T(8,128)S(1)}, u32[]{:S(2)}, u32[]{:S(2)}) %collective-permute-start.11) | collective-permute-done | bytes 131104 | tf_op jit(solution)/shard_map/ppermute | solution.py:290
  67.7 1.7 %collective-permute-start.12 = (f32[256,128]{1,0:T(8,128)S(1)}, f32[256,128]{1,0:T(8,128)S(1)}, u32[]{:S(2)}, u32[]{:S(2)}) collective-permute-start(f32[256,128]{1,0:T(8,128)S(1)} %fusion.18), channel_id=1, source_target_pairs={{0,16},{2,18},{4,20},{6,22},{8,24},{10,26},{12,28},{14,30},{16,0},... | collective-permute-start | bytes 393224 | tf_op jit(solution)/shard_map/ppermute | solution.py:290
  69.4 6.8 %collective-permute-done.12 = f32[256,128]{1,0:T(8,128)S(1)} collective-permute-done((f32[256,128]{1,0:T(8,128)S(1)}, f32[256,128]{1,0:T(8,128)S(1)}, u32[]{:S(2)}, u32[]{:S(2)}) %collective-permute-start.12) | collective-permute-done | bytes 131104 | tf_op jit(solution)/shard_map/ppermute | solution.py:290
  76.4 5.0 %collective-permute-done.13 = f32[256,128]{1,0:T(8,128)S(1)} collective-permute-done((f32[256,128]{1,0:T(8,128)S(1)}, f32[256,128]{1,0:T(8,128)S(1)}, u32[]{:S(2)}, u32[]{:S(2)}) %collective-permute-start.13) | collective-permute-done | bytes 131104 | tf_op jit(solution)/shard_map/ppermute | solution.py:290
  81.6 2.1 %collective-permute-start.15 = (f32[256,128]{1,0:T(8,128)S(1)}, f32[256,128]{1,0:T(8,128)S(1)}, u32[]{:S(2)}, u32[]{:S(2)}) collective-permute-start(f32[256,128]{1,0:T(8,128)S(1)} %fusion.3), channel_id=1, source_target_pairs={{0,4},{2,6},{4,0},{6,2},{8,12},{10,14},{12,8},{14,10},{16,20},{18,... | collective-permute-start | bytes 393224 | tf_op jit(solution)/shard_map/ppermute | solution.py:290
  85.2 7.0 %shard_map.99 = (f32[1024,1024]{1,0:T(8,128)S(1)}, bf16[8,8,128,128]{3,2,1,0:T(8,128)(2,1)S(1)}) custom-call(s32[1,20,8]{2,1,0:T(8,128)S(1)} %copy-done.8, bf16[1024,1024]{1,0:T(8,128)(2,1)S(1)} %copy-done.6, bf16[1024,1024]{1,0:T(8,128)(2,1)S(1)} %copy-done, bf16[1024,1024]{1,0:T(8,128)(2,1)S(1)} %get-tuple-element.31.grad), custom_call_target="tpu_custom_call" | custom-call | flops 1073741824 | bytes 8388608 | tf_op jit(solution)/shard_map/pallas_call | solution.py:484
  92.2 2.9 %shard_map.100.value_in = f32[1024,1024]{1,0:T(8,128)S(1)} custom-call(bf16[1024,1024]{1,0:T(8,128)(2,1)S(1)} %copy-done.2, bf16[1024,1024]{1,0:T(8,128)(2,1)S(1)} %get-tuple-element.31.grad, bf16[1024,1024]{1,0:T(8,128)(2,1)S(1)} %get-tuple-element.36.att_t, bf16[8,8,128,128]{3,2,1,0:T(8,128)(2,1)S(1)} %get-tuple-element.37.readers), custom_call_target="tpu_custom_call" | custom-call | flops 536870912 | bytes 8388608 | tf_op jit(solution)/shard_map/pallas_call | solution.py:487
  95.0 7.5 %shard_map.98 = (bf16[1024,1024]{1,0:T(8,128)(2,1)}, bf16[1024,1024]{1,0:T(8,128)(2,1)}) custom-call(s32[1]{0:T(128)} %bitcast.pref, s32[1,20,8]{2,1,0:T(8,128)S(1)} %copy-done.8, bf16[1024,1024]{1,0:T(8,128)(2,1)S(1)} %copy-done.2, bf16[1024,1024]{1,0:T(8,128)(2,1)S(1)} %copy-done, bf16[1024,1024]{1,0:T(8,128)(2,1)S(1)} %get-tuple-element.31.grad, ...), custom_call_target="tpu_custom_call" | custom-call | flops 805306368 | bytes 8388608 | tf_op jit(solution)/shard_map/pallas_call | solution.py:475
  102.5 5.1 %shard_map.101 = (bf16[1024,1024]{1,0:T(8,128)(2,1)}, bf16[1024,1024]{1,0:T(8,128)(2,1)}) custom-call(s32[1]{0:T(128)} %bitcast.pref, bf16[1024,1024]{1,0:T(8,128)(2,1)S(1)} %copy-done.2, bf16[1024,1024]{1,0:T(8,128)(2,1)S(1)} %copy-done, f32[1024,1024]{1,0:T(8,128)S(1)} %get-tuple-element.35.key_in, f32[1024,1024]{1,0:T(8,128)S(1)} %shard_map.100.value_in, ...), custom_call_target="tpu_custom_call" | custom-call | flops 536870912 | bytes 8388608 | tf_op jit(solution)/shard_map/pallas_call | solution.py:493
  (65 shorter events, 19.6 us)
Async XLA Ops:
  6.3 26.9 %copy-start.10 = (f32[264,128]{1,0:T(8,128)S(1)}, f32[264,128]{1,0:T(8,128)}, u32[]{:S(2)}) copy-start(f32[264,128]{1,0:T(8,128)} %get-tuple-element.25) | copy-start | bytes 405508
  6.3 29.4 %copy-start.9 = (f32[1024]{0:T(1024)S(1)}, f32[1024]{0:T(1024)}, u32[]{:S(2)}) copy-start(f32[1024]{0:T(1024)} %param.10) | copy-start | bytes 12292
  6.3 7.3 %collective-permute-start = (f32[264,128]{1,0:T(8,128)}, f32[264,128]{1,0:T(8,128)S(1)}, u32[]{:S(2)}, u32[]{:S(2)}) collective-permute-start(f32[264,128]{1,0:T(8,128)} %get-tuple-element.26), channel_id=1, source_target_pairs={{0,2},{2,0},{4,6},{6,4},{8,10},{10,8},{12,14},{14,12},{16,18},{18,... | collective-permute-start | bytes 405512 | tf_op jit(solution)/shard_map/ppermute | solution.py:290
  9.4 8.2 %collective-permute-start.1 = (f32[264,128]{1,0:T(8,128)}, f32[264,128]{1,0:T(8,128)S(1)}, u32[]{:S(2)}, u32[]{:S(2)}) collective-permute-start(f32[264,128]{1,0:T(8,128)} %get-tuple-element.27), channel_id=1, source_target_pairs={{0,4},{2,6},{4,0},{6,2},{8,12},{10,14},{12,8},{14,10},{16,20},{18,... | collective-permute-start | bytes 405512 | tf_op jit(solution)/shard_map/ppermute | solution.py:290
  10.9 6.6 %collective-permute-start.2 = (f32[264,128]{1,0:T(8,128)}, f32[264,128]{1,0:T(8,128)S(1)}, u32[]{:S(2)}, u32[]{:S(2)}) collective-permute-start(f32[264,128]{1,0:T(8,128)} %get-tuple-element.28), channel_id=1, source_target_pairs={{0,6},{2,4},{4,2},{6,0},{8,14},{10,12},{12,10},{14,8},{16,22},{18,... | collective-permute-start | bytes 405512 | tf_op jit(solution)/shard_map/ppermute | solution.py:290
  18.5 5.0 %collective-permute-start.3 = (f32[256,128]{1,0:T(8,128)S(1)}, f32[256,128]{1,0:T(8,128)S(1)}, u32[]{:S(2)}, u32[]{:S(2)}) collective-permute-start(f32[256,128]{1,0:T(8,128)S(1)} %add_add_fusion), channel_id=1, source_target_pairs={{0,8},{2,10},{4,12},{6,14},{8,0},{10,2},{12,4},{14,6},{16,24},{18,... | collective-permute-start | bytes 393224 | tf_op jit(solution)/shard_map/ppermute | solution.py:290
  23.5 7.3 %collective-permute-start.4 = (f32[256,128]{1,0:T(8,128)S(1)}, f32[256,128]{1,0:T(8,128)S(1)}, u32[]{:S(2)}, u32[]{:S(2)}) collective-permute-start(f32[256,128]{1,0:T(8,128)S(1)} %add.237), channel_id=1, source_target_pairs={{0,16},{2,18},{4,20},{6,22},{8,24},{10,26},{12,28},{14,30},{16,0},... | collective-permute-start | bytes 393224 | tf_op jit(solution)/shard_map/ppermute | solution.py:290
  31.9 17.1 %collective-permute-start.5 = (f32[1,256,128]{2,1,0:T(8,128)S(1)}, f32[1,256,128]{2,1,0:T(8,128)S(1)}, u32[]{:S(2)}, u32[]{:S(2)}) collective-permute-start(f32[1,256,128]{2,1,0:T(8,128)S(1)} %bitcast.334), channel_id=1, source_target_pairs={{0,2},{2,0},{4,6},{6,4},{8,10},{10,8},{12,14},{14,12},{16,18},{18,... | collective-permute-start | bytes 393224 | tf_op jit(solution)/shard_map/ppermute | solution.py:290
  33.3 15.7 %collective-permute-start.6 = (f32[1,256,128]{2,1,0:T(8,128)S(1)}, f32[1,256,128]{2,1,0:T(8,128)S(1)}, u32[]{:S(2)}, u32[]{:S(2)}) collective-permute-start(f32[1,256,128]{2,1,0:T(8,128)S(1)} %bitcast.336), channel_id=1, source_target_pairs={{0,4},{2,6},{4,0},{6,2},{8,12},{10,14},{12,8},{14,10},{16,20},{18,... | collective-permute-start | bytes 393224 | tf_op jit(solution)/shard_map/ppermute | solution.py:290
  34.2 14.8 %collective-permute-start.7 = (f32[1,256,128]{2,1,0:T(8,128)S(1)}, f32[1,256,128]{2,1,0:T(8,128)S(1)}, u32[]{:S(2)}, u32[]{:S(2)}) collective-permute-start(f32[1,256,128]{2,1,0:T(8,128)S(1)} %bitcast.335), channel_id=1, source_target_pairs={{0,6},{2,4},{4,2},{6,0},{8,14},{10,12},{12,10},{14,8},{16,22},{18,... | collective-permute-start | bytes 393224 | tf_op jit(solution)/shard_map/ppermute | solution.py:290
  37.3 2.3 %copy-start = (bf16[1024,1024]{1,0:T(8,128)(2,1)S(1)}, bf16[1024,1024]{1,0:T(8,128)(2,1)}, u32[]{:S(2)}) copy-start(bf16[1024,1024]{1,0:T(8,128)(2,1)} %v.7) | copy-start | bytes 6291460
  37.3 2.3 %copy-start.8 = (s32[1,20,8]{2,1,0:T(8,128)S(1)}, s32[1,20,8]{2,1,0:T(8,128)}, u32[]{:S(2)}) copy-start(s32[1,20,8]{2,1,0:T(8,128)} %copy.18.codes) | copy-start | bytes 1924
  42.8 6.2 %copy-start.4 = (f32[1024,1024]{1,0:T(8,128)S(1)}, f32[1024,1024]{1,0:T(8,128)}, u32[]{:S(2)}) copy-start(f32[1024,1024]{1,0:T(8,128)} %copy-done.3) | copy-start | bytes 12582916
  42.8 6.2 %copy-start.6 = (bf16[1024,1024]{1,0:T(8,128)(2,1)S(1)}, bf16[1024,1024]{1,0:T(8,128)(2,1)}, u32[]{:S(2)}) copy-start(bf16[1024,1024]{1,0:T(8,128)(2,1)} %q.7) | copy-start | bytes 6291460
  51.8 1.2 %collective-permute-start.8 = (f32[2,1024]{1,0:T(2,128)S(1)}, f32[2,1024]{1,0:T(2,128)S(1)}, u32[]{:S(2)}, u32[]{:S(2)}) collective-permute-start(f32[2,1024]{1,0:T(2,128)S(1)} %get-tuple-element.30), channel_id=1, source_target_pairs={{0,1},{1,0},{2,3},{3,2},{4,5},{5,4},{6,7},{7,6},{8,9},{9,8},{10,11... | collective-permute-start | bytes 24584 | tf_op jit(solution)/shard_map/ppermute | solution.py:290
  57.9 6.4 %collective-permute-start.9 = (f32[1,256,128]{2,1,0:T(8,128)S(1)}, f32[1,256,128]{2,1,0:T(8,128)S(1)}, u32[]{:S(2)}, u32[]{:S(2)}) collective-permute-start(f32[1,256,128]{2,1,0:T(8,128)S(1)} %get-tuple-element.39), channel_id=1, source_target_pairs={{0,2},{2,0},{4,6},{6,4},{8,10},{10,8},{12,14},{14,12},{16,18},{18,... | collective-permute-start | bytes 393224 | tf_op jit(solution)/shard_map/ppermute | solution.py:290
  59.1 6.8 %collective-permute-start.10 = (f32[1,256,128]{2,1,0:T(8,128)S(1)}, f32[1,256,128]{2,1,0:T(8,128)S(1)}, u32[]{:S(2)}, u32[]{:S(2)}) collective-permute-start(f32[1,256,128]{2,1,0:T(8,128)S(1)} %get-tuple-element.40), channel_id=1, source_target_pairs={{0,4},{2,6},{4,0},{6,2},{8,12},{10,14},{12,8},{14,10},{16,20},{18,... | collective-permute-start | bytes 393224 | tf_op jit(solution)/shard_map/ppermute | solution.py:290
  60.0 7.7 %collective-permute-start.11 = (f32[1,256,128]{2,1,0:T(8,128)S(1)}, f32[1,256,128]{2,1,0:T(8,128)S(1)}, u32[]{:S(2)}, u32[]{:S(2)}) collective-permute-start(f32[1,256,128]{2,1,0:T(8,128)S(1)} %get-tuple-element.41), channel_id=1, source_target_pairs={{0,6},{2,4},{4,2},{6,0},{8,14},{10,12},{12,10},{14,8},{16,22},{18,... | collective-permute-start | bytes 393224 | tf_op jit(solution)/shard_map/ppermute | solution.py:290
  67.7 8.5 %collective-permute-start.12 = (f32[256,128]{1,0:T(8,128)S(1)}, f32[256,128]{1,0:T(8,128)S(1)}, u32[]{:S(2)}, u32[]{:S(2)}) collective-permute-start(f32[256,128]{1,0:T(8,128)S(1)} %fusion.18), channel_id=1, source_target_pairs={{0,16},{2,18},{4,20},{6,22},{8,24},{10,26},{12,28},{14,30},{16,0},... | collective-permute-start | bytes 393224 | tf_op jit(solution)/shard_map/ppermute | solution.py:290
  76.3 5.1 %collective-permute-start.13 = (f32[256,128]{1,0:T(8,128)S(1)}, f32[256,128]{1,0:T(8,128)S(1)}, u32[]{:S(2)}, u32[]{:S(2)}) collective-permute-start(f32[256,128]{1,0:T(8,128)S(1)} %fusion.14), channel_id=1, source_target_pairs={{0,8},{2,10},{4,12},{6,14},{8,0},{10,2},{12,4},{14,6},{16,24},{18,... | collective-permute-start | bytes 393224 | tf_op jit(solution)/shard_map/ppermute | solution.py:290
  81.5 21.0 %collective-permute-start.14 = (f32[256,128]{1,0:T(8,128)S(1)}, f32[256,128]{1,0:T(8,128)S(1)}, u32[]{:S(2)}, u32[]{:S(2)}) collective-permute-start(f32[256,128]{1,0:T(8,128)S(1)} %get-tuple-element.50), channel_id=1, source_target_pairs={{0,2},{2,0},{4,6},{6,4},{8,10},{10,8},{12,14},{14,12},{16,18},{18,... | collective-permute-start | bytes 393224 | tf_op jit(solution)/shard_map/ppermute | solution.py:290
  81.6 20.9 %collective-permute-start.15 = (f32[256,128]{1,0:T(8,128)S(1)}, f32[256,128]{1,0:T(8,128)S(1)}, u32[]{:S(2)}, u32[]{:S(2)}) collective-permute-start(f32[256,128]{1,0:T(8,128)S(1)} %fusion.3), channel_id=1, source_target_pairs={{0,4},{2,6},{4,0},{6,2},{8,12},{10,14},{12,8},{14,10},{16,20},{18,... | collective-permute-start | bytes 393224 | tf_op jit(solution)/shard_map/ppermute | solution.py:290
  83.8 18.7 %collective-permute-start.16 = (f32[256,128]{1,0:T(8,128)S(1)}, f32[256,128]{1,0:T(8,128)S(1)}, u32[]{:S(2)}, u32[]{:S(2)}) collective-permute-start(f32[256,128]{1,0:T(8,128)S(1)} %get-tuple-element.44), channel_id=1, source_target_pairs={{0,6},{2,4},{4,2},{6,0},{8,14},{10,12},{12,10},{14,8},{16,22},{18,... | collective-permute-start | bytes 393224 | tf_op jit(solution)/shard_map/ppermute | solution.py:290
  85.2 7.0 %copy-start.2 = (bf16[1024,1024]{1,0:T(8,128)(2,1)S(1)}, bf16[1024,1024]{1,0:T(8,128)(2,1)}, u32[]{:S(2)}) copy-start(bf16[1024,1024]{1,0:T(8,128)(2,1)} %k.7) | copy-start | bytes 6291460
  (4 other events, 6.7 us)
where the time goes:
time: 108 us
  Pallas kernels  40.7 us (38%)
  waiting for transfers between devices  33.2 us (31%)
  starting transfers between devices  21.6 us (20%)
  local copies, waits for them, and re-layouts  8.87 us (8%)
  other arithmetic  2.37 us (2%)
    ppermute x17, waiting for transfers between devices, exchange(): return lax.ppermute(x, axis, [(i, i ^ distance) for i in range(count)])  33.2 us
    ppermute x17, starting transfers between devices, exchange(): return lax.ppermute(x, axis, [(i, i ^ distance) for i in range(count)])  21.6 us
    unnamed x23, local copies, waits for them, and re-layouts  8.16 us
    pallas_call x1, Pallas kernels, local(): call(functools.partial(query_kernel, pieces, each, features), 3, [smem, s...  7.46 us
    pallas_call x1, Pallas kernels, local(): call(key_kernel, 4, [smem] + [vmem] * 3, [wide, jax.ShapeDtypeStruct((hea...  6.98 us
    pallas_call x1, Pallas kernels, local(): call(functools.partial(inside_kernel, pair), 5, [smem, vmem, vmem, vmem],...  6.13 us
    pallas_call x1, Pallas kernels, local(): call(functools.partial(outer_kernel, pieces, each), 2, [smem] + [vmem] *...  5.05 us
    pallas_call x1, Pallas kernels, local(): call(functools.partial(grad_kernel, pieces, each, features), 1, [smem] +...  4.82 us
  transfers between devices with their start and end apart: 17, of which 10 were waited for; matrix products, arithmetic and copies ran while one was open for 1% of the time, Pallas kernels for 22%

commit v1 on v0

--- a/solution.py
+++ b/solution.py
@@ -11,6 +11,8 @@
 
 D = 128
 GROUP = 1024
+ROWS = 256
+WIDE = 512
 CHUNK = 128
 F32 = jnp.float32
 BF16 = jnp.bfloat16
@@ -32,7 +34,7 @@
 
 def weight(codes, g, level, h):
     factor = (2.0 ** (-(level - 1) / 2) if level else 1.0) / 4 / math.sqrt(D)
-    return codes[g, level, h].astype(F32) * factor
+    return codes[g, h, level].astype(F32) * factor
 
 
 def tile_weights(codes, g, h, transposed=False):
@@ -89,37 +91,53 @@
     return jnp.concatenate([a, b], axis)
 
 
-def state_kernel(parts, each, far, pref, codes, k_hbm, v_hbm, *refs):
-    outs, (k, v, state, sems) = refs[:parts], refs[parts:]
-    width = each * D
+def add_states(state, first, k, v, r):
+    for h in range(k.shape[1] // D):
+        c = slice(h * D, (h + 1) * D)
+        y = dot(k[r, c], v[r, c], 0, 0)
+        state[h] = y if first else state[h] + y
+
+
+def place(pieces):
+    return lax.axis_index("seq") % pieces
+
+
+def state_kernel(parts, each, far, codes_hbm, k_hbm, v_hbm, *refs):
+    outs, (k, v, state, codes, sems, codes_sem) = refs[:parts], refs[parts:]
+    blocks = [slice(i, i + ROWS) for i in range(0, k.shape[0], ROWS)]
     copies = []
-    for n in range(parts):
-        cols = slice(n * width, (n + 1) * width)
+    for n, r in enumerate(blocks):
         pair = [
-            pltpu.make_async_copy(k_hbm.at[:, cols], k.at[n], sems.at[0, n]),
-            pltpu.make_async_copy(v_hbm.at[:, cols], v.at[n], sems.at[1, n]),
+            pltpu.make_async_copy(k_hbm.at[r, :], k.at[r, :], sems.at[0, n]),
+            pltpu.make_async_copy(v_hbm.at[r, :], v.at[r, :], sems.at[1, n]),
         ]
         for c in pair:
             c.start()
         copies.append(pair)
+        if n == 0:
+            codes_copy = pltpu.make_async_copy(codes_hbm, codes, codes_sem)
+            codes_copy.start()
     first, bits = far
-    p = pref[0]
+    p = place(parts)
+    index = lax.axis_index("seq")
+    reads = [(lax.shift_right_logical(index, level) & 1).astype(F32) for level in range(bits)]
+    codes_copy.wait()
     for m, out in enumerate(outs):
-        row = width
+        row = each * D
         for level in range(bits):
             for i in range(each):
-                out[row : row + 1, :] = jnp.full((1, D), weight(codes, 0, first + level, (m ^ p) * each + i), F32)
+                w = weight(codes, 0, first + level, (m ^ p) * each + i)
+                out[row : row + 1, :] = jnp.full((1, D), w * reads[level], F32)
                 row += 1
         if row < out.shape[0]:
             out[row:, :] = jnp.zeros((out.shape[0] - row, D), F32)
-    for n in range(parts):
+    for n, r in enumerate(blocks):
         for c in copies[n]:
             c.wait()
+        add_states(state, n == 0, k, v, r)
+    for m, out in enumerate(outs):
         for i in range(each):
-            cols = slice(i * D, (i + 1) * D)
-            state[n, cols, :] = dot(k[n, :, cols], v[n, :, cols], 0, 0)
-    for m, out in enumerate(outs):
-        out[:width, :] = state[m ^ p]
+            out[i * D : (i + 1) * D, :] = state[(m ^ p) * each + i]
 
 
 def inside_kernel(pair, codes, q, k, v, part, maps, att_t, *tiles):
@@ -148,7 +166,10 @@
                 part[r, c] = dot(cat(tiles[n][r, :], q[r, c], 1), cat(v[r, c], maps[h, i], 0), 1, 0)
 
 
-def scale_kernel(u, gain, scaled):
+def scale_kernel(pieces, u, gain, scaled, zeros, spot):
+    zeros[...] = jnp.zeros_like(zeros)
+    spot[0] = place(pieces)
+
     @pl.loop(0, u.shape[0] // CHUNK)
     def _(i):
         r = pl.ds(pl.multiple_of(i * CHUNK, CHUNK), CHUNK)
@@ -162,24 +183,38 @@
                 out[(m ^ p) * each + i, g] = piece[g, i * D : (i + 1) * D, :].astype(out.dtype)
 
 
-def attend_kernel(pieces, each, pref, q, part, scaled, *refs):
-    far, (att, stats, maps) = refs[:pieces], refs[pieces:]
-    sort_pieces(far, each, pref[0], maps)
-    heads = q.shape[1] // D
-
-    @pl.loop(0, q.shape[0] // CHUNK)
-    def _(step):
-        r = pl.ds(pl.multiple_of(step * CHUNK, CHUNK), CHUNK)
-        g = (step * CHUNK) // GROUP
-        squares = dots = None
-        for h in range(heads):
-            c = slice(h * D, (h + 1) * D)
-            a = part[r, c] + dot(q[r, c], maps[h, g], 1, 0)
-            att[r, c] = a
-            squares = a * a if h == 0 else squares + a * a
-            dots = scaled[r, c] * a if h == 0 else dots + scaled[r, c] * a
-        stats[0:1, r] = jnp.sum(squares.T, axis=0, keepdims=True)
-        stats[1:2, r] = jnp.sum(dots.T, axis=0, keepdims=True)
+def attend_kernel(offsets, pieces, each, q, part, scaled, stats_in, *refs):
+    count = len(offsets)
+    far, (att, stats, maps) = refs[:count], refs[count:]
+    for n, piece in enumerate(far):
+        for i in range(each):
+            for g in range(piece.shape[0]):
+                maps[n * each + i, g] = piece[g, i * D : (i + 1) * D, :].astype(BF16)
+
+    def attend(heads):
+        cols = [slice(h * D, (h + 1) * D) for h in heads]
+
+        @pl.loop(0, q.shape[0] // WIDE)
+        def _(step):
+            r = pl.ds(pl.multiple_of(step * WIDE, WIDE), WIDE)
+            g = (step * WIDE) // GROUP
+            for n, c in enumerate(cols):
+                att[r, c] = part[r, c] + dot(q[r, c], maps[n, g], 1, 0)
+            for block in range(WIDE // CHUNK):
+                b = pl.ds(pl.multiple_of(step * WIDE + block * CHUNK, CHUNK), CHUNK)
+                squares = dots = None
+                for n, c in enumerate(cols):
+                    a = att[b, c]
+                    squares = a * a if n == 0 else squares + a * a
+                    dots = scaled[b, c] * a if n == 0 else dots + scaled[b, c] * a
+                stats[0:1, b] = stats_in[0:1, b] + jnp.sum(squares.T, axis=0, keepdims=True)
+                stats[1:2, b] = stats_in[1:2, b] + jnp.sum(dots.T, axis=0, keepdims=True)
+
+    for p in range(pieces):
+
+        @pl.when(place(pieces) == p)
+        def _(p=p):
+            attend([(m ^ p) * each + i for m in offsets for i in range(each)])
 
 
 def token_factors(stats, features, inv_s, beta_s):
@@ -188,39 +223,40 @@
         r = pl.ds(pl.multiple_of(step * CHUNK, CHUNK), CHUNK)
         inv = lax.rsqrt(stats[0:1, r] / features + 1e-06)
         inv_s[r, :] = jnp.broadcast_to(inv, (CHUNK, CHUNK)).T
-        if beta_s is not None:
-            beta = inv * inv * inv * stats[1:2, r] / features
-            beta_s[r, :] = jnp.broadcast_to(beta, (CHUNK, CHUNK)).T
-
-
-def grad_kernel(pieces, each, features, pref, q, att, scaled, stats, grad, *refs):
+        beta = inv * inv * inv * stats[1:2, r] / features
+        beta_s[r, :] = jnp.broadcast_to(beta, (CHUNK, CHUNK)).T
+
+
+def grad_kernel(pieces, each, features, q, att, scaled, stats, grad, *refs):
     outs, (inv, beta, sums) = refs[:pieces], refs[pieces:]
     token_factors(stats, features, inv, beta)
     groups = q.shape[0] // GROUP
 
-    @pl.loop(0, q.shape[1] // D)
-    def _(h):
-        c = col(h)
-        for r in chunk_rows(q.shape[0]):
-            grad[r, c] = (inv[r, :] * scaled[r, c] - att[r, c] * beta[r, :]).astype(BF16)
-        for g in range(groups):
-            r = slice(g * GROUP, (g + 1) * GROUP)
-            sums[h, g] = dot(q[r, c], grad[r, c], 0, 0)
+    sums[...] = jnp.zeros_like(sums)
+
+    @pl.loop(0, q.shape[0] // ROWS)
+    def _(step):
+        r = pl.ds(pl.multiple_of(step * ROWS, ROWS), ROWS)
+        group = (step * ROWS) // GROUP
+        for h in range(q.shape[1] // D):
+            c = slice(h * D, (h + 1) * D)
+            gr = (inv[r, :] * scaled[r, c] - att[r, c] * beta[r, :]).astype(BF16)
+            grad[r, c] = gr
+            sums[h, group] += dot(q[r, c], gr, 0, 0)
 
     for m, out in enumerate(outs):
         for g in range(groups):
             for i in range(each):
-                out[g, i * D : (i + 1) * D, :] = sums[(m ^ pref[0]) * each + i, g]
-
-
-def query_kernel(pieces, each, features, pref, codes, k, v, grad, maps, att, stats, gain, *refs):
-    far, (dq, normed, reach, inv, tiles, outer) = refs[:pieces], refs[pieces:]
+                out[g, i * D : (i + 1) * D, :] = sums[(m ^ place(pieces)) * each + i, g]
+
+
+def query_kernel(pieces, each, codes, k, v, grad, maps, *refs):
+    far, (dq, reach, tiles, outer) = refs[:pieces], refs[pieces:]
     h = pl.program_id(0)
 
     @pl.when(h == 0)
     def _():
-        token_factors(stats, features, inv, None)
-        sort_pieces(far, each, pref[0], reach)
+        sort_pieces(far, each, place(pieces), reach)
 
     c = col(h)
     rows = chunk_rows(k.shape[0])
@@ -233,9 +269,17 @@
         tiles[r, :] = (w * y[:, :D]).astype(BF16)
         outer[r, :] = y[:, D:]
     for r in rows:
-        normed[r, :] = (att[r, c] * inv[r, :] * gain[:, c]).astype(BF16)
-    for r in rows:
         dq[r, :] = (dot(tiles[r, :], k[r, c], 1, 0) + outer[r, :]).astype(BF16)
+
+
+def normed_kernel(features, att, stats, gain, normed):
+    for n in range(ROWS // CHUNK):
+        start = pl.program_id(0) * ROWS + n * CHUNK
+        b = pl.ds(pl.multiple_of(start, CHUNK), CHUNK)
+        inv = jnp.broadcast_to(lax.rsqrt(stats[0:1, b] / features + 1e-06), (CHUNK, CHUNK)).T
+        for h in range(att.shape[1] // D):
+            c = slice(h * D, (h + 1) * D)
+            normed[n * CHUNK : (n + 1) * CHUNK, c] = (att[b, c] * inv * gain[:, c]).astype(BF16)
 
 
 def key_kernel(codes, q, v, grad, key_in, readers, tiles, outer):
@@ -268,21 +312,27 @@
             value_in[r, c] = dot(cat(att_t[r, c], k[r, c], 1), cat(grad[r, c], readers[h, i], 0), 1, 0)
 
 
-def outer_kernel(pieces, each, pref, k, v, key_in, value_in, *refs):
-    far, (dk, dv, maps) = refs[:pieces], refs[pieces:]
-    step = pl.program_id(0)
-
-    @pl.when(step == 0)
+def outer_kernel(base, count, each, pref, k, v, key_in, value_in, *refs):
+    far, (dk, dv, maps) = refs[:count], refs[-3:]
+    j, step = pl.program_id(0), pl.program_id(1)
+
+    @pl.when((j == 0) & (step == 0))
     def _():
-        for m, piece in enumerate(far):
+        for n, piece in enumerate(far):
             for i in range(each):
-                maps[(m ^ pref[0]) * each + i] = piece[i * D : (i + 1) * D, :].astype(BF16)
-
-    r = pl.ds(pl.multiple_of(step * CHUNK, CHUNK), CHUNK)
-    for h in range(k.shape[1] // D):
-        c = slice(h * D, (h + 1) * D)
-        dk[:, c] = (key_in[r, c] + dot(v[r, c], maps[h], 1, 1)).astype(BF16)
-        dv[:, c] = (value_in[r, c] + dot(k[r, c], maps[h], 1, 0)).astype(BF16)
+                maps[n * each + i] = piece[i * D : (i + 1) * D, :].astype(BF16)
+
+    r = pl.ds(pl.multiple_of(step * WIDE, WIDE), WIDE)
+    for part in range(k.shape[1] // D // each):
+
+        @pl.when((base + j) ^ pref[0] == part)
+        def _(part=part):
+            for i in range(each):
+                c = slice((part * each + i) * D, (part * each + i + 1) * D)
+                here = slice(i * D, (i + 1) * D)
+                m = maps[j * each + i]
+                dk[:, here] = (key_in[r, c] + dot(v[r, c], m, 1, 1)).astype(BF16)
+                dv[:, here] = (value_in[r, c] + dot(k[r, c], m, 1, 0)).astype(BF16)
 
 
 def exchange(x, axis, distance):
@@ -311,7 +361,6 @@
         used = groups * self.bits * self.segs
         self.extra = -(-used // 8) * 8
         self.p = self.me % self.inner
-        self.outer = self.me // self.inner
         self.fast = self.rows % D == 0 and groups == 1
 
     def take(self, ext, m):
@@ -334,11 +383,9 @@
             acc = jnp.zeros((self.groups, self.segs, self.seg, D), F32)
             for other in range(self.inner):
                 if other != m:
-                    reads = ((self.p ^ other) < (self.p ^ m)).astype(F32)
-                    acc = acc + (w[:, (m ^ other).bit_length() - 1] * reads) * state[other][None]
+                    acc = acc + w[:, (m ^ other).bit_length() - 1] * state[other][None]
             for bit, came in enumerate(outer):
-                reads = ((self.outer >> bit) & 1).astype(F32)
-                acc = acc + (w[:, self.inner_bits + bit] * reads) * came[None]
+                acc = acc + w[:, self.inner_bits + bit] * came[None]
             back.append(acc.reshape(self.groups, self.rows, D))
         return [back[0]] + [exchange(back[m], "seq", m) for m in range(1, self.inner)], ext
 
@@ -352,8 +399,7 @@
 
         total = None
         for bit in reversed(range(self.bits - self.inner_bits)):
-            reads = ((self.outer >> bit) & 1).astype(F32)
-            send = reads * functools.reduce(
+            send = functools.reduce(
                 lambda a, b: a + b, [read_at(m, self.inner_bits + bit) for m in range(self.inner)]
             )
             if total is not None:
@@ -365,8 +411,7 @@
             acc = total if total is not None else jnp.zeros((self.segs, self.seg, D), F32)
             for other in range(self.inner):
                 if other != m:
-                    reads = ((self.p ^ other) > (self.p ^ m)).astype(F32)
-                    acc = acc + reads * read_at(other, (m ^ other).bit_length() - 1)
+                    acc = acc + read_at(other, (m ^ other).bit_length() - 1)
             back.append(acc.reshape(self.rows, D))
         return [back[0]] + [exchange(back[m], "seq", m) for m in range(1, self.inner)]
 
@@ -389,27 +434,30 @@
     far = Far(groups, heads)
     first_far = log2(GROUP) + log2(groups) + 1
     pieces, each = (far.inner, heads // far.inner) if far.fast else (1, heads)
-    pref = (far.p if far.fast else jnp.zeros_like(far.p)).astype(jnp.int32).reshape(1)
     gain = norm_gain.reshape(1, width)
+    codes = jnp.swapaxes(level_codes, 1, 2)
     pair = 2 if heads % 2 == 0 else 1
 
     smem = pl.BlockSpec(memory_space=pltpu.SMEM)
     vmem = pl.BlockSpec(memory_space=pltpu.VMEM)
     wide = jax.ShapeDtypeStruct((tokens, width), F32)
     narrow = jax.ShapeDtypeStruct((tokens, width), BF16)
+    sums = jax.ShapeDtypeStruct((2, tokens), F32)
+    turns = [(0, 1), (2, 3)] if pieces == 4 else [tuple(range(pieces))]
     tile16 = pltpu.VMEM((tokens, D), BF16)
     tile32 = pltpu.VMEM((tokens, D), F32)
     unit = tokens * D * D * heads
 
     def call(kernel, units, ins, outs, scratch=(), limit=12, **kw):
-        kw.setdefault("out_specs", [vmem] * len(outs))
+        if "grid_spec" not in kw:
+            kw.setdefault("out_specs", [vmem] * len(outs))
+            kw["in_specs"] = ins
+            kw["scratch_shapes"] = list(scratch)
         return pl.pallas_call(
             kernel,
-            in_specs=ins,
             out_shape=outs,
-            scratch_shapes=list(scratch),
             compiler_params=pltpu.CompilerParams(vmem_limit_bytes=limit << 20),
-            cost_estimate=pl.CostEstimate(flops=2 * units * unit, bytes_accessed=tokens * width * 8, transcendentals=0),
+            cost_estimate=pl.CostEstimate(flops=int(2 * units * unit), bytes_accessed=tokens * width * 8, transcendentals=0),
             **kw,
         )
 
@@ -417,12 +465,14 @@
         sends = call(
             functools.partial(state_kernel, pieces, each, (first_far, far.bits)),
             1,
-            [smem, smem] + [pl.BlockSpec(memory_space=pltpu.HBM)] * 2,
+            [pl.BlockSpec(memory_space=pltpu.HBM)] * 3,
             [jax.ShapeDtypeStruct((far.rows + far.extra, D), F32)] * pieces,
-            [pltpu.VMEM((pieces, tokens, each * D), BF16)] * 2
-            + [pltpu.VMEM((pieces, each * D, D), F32), pltpu.SemaphoreType.DMA((2, pieces))],
+            [pltpu.VMEM((tokens, width), BF16)] * 2
+            + [pltpu.VMEM((heads, D, D), F32), pltpu.SMEM(codes.shape, jnp.int32)]
+            + [pltpu.SemaphoreType.DMA((2, tokens // ROWS)), pltpu.SemaphoreType.DMA],
             limit=58,
-        )(pref, level_codes, key_rows, value_rows)
+        )(codes, key_rows, value_rows)
+        sends = list(sends)
     else:
         state = jnp.einsum(
             "she,shf->hef",
@@ -431,74 +481,104 @@
             preferred_element_type=F32,
         ).reshape(heads * D, D)
         lam = level_scale(level_codes)
-        per_row = jnp.repeat(lam[:, first_far : first_far + far.bits, :], D // far.seg, axis=2)
+        reads = (far.me >> jnp.arange(far.bits)) & 1
+        weights = lam[:, first_far : first_far + far.bits, :] * reads.astype(F32)[None, :, None]
+        per_row = jnp.repeat(weights, D // far.seg, axis=2)
         sends = []
         for m, piece in enumerate(far.split_pieces(state)):
             w = lax.dynamic_slice_in_dim(per_row, (far.p ^ m) * far.segs, far.segs, 2).reshape(-1, 1)
             w = jnp.pad(w, ((0, far.extra - w.shape[0]), (0, 0)))
             sends.append(jnp.concatenate([piece, jnp.broadcast_to(w, (far.extra, D))], 0))
 
+    upstream, sends[1] = lax.optimization_barrier((upstream, sends[1]))
     part, maps, att_t = call(
         functools.partial(inside_kernel, pair),
         5,
         [smem, vmem, vmem, vmem],
         [wide, jax.ShapeDtypeStruct((heads, chunks, D, D), BF16), narrow],
         [tile16] * pair,
-    )(level_codes, query_rows, key_rows, value_rows)
-    scaled = call(scale_kernel, 1, [vmem, vmem], [wide])(upstream, gain)[0]
+    )(codes, query_rows, key_rows, value_rows)
+    scaled, stats, pref = call(
+        functools.partial(scale_kernel, pieces),
+        1,
+        [vmem, vmem],
+        [wide, sums, jax.ShapeDtypeStruct((1,), jnp.int32)],
+        out_specs=[vmem, vmem, smem],
+    )(upstream, gain)
 
     far_maps, ext = far.forward(sends)
     if not far.fast:
         far_maps = [far.gather_pieces(far_maps)]
 
-    att, stats = call(
-        functools.partial(attend_kernel, pieces, each),
-        1,
-        [smem] + [vmem] * (3 + pieces),
-        [wide, jax.ShapeDtypeStruct((2, tokens), F32)],
-        [pltpu.VMEM((heads, groups, D, D), BF16)],
-    )(pref, query_rows, part, scaled, *far_maps)
+    att = part
+    for offsets in turns:
+        att, stats = call(
+            functools.partial(attend_kernel, offsets, pieces, each),
+            1,
+            [vmem] * (4 + len(offsets)),
+            [wide, sums],
+            [pltpu.VMEM((len(offsets) * each, groups, D, D), BF16)],
+            input_output_aliases={1: 0},
+        )(query_rows, att, scaled, stats, *[far_maps[m] for m in offsets])
 
     stats = sum_over(stats, "head")
 
     grad, *map_grads = call(
         functools.partial(grad_kernel, pieces, each, features),
         1,
-        [smem] + [vmem] * 4,
+        [vmem] * 4,
         [narrow] + [jax.ShapeDtypeStruct((groups, each * D, D), F32)] * pieces,
         [tile32, tile32, pltpu.VMEM((heads, groups, D, D), F32)],
-    )(pref, query_rows, att, scaled, stats)
+    )(query_rows, att, scaled, stats)
 
     if not far.fast:
         map_grads = far.split_pieces(map_grads[0])
 
-    query_gradient, normed = call(
-        functools.partial(query_kernel, pieces, each, features),
+    query_gradient = call(
+        functools.partial(query_kernel, pieces, each),
         3,
-        [smem, smem] + [vmem] * (7 + pieces),
-        [narrow, narrow],
-        [pltpu.VMEM((heads, groups, D, D), F32), tile32, tile16, tile32],
+        [smem] + [vmem] * (4 + pieces),
+        [narrow],
+        [pltpu.VMEM((heads, groups, D, D), F32), tile16, tile32],
         grid=(heads,),
-        out_specs=[pl.BlockSpec((tokens, D), lambda h: (0, h))] * 2,
-    )(pref, level_codes, key_rows, value_rows, grad, maps, att, stats, gain, *far_maps)
+        out_specs=[pl.BlockSpec((tokens, D), lambda h: (0, h))],
+    )(codes, key_rows, value_rows, grad, maps, *far_maps)[0]
+    normed = call(
+        functools.partial(normed_kernel, features),
+        1,
+        [vmem] * 3,
+        [narrow],
+        grid=(tokens // ROWS,),
+        out_specs=[pl.BlockSpec((ROWS, width), lambda i: (i, 0))],
+    )(att, stats, gain)[0]
     key_in, readers = call(
         key_kernel, 4, [smem] + [vmem] * 3, [wide, jax.ShapeDtypeStruct((heads, chunks, D, D), BF16)], [tile16, tile32]
-    )(level_codes, query_rows, value_rows, grad)
+    )(codes, query_rows, value_rows, grad)
     value_in = call(value_kernel, 2, [vmem] * 4, [wide])(key_rows, grad, att_t, readers)[0]
 
     state_grads = far.backward(map_grads, ext)
     if not far.fast:
         state_grads = [far.gather_pieces(state_grads)]
 
-    key_gradient, value_gradient = call(
-        functools.partial(outer_kernel, pieces, each),
-        2,
-        [smem] + [vmem] * (4 + pieces),
-        [narrow, narrow],
-        [pltpu.VMEM((heads, D, D), BF16)],
-        grid=(tokens // CHUNK,),
-        out_specs=[pl.BlockSpec((CHUNK, width), lambda i: (i, 0))] * 2,
-    )(pref, key_rows, value_rows, key_in, value_in, *state_grads)
+    done = []
+    for offsets in turns:
+        base, count = offsets[0], len(offsets)
+        block = pl.BlockSpec((WIDE, each * D), lambda j, i, pref, base=base: (i, (base + j) ^ pref[0]))
+        done = call(
+            functools.partial(outer_kernel, base, count, each),
+            2 / len(turns),
+            None,
+            [narrow, narrow],
+            grid_spec=pltpu.PrefetchScalarGridSpec(
+                num_scalar_prefetch=1,
+                grid=(count, tokens // WIDE),
+                in_specs=[vmem] * (4 + count) + [pl.BlockSpec(memory_space=pl.ANY)] * len(done),
+                out_specs=[block, block],
+                scratch_shapes=[pltpu.VMEM((count * each, D, D), BF16)],
+            ),
+            input_output_aliases={5 + count + i: i for i in range(len(done))},
+        )(pref, key_rows, value_rows, key_in, value_in, *[state_grads[m] for m in offsets], *done)
+    key_gradient, value_gradient = done
     return (normed, query_gradient, key_gradient, value_gradient)
 
 

time: 108 us -> 91.9 us (0.85)
  local copies, waits for them, and re-layouts: 8.87 us -> 0.74 us
  waiting for transfers between devices: 33.2 us -> 27.4 us
  other arithmetic: 2.37 us -> 0.48 us
    unnamed x23 -> x14, local copies, waits for them, and re-layouts: 8.16 us -> 0.04 us
    ppermute x17, waiting for transfers between devices: 33.2 us -> 27.4 us  [exchange(): return lax.ppermute(x, axis, [(i, i ^ distance) for i in range(count)])]
    pallas_call x5 -> x8, Pallas kernels: 20.4 us -> 21.3 us  [the longest x2 6.59 us: local(): call(functools.partial(outer_kernel, base, count, each), 2 / len(turns),...]
  transfers between devices with their start and end apart: 17 -> 17, of which waited for: 10 -> 9; matrix products, arithmetic and copies ran while one was open for 1% -> 1% of each run, Pallas kernels for 22% -> 32%
where the time goes in v1:
time: 91.9 us; the launch traced here: 91.7 us
  Pallas kernels  40.6 us (44%)
  waiting for transfers between devices  27.4 us (30%)
  starting transfers between devices  21.6 us (24%)
    ppermute x17, waiting for transfers between devices, exchange(): return lax.ppermute(x, axis, [(i, i ^ distance) for i in range(count)])  27.4 us
    ppermute x17, starting transfers between devices, exchange(): return lax.ppermute(x, axis, [(i, i ^ distance) for i in range(count)])  21.6 us
    pallas_call x1, Pallas kernels, local(): call(key_kernel, 4, [smem] + [vmem] * 3, [wide, jax.ShapeDtypeStruct((hea...  6.81 us
    pallas_call x2, Pallas kernels, local(): call(functools.partial(outer_kernel, base, count, each), 2 / len(turns),...  6.59 us
    pallas_call x1, Pallas kernels, local(): call(functools.partial(query_kernel, pieces, each), 3, [smem] + [vmem] *...  6.02 us
    pallas_call x1, Pallas kernels, local(): call(functools.partial(inside_kernel, pair), 5, [smem, vmem, vmem, vmem],...  5.97 us
    pallas_call x1, Pallas kernels, local(): call(functools.partial(state_kernel, pieces, each, (first_far, far.bits))...  3.66 us
    pallas_call x2, Pallas kernels, local(): call(functools.partial(attend_kernel, offsets, pieces, each), 1, [vmem] *...  2.95 us
  transfers between devices with their start and end apart: 17, of which 9 were waited for; matrix products, arithmetic and copies ran while one was open for 1% of the time, Pallas kernels for 32%

profile of v1, /device:TPU:0, one launch (start us, length us, event | category | flops | bytes accessed | tf_op | source)
XLA Modules:
  0.0 91.7 jit_solution(15971839270301144497)
XLA Ops:
  0.7 3.7 %shard_map.94 = (f32[264,128]{1,0:T(8,128)}, f32[264,128]{1,0:T(8,128)}, f32[264,128]{1,0:T(8,128)}, f32[264,128]{1,0:T(8,128)}) custom-call(s32[1,8,20]{2,1,0:T(8,128)} %bitcast.238, bf16[1024,1024]{1,0:T(8,128)(2,1)} %k.9, bf16[1024,1024]{1,0:T(8,128)(2,1)} %v.9), custom_call_target="tpu_custom_call" | custom-call | flops 268435456 | bytes 8388608 | tf_op jit(solution)/shard_map/pallas_call | solution.py:465
  4.3 3.0 %collective-permute-start = (f32[264,128]{1,0:T(8,128)}, f32[264,128]{1,0:T(8,128)S(1)}, u32[]{:S(2)}, u32[]{:S(2)}) collective-permute-start(f32[264,128]{1,0:T(8,128)} %get-tuple-element.37), channel_id=1, source_target_pairs={{0,2},{2,0},{4,6},{6,4},{8,10},{10,8},{12,14},{14,12},{16,18},{18,... | collective-permute-start | bytes 405512 | tf_op jit(solution)/shard_map/ppermute | solution.py:340
  7.4 1.5 %collective-permute-start.1 = (f32[264,128]{1,0:T(8,128)}, f32[264,128]{1,0:T(8,128)S(1)}, u32[]{:S(2)}, u32[]{:S(2)}) collective-permute-start(f32[264,128]{1,0:T(8,128)} %get-tuple-element.38), channel_id=1, source_target_pairs={{0,4},{2,6},{4,0},{6,2},{8,12},{10,14},{12,8},{14,10},{16,20},{18,... | collective-permute-start | bytes 405512 | tf_op jit(solution)/shard_map/ppermute | solution.py:340
  11.7 3.9 %collective-permute-done.1 = f32[264,128]{1,0:T(8,128)S(1)} collective-permute-done((f32[264,128]{1,0:T(8,128)}, f32[264,128]{1,0:T(8,128)S(1)}, u32[]{:S(2)}, u32[]{:S(2)}) %collective-permute-start.1) | collective-permute-done | bytes 135200 | tf_op jit(solution)/shard_map/ppermute | solution.py:340
  15.6 1.6 %collective-permute-start.3 = (f32[256,128]{1,0:T(8,128)S(1)}, f32[256,128]{1,0:T(8,128)S(1)}, u32[]{:S(2)}, u32[]{:S(2)}) collective-permute-start(f32[256,128]{1,0:T(8,128)S(1)} %add_add_fusion), channel_id=1, source_target_pairs={{0,8},{2,10},{4,12},{6,14},{8,0},{10,2},{12,4},{14,6},{16,24},{18,... | collective-permute-start | bytes 393224 | tf_op jit(solution)/shard_map/ppermute | solution.py:340
  17.2 3.4 %collective-permute-done.3 = f32[256,128]{1,0:T(8,128)S(1)} collective-permute-done((f32[256,128]{1,0:T(8,128)S(1)}, f32[256,128]{1,0:T(8,128)S(1)}, u32[]{:S(2)}, u32[]{:S(2)}) %collective-permute-start.3) | collective-permute-done | bytes 131104 | tf_op jit(solution)/shard_map/ppermute | solution.py:340
  20.6 2.7 %collective-permute-start.4 = (f32[256,128]{1,0:T(8,128)S(1)}, f32[256,128]{1,0:T(8,128)S(1)}, u32[]{:S(2)}, u32[]{:S(2)}) collective-permute-start(f32[256,128]{1,0:T(8,128)S(1)} %add.227), channel_id=1, source_target_pairs={{0,16},{2,18},{4,20},{6,22},{8,24},{10,26},{12,28},{14,30},{16,0},... | collective-permute-start | bytes 393224 | tf_op jit(solution)/shard_map/ppermute | solution.py:340
  23.3 4.7 %collective-permute-done.4 = f32[256,128]{1,0:T(8,128)S(1)} collective-permute-done((f32[256,128]{1,0:T(8,128)S(1)}, f32[256,128]{1,0:T(8,128)S(1)}, u32[]{:S(2)}, u32[]{:S(2)}) %collective-permute-start.4) | collective-permute-done | bytes 131104 | tf_op jit(solution)/shard_map/ppermute | solution.py:340
  31.9 6.0 %shard_map.93 = (f32[1024,1024]{1,0:T(8,128)S(1)}, bf16[8,8,128,128]{3,2,1,0:T(8,128)(2,1)S(1)}, bf16[1024,1024]{1,0:T(8,128)(2,1)S(1)}) custom-call(s32[1,8,20]{2,1,0:T(8,128)S(1)} %bitcast.239, bf16[1024,1024]{1,0:T(8,128)(2,1)S(1)} %copy-done.2, bf16[1024,1024]{1,0:T(8,128)(2,1)S(1)} %copy-done, bf16[1024,1024]{1,0:T(8,128)(2,1)S(1)} %copy-done.1), custom_call_target="tpu_custom_call" | custom-call | flops 1342177280 | bytes 8388608 | tf_op jit(solution)/shard_map/pallas_call | solution.py:494
  39.3 1.6 %shard_map.97 = (f32[1024,1024]{1,0:T(8,128)S(1)}, f32[2,1024]{1,0:T(2,128)S(1)}) custom-call(bf16[1024,1024]{1,0:T(8,128)(2,1)S(1)} %copy-done.2, f32[1024,1024]{1,0:T(8,128)S(1)} %get-tuple-element.40.part, f32[1024,1024]{1,0:T(8,128)S(1)} %get-tuple-element.34.scaled, f32[2,1024]{1,0:T(2,128)S(1)} %get-tuple-element.41.stats_in, ...), custom_call_target="tpu_custom_call", output_to_operand_aliasing={{0}: (1, {})} | custom-call | flops 268435456 | bytes 8388608 | tf_op jit(solution)/shard_map/pallas_call | solution.py:515
  42.2 2.7 %shard_map.99 = (bf16[1024,1024]{1,0:T(8,128)(2,1)S(1)}, f32[1,256,128]{2,1,0:T(8,128)S(1)}, f32[1,256,128]{2,1,0:T(8,128)S(1)}, f32[1,256,128]{2,1,0:T(8,128)S(1)}, f32[1,256,128]{2,1,0:T(8,128)S(1)}) custom-call(bf16[1024,1024]{1,0:T(8,128)(2,1)S(1)} %copy-done.2, f32[1024,1024]{1,0:T(8,128)S(1)} %get-tuple-element.42.att, ...), custom_call_target="tpu_custom_call" | custom-call | flops 268435456 | bytes 8388608 | tf_op jit(solution)/shard_map/pallas_call | solution.py:526
  48.5 2.9 %collective-permute-done.9 = f32[1,256,128]{2,1,0:T(8,128)S(1)} collective-permute-done((f32[1,256,128]{2,1,0:T(8,128)S(1)}, f32[1,256,128]{2,1,0:T(8,128)S(1)}, u32[]{:S(2)}, u32[]{:S(2)}) %collective-permute-start.9) | collective-permute-done | bytes 131104 | tf_op jit(solution)/shard_map/ppermute | solution.py:340
  51.3 1.6 %collective-permute-done.10 = f32[1,256,128]{2,1,0:T(8,128)S(1)} collective-permute-done((f32[1,256,128]{2,1,0:T(8,128)S(1)}, f32[1,256,128]{2,1,0:T(8,128)S(1)}, u32[]{:S(2)}, u32[]{:S(2)}) %collective-permute-start.10) | collective-permute-done | bytes 131104 | tf_op jit(solution)/shard_map/ppermute | solution.py:340
  52.9 1.8 %collective-permute-done.11 = f32[1,256,128]{2,1,0:T(8,128)S(1)} collective-permute-done((f32[1,256,128]{2,1,0:T(8,128)S(1)}, f32[1,256,128]{2,1,0:T(8,128)S(1)}, u32[]{:S(2)}, u32[]{:S(2)}) %collective-permute-start.11) | collective-permute-done | bytes 131104 | tf_op jit(solution)/shard_map/ppermute | solution.py:340
  54.8 1.7 %collective-permute-start.12 = (f32[256,128]{1,0:T(8,128)S(1)}, f32[256,128]{1,0:T(8,128)S(1)}, u32[]{:S(2)}, u32[]{:S(2)}) collective-permute-start(f32[256,128]{1,0:T(8,128)S(1)} %fusion.13), channel_id=1, source_target_pairs={{0,16},{2,18},{4,20},{6,22},{8,24},{10,26},{12,28},{14,30},{16,0},... | collective-permute-start | bytes 393224 | tf_op jit(solution)/shard_map/ppermute | solution.py:340
  56.4 6.8 %collective-permute-done.12 = f32[256,128]{1,0:T(8,128)S(1)} collective-permute-done((f32[256,128]{1,0:T(8,128)S(1)}, f32[256,128]{1,0:T(8,128)S(1)}, u32[]{:S(2)}, u32[]{:S(2)}) %collective-permute-start.12) | collective-permute-done | bytes 131104 | tf_op jit(solution)/shard_map/ppermute | solution.py:340
  63.4 6.8 %shard_map.101 = (f32[1024,1024]{1,0:T(8,128)S(1)}, bf16[8,8,128,128]{3,2,1,0:T(8,128)(2,1)S(1)}) custom-call(s32[1,8,20]{2,1,0:T(8,128)S(1)} %bitcast.240, bf16[1024,1024]{1,0:T(8,128)(2,1)S(1)} %copy-done.2, bf16[1024,1024]{1,0:T(8,128)(2,1)S(1)} %copy-done.1, bf16[1024,1024]{1,0:T(8,128)(2,1)S(1)} %get-tuple-element.44.grad), custom_call_target="tpu_custom_call" | custom-call | flops 1073741824 | bytes 8388608 | tf_op jit(solution)/shard_map/pallas_call | solution.py:554
  70.4 1.6 %collective-permute-start.15 = (f32[256,128]{1,0:T(8,128)S(1)}, f32[256,128]{1,0:T(8,128)S(1)}, u32[]{:S(2)}, u32[]{:S(2)}) collective-permute-start(f32[256,128]{1,0:T(8,128)S(1)} %get-tuple-element.66), channel_id=1, source_target_pairs={{0,6},{2,4},{4,2},{6,0},{8,14},{10,12},{12,10},{14,8},{16,22},{18,... | collective-permute-start | bytes 393224 | tf_op jit(solution)/shard_map/ppermute | solution.py:340
  72.0 2.0 %collective-permute-start.14 = (f32[256,128]{1,0:T(8,128)S(1)}, f32[256,128]{1,0:T(8,128)S(1)}, u32[]{:S(2)}, u32[]{:S(2)}) collective-permute-start(f32[256,128]{1,0:T(8,128)S(1)} %fusion.28), channel_id=1, source_target_pairs={{0,4},{2,6},{4,0},{6,2},{8,12},{10,14},{12,8},{14,10},{16,20},{18,... | collective-permute-start | bytes 393224 | tf_op jit(solution)/shard_map/ppermute | solution.py:340
  74.0 2.8 %shard_map.102.value_in = f32[1024,1024]{1,0:T(8,128)S(1)} custom-call(bf16[1024,1024]{1,0:T(8,128)(2,1)S(1)} %copy-done, bf16[1024,1024]{1,0:T(8,128)(2,1)S(1)} %get-tuple-element.44.grad, bf16[1024,1024]{1,0:T(8,128)(2,1)S(1)} %get-tuple-element.48.att_t, bf16[8,8,128,128]{3,2,1,0:T(8,128)(2,1)S(1)} %get-tuple-element.49.readers), custom_call_target="tpu_custom_call" | custom-call | flops 536870912 | bytes 8388608 | tf_op jit(solution)/shard_map/pallas_call | solution.py:557
  76.8 2.2 %shard_map.98 = bf16[1024,1024]{1,0:T(8,128)(2,1)} custom-call(f32[1024,1024]{1,0:T(8,128)S(1)} %get-tuple-element.42.att, f32[2,1024]{1,0:T(2,128)S(1)} %add.245.stats, f32[1,1024]{1,0:T(1,128)S(1)} %bitcast.243), custom_call_target="tpu_custom_call" | custom-call | flops 268435456 | bytes 8388608 | tf_op jit(solution)/shard_map/pallas_call | solution.py:546
  79.0 6.0 %shard_map.100 = bf16[1024,1024]{1,0:T(8,128)(2,1)} custom-call(s32[1,8,20]{2,1,0:T(8,128)S(1)} %bitcast.241, bf16[1024,1024]{1,0:T(8,128)(2,1)S(1)} %copy-done, bf16[1024,1024]{1,0:T(8,128)(2,1)S(1)} %copy-done.1, bf16[1024,1024]{1,0:T(8,128)(2,1)S(1)} %get-tuple-element.44.grad, bf16[8,8,128,128]{3,2,1,0:T(8,128)(2,1)S(1)} %get-tuple-element.45.maps, ...), custom_call_target="tpu_custom_call" | custom-call | flops 805306368 | bytes 8388608 | tf_op jit(solution)/shard_map/pallas_call | solution.py:537
  85.1 3.3 %shard_map.103 = (bf16[1024,1024]{1,0:T(8,128)(2,1)}, bf16[1024,1024]{1,0:T(8,128)(2,1)}) custom-call(s32[1]{0:T(128)} %get-tuple-element.46.pref, bf16[1024,1024]{1,0:T(8,128)(2,1)S(1)} %copy-done, bf16[1024,1024]{1,0:T(8,128)(2,1)S(1)} %copy-done.1, f32[1024,1024]{1,0:T(8,128)S(1)} %get-tuple-element.47.key_in, f32[1024,1024]{1,0:T(8,128)S(1)} %shard_map.102.value_in, ...), custom_call_target="tpu_custom_call" | custom-call | flops 268435456 | bytes 8388608 | tf_op jit(solution)/shard_map/pallas_call | solution.py:567
  88.4 3.3 %shard_map.104 = (bf16[1024,1024]{1,0:T(8,128)(2,1)}, bf16[1024,1024]{1,0:T(8,128)(2,1)}) custom-call(s32[1]{0:T(128)} %get-tuple-element.46.pref, bf16[1024,1024]{1,0:T(8,128)(2,1)S(1)} %copy-done, bf16[1024,1024]{1,0:T(8,128)(2,1)S(1)} %copy-done.1, f32[1024,1024]{1,0:T(8,128)S(1)} %get-tuple-element.47.key_in, ...), custom_call_target="tpu_custom_call", output_to_operand_aliasing={{0}: (7, {}), {1}: (8, {})} | custom-call | flops 268435456 | bytes 8388608 | tf_op jit(solution)/shard_map/pallas_call | solution.py:567
  (53 shorter events, 13.3 us)
Async XLA Ops:
  0.6 9.0 %copy-start.3 = (bf16[1024,1024]{1,0:T(8,128)(2,1)S(1)}, bf16[1024,1024]{1,0:T(8,128)(2,1)}, u32[]{:S(2)}) copy-start(bf16[1024,1024]{1,0:T(8,128)(2,1)} %u) | copy-start | bytes 6291460
  0.6 9.0 %copy-start.5 = (f32[1024]{0:T(1024)S(1)}, f32[1024]{0:T(1024)}, u32[]{:S(2)}) copy-start(f32[1024]{0:T(1024)} %param.10) | copy-start | bytes 12292
  0.7 31.3 %copy-start.2 = (bf16[1024,1024]{1,0:T(8,128)(2,1)S(1)}, bf16[1024,1024]{1,0:T(8,128)(2,1)}, u32[]{:S(2)}) copy-start(bf16[1024,1024]{1,0:T(8,128)(2,1)} %q.9) | copy-start | bytes 6291460
  4.3 11.2 %copy-start.6 = (f32[264,128]{1,0:T(8,128)S(1)}, f32[264,128]{1,0:T(8,128)}, u32[]{:S(2)}) copy-start(f32[264,128]{1,0:T(8,128)} %get-tuple-element.36) | copy-start | bytes 405508
  4.3 7.3 %collective-permute-start = (f32[264,128]{1,0:T(8,128)}, f32[264,128]{1,0:T(8,128)S(1)}, u32[]{:S(2)}, u32[]{:S(2)}) collective-permute-start(f32[264,128]{1,0:T(8,128)} %get-tuple-element.37), channel_id=1, source_target_pairs={{0,2},{2,0},{4,6},{6,4},{8,10},{10,8},{12,14},{14,12},{16,18},{18,... | collective-permute-start | bytes 405512 | tf_op jit(solution)/shard_map/ppermute | solution.py:340
  7.4 8.1 %collective-permute-start.1 = (f32[264,128]{1,0:T(8,128)}, f32[264,128]{1,0:T(8,128)S(1)}, u32[]{:S(2)}, u32[]{:S(2)}) collective-permute-start(f32[264,128]{1,0:T(8,128)} %get-tuple-element.38), channel_id=1, source_target_pairs={{0,4},{2,6},{4,0},{6,2},{8,12},{10,14},{12,8},{14,10},{16,20},{18,... | collective-permute-start | bytes 405512 | tf_op jit(solution)/shard_map/ppermute | solution.py:340
  8.9 6.6 %collective-permute-start.2 = (f32[264,128]{1,0:T(8,128)}, f32[264,128]{1,0:T(8,128)S(1)}, u32[]{:S(2)}, u32[]{:S(2)}) collective-permute-start(f32[264,128]{1,0:T(8,128)} %get-tuple-element.39), channel_id=1, source_target_pairs={{0,6},{2,4},{4,2},{6,0},{8,14},{10,12},{12,10},{14,8},{16,22},{18,... | collective-permute-start | bytes 405512 | tf_op jit(solution)/shard_map/ppermute | solution.py:340
  9.6 22.3 %copy-start.1 = (bf16[1024,1024]{1,0:T(8,128)(2,1)S(1)}, bf16[1024,1024]{1,0:T(8,128)(2,1)}, u32[]{:S(2)}) copy-start(bf16[1024,1024]{1,0:T(8,128)(2,1)} %v.9) | copy-start | bytes 6291460
  10.4 21.5 %copy-start = (bf16[1024,1024]{1,0:T(8,128)(2,1)S(1)}, bf16[1024,1024]{1,0:T(8,128)(2,1)}, u32[]{:S(2)}) copy-start(bf16[1024,1024]{1,0:T(8,128)(2,1)} %k.9) | copy-start | bytes 6291460
  10.4 21.5 %copy-start.4 = (s32[1,20,8]{1,2,0:T(8,128)S(1)}, s32[1,20,8]{1,2,0:T(8,128)}, u32[]{:S(2)}) copy-start(s32[1,20,8]{1,2,0:T(8,128)} %param.9) | copy-start | bytes 1924
  15.6 5.0 %collective-permute-start.3 = (f32[256,128]{1,0:T(8,128)S(1)}, f32[256,128]{1,0:T(8,128)S(1)}, u32[]{:S(2)}, u32[]{:S(2)}) collective-permute-start(f32[256,128]{1,0:T(8,128)S(1)} %add_add_fusion), channel_id=1, source_target_pairs={{0,8},{2,10},{4,12},{6,14},{8,0},{10,2},{12,4},{14,6},{16,24},{18,... | collective-permute-start | bytes 393224 | tf_op jit(solution)/shard_map/ppermute | solution.py:340
  20.6 7.3 %collective-permute-start.4 = (f32[256,128]{1,0:T(8,128)S(1)}, f32[256,128]{1,0:T(8,128)S(1)}, u32[]{:S(2)}, u32[]{:S(2)}) collective-permute-start(f32[256,128]{1,0:T(8,128)S(1)} %add.227), channel_id=1, source_target_pairs={{0,16},{2,18},{4,20},{6,22},{8,24},{10,26},{12,28},{14,30},{16,0},... | collective-permute-start | bytes 393224 | tf_op jit(solution)/shard_map/ppermute | solution.py:340
  28.1 9.8 %collective-permute-start.5 = (f32[1,256,128]{2,1,0:T(8,128)S(1)}, f32[1,256,128]{2,1,0:T(8,128)S(1)}, u32[]{:S(2)}, u32[]{:S(2)}) collective-permute-start(f32[1,256,128]{2,1,0:T(8,128)S(1)} %bitcast.244), channel_id=1, source_target_pairs={{0,2},{2,0},{4,6},{6,4},{8,10},{10,8},{12,14},{14,12},{16,18},{18,... | collective-permute-start | bytes 393224 | tf_op jit(solution)/shard_map/ppermute | solution.py:340
  29.5 9.9 %collective-permute-start.6 = (f32[1,256,128]{2,1,0:T(8,128)S(1)}, f32[1,256,128]{2,1,0:T(8,128)S(1)}, u32[]{:S(2)}, u32[]{:S(2)}) collective-permute-start(f32[1,256,128]{2,1,0:T(8,128)S(1)} %bitcast.246), channel_id=1, source_target_pairs={{0,4},{2,6},{4,0},{6,2},{8,12},{10,14},{12,8},{14,10},{16,20},{18,... | collective-permute-start | bytes 393224 | tf_op jit(solution)/shard_map/ppermute | solution.py:340
  30.4 8.9 %collective-permute-start.7 = (f32[1,256,128]{2,1,0:T(8,128)S(1)}, f32[1,256,128]{2,1,0:T(8,128)S(1)}, u32[]{:S(2)}, u32[]{:S(2)}) collective-permute-start(f32[1,256,128]{2,1,0:T(8,128)S(1)} %bitcast.245), channel_id=1, source_target_pairs={{0,6},{2,4},{4,2},{6,0},{8,14},{10,12},{12,10},{14,8},{16,22},{18,... | collective-permute-start | bytes 393224 | tf_op jit(solution)/shard_map/ppermute | solution.py:340
  40.9 1.2 %collective-permute-start.8 = (f32[2,1024]{1,0:T(2,128)S(1)}, f32[2,1024]{1,0:T(2,128)S(1)}, u32[]{:S(2)}, u32[]{:S(2)}) collective-permute-start(f32[2,1024]{1,0:T(2,128)S(1)} %get-tuple-element.43), channel_id=1, source_target_pairs={{0,1},{1,0},{2,3},{3,2},{4,5},{5,4},{6,7},{7,6},{8,9},{9,8},{10,11... | collective-permute-start | bytes 24584 | tf_op jit(solution)/shard_map/ppermute | solution.py:340
  44.9 6.4 %collective-permute-start.9 = (f32[1,256,128]{2,1,0:T(8,128)S(1)}, f32[1,256,128]{2,1,0:T(8,128)S(1)}, u32[]{:S(2)}, u32[]{:S(2)}) collective-permute-start(f32[1,256,128]{2,1,0:T(8,128)S(1)} %get-tuple-element.51), channel_id=1, source_target_pairs={{0,2},{2,0},{4,6},{6,4},{8,10},{10,8},{12,14},{14,12},{16,18},{18,... | collective-permute-start | bytes 393224 | tf_op jit(solution)/shard_map/ppermute | solution.py:340
  46.1 6.8 %collective-permute-start.10 = (f32[1,256,128]{2,1,0:T(8,128)S(1)}, f32[1,256,128]{2,1,0:T(8,128)S(1)}, u32[]{:S(2)}, u32[]{:S(2)}) collective-permute-start(f32[1,256,128]{2,1,0:T(8,128)S(1)} %get-tuple-element.52), channel_id=1, source_target_pairs={{0,4},{2,6},{4,0},{6,2},{8,12},{10,14},{12,8},{14,10},{16,20},{18,... | collective-permute-start | bytes 393224 | tf_op jit(solution)/shard_map/ppermute | solution.py:340
  47.0 7.7 %collective-permute-start.11 = (f32[1,256,128]{2,1,0:T(8,128)S(1)}, f32[1,256,128]{2,1,0:T(8,128)S(1)}, u32[]{:S(2)}, u32[]{:S(2)}) collective-permute-start(f32[1,256,128]{2,1,0:T(8,128)S(1)} %get-tuple-element.53), channel_id=1, source_target_pairs={{0,6},{2,4},{4,2},{6,0},{8,14},{10,12},{12,10},{14,8},{16,22},{18,... | collective-permute-start | bytes 393224 | tf_op jit(solution)/shard_map/ppermute | solution.py:340
  54.8 8.5 %collective-permute-start.12 = (f32[256,128]{1,0:T(8,128)S(1)}, f32[256,128]{1,0:T(8,128)S(1)}, u32[]{:S(2)}, u32[]{:S(2)}) collective-permute-start(f32[256,128]{1,0:T(8,128)S(1)} %fusion.13), channel_id=1, source_target_pairs={{0,16},{2,18},{4,20},{6,22},{8,24},{10,26},{12,28},{14,30},{16,0},... | collective-permute-start | bytes 393224 | tf_op jit(solution)/shard_map/ppermute | solution.py:340
  63.3 6.9 %collective-permute-start.13 = (f32[256,128]{1,0:T(8,128)S(1)}, f32[256,128]{1,0:T(8,128)S(1)}, u32[]{:S(2)}, u32[]{:S(2)}) collective-permute-start(f32[256,128]{1,0:T(8,128)S(1)} %fusion.10), channel_id=1, source_target_pairs={{0,8},{2,10},{4,12},{6,14},{8,0},{10,2},{12,4},{14,6},{16,24},{18,... | collective-permute-start | bytes 393224 | tf_op jit(solution)/shard_map/ppermute | solution.py:340
  70.3 14.7 %collective-permute-start.16 = (f32[256,128]{1,0:T(8,128)S(1)}, f32[256,128]{1,0:T(8,128)S(1)}, u32[]{:S(2)}, u32[]{:S(2)}) collective-permute-start(f32[256,128]{1,0:T(8,128)S(1)} %get-tuple-element.64), channel_id=1, source_target_pairs={{0,2},{2,0},{4,6},{6,4},{8,10},{10,8},{12,14},{14,12},{16,18},{18,... | collective-permute-start | bytes 393224 | tf_op jit(solution)/shard_map/ppermute | solution.py:340
  70.4 17.9 %collective-permute-start.15 = (f32[256,128]{1,0:T(8,128)S(1)}, f32[256,128]{1,0:T(8,128)S(1)}, u32[]{:S(2)}, u32[]{:S(2)}) collective-permute-start(f32[256,128]{1,0:T(8,128)S(1)} %get-tuple-element.66), channel_id=1, source_target_pairs={{0,6},{2,4},{4,2},{6,0},{8,14},{10,12},{12,10},{14,8},{16,22},{18,... | collective-permute-start | bytes 393224 | tf_op jit(solution)/shard_map/ppermute | solution.py:340
  72.0 16.4 %collective-permute-start.14 = (f32[256,128]{1,0:T(8,128)S(1)}, f32[256,128]{1,0:T(8,128)S(1)}, u32[]{:S(2)}, u32[]{:S(2)}) collective-permute-start(f32[256,128]{1,0:T(8,128)S(1)} %fusion.28), channel_id=1, source_target_pairs={{0,4},{2,6},{4,0},{6,2},{8,12},{10,14},{12,8},{14,10},{16,20},{18,... | collective-permute-start | bytes 393224 | tf_op jit(solution)/shard_map/ppermute | solution.py:340

commit v2 on v1

--- a/solution.py
+++ b/solution.py
@@ -166,7 +166,8 @@
                 part[r, c] = dot(cat(tiles[n][r, :], q[r, c], 1), cat(v[r, c], maps[h, i], 0), 1, 0)
 
 
-def scale_kernel(pieces, u, gain, scaled, zeros, spot):
+def scale_kernel(pieces, u, gain, send, scaled, zeros, spot, own):
+    own[...] = send[...]
     zeros[...] = jnp.zeros_like(zeros)
     spot[0] = place(pieces)
 
@@ -218,13 +219,13 @@
 
 
 def token_factors(stats, features, inv_s, beta_s):
-    @pl.loop(0, stats.shape[1] // CHUNK)
-    def _(step):
-        r = pl.ds(pl.multiple_of(step * CHUNK, CHUNK), CHUNK)
-        inv = lax.rsqrt(stats[0:1, r] / features + 1e-06)
-        inv_s[r, :] = jnp.broadcast_to(inv, (CHUNK, CHUNK)).T
-        beta = inv * inv * inv * stats[1:2, r] / features
-        beta_s[r, :] = jnp.broadcast_to(beta, (CHUNK, CHUNK)).T
+    inv = lax.rsqrt(stats[0:1, :] / features + 1e-06)
+    beta = inv * inv * inv * stats[1:2, :] / features
+    both = jnp.concatenate([inv, beta, jnp.zeros((6, inv.shape[1]), F32)], 0)
+    for r in chunk_rows(stats.shape[1]):
+        turned = both[:, r].T
+        inv_s[r, :] = jnp.broadcast_to(turned[:, 0:1], (CHUNK, CHUNK))
+        beta_s[r, :] = jnp.broadcast_to(turned[:, 1:2], (CHUNK, CHUNK))
 
 
 def grad_kernel(pieces, each, features, q, att, scaled, stats, grad, *refs):
@@ -232,17 +233,14 @@
     token_factors(stats, features, inv, beta)
     groups = q.shape[0] // GROUP
 
-    sums[...] = jnp.zeros_like(sums)
-
-    @pl.loop(0, q.shape[0] // ROWS)
-    def _(step):
-        r = pl.ds(pl.multiple_of(step * ROWS, ROWS), ROWS)
-        group = (step * ROWS) // GROUP
+    for start in range(0, q.shape[0], ROWS):
+        r = slice(start, start + ROWS)
         for h in range(q.shape[1] // D):
             c = slice(h * D, (h + 1) * D)
             gr = (inv[r, :] * scaled[r, c] - att[r, c] * beta[r, :]).astype(BF16)
             grad[r, c] = gr
-            sums[h, group] += dot(q[r, c], gr, 0, 0)
+            y = dot(q[r, c], gr, 0, 0)
+            sums[h, start // GROUP] = y if start % GROUP == 0 else sums[h, start // GROUP] + y
 
     for m, out in enumerate(outs):
         for g in range(groups):
@@ -273,8 +271,8 @@
 
 
 def normed_kernel(features, att, stats, gain, normed):
-    for n in range(ROWS // CHUNK):
-        start = pl.program_id(0) * ROWS + n * CHUNK
+    for n in range(WIDE // CHUNK):
+        start = pl.program_id(0) * WIDE + n * CHUNK
         b = pl.ds(pl.multiple_of(start, CHUNK), CHUNK)
         inv = jnp.broadcast_to(lax.rsqrt(stats[0:1, b] / features + 1e-06), (CHUNK, CHUNK)).T
         for h in range(att.shape[1] // D):
@@ -314,15 +312,14 @@
 
 def outer_kernel(base, count, each, pref, k, v, key_in, value_in, *refs):
     far, (dk, dv, maps) = refs[:count], refs[-3:]
-    j, step = pl.program_id(0), pl.program_id(1)
-
-    @pl.when((j == 0) & (step == 0))
+    j = pl.program_id(0)
+
+    @pl.when(j == 0)
     def _():
         for n, piece in enumerate(far):
             for i in range(each):
                 maps[n * each + i] = piece[i * D : (i + 1) * D, :].astype(BF16)
 
-    r = pl.ds(pl.multiple_of(step * WIDE, WIDE), WIDE)
     for part in range(k.shape[1] // D // each):
 
         @pl.when((base + j) ^ pref[0] == part)
@@ -331,8 +328,8 @@
                 c = slice((part * each + i) * D, (part * each + i + 1) * D)
                 here = slice(i * D, (i + 1) * D)
                 m = maps[j * each + i]
-                dk[:, here] = (key_in[r, c] + dot(v[r, c], m, 1, 1)).astype(BF16)
-                dv[:, here] = (value_in[r, c] + dot(k[r, c], m, 1, 0)).astype(BF16)
+                dk[:, here] = (key_in[:, c] + dot(v[:, c], m, 1, 1)).astype(BF16)
+                dv[:, here] = (value_in[:, c] + dot(k[:, c], m, 1, 0)).astype(BF16)
 
 
 def exchange(x, axis, distance):
@@ -498,13 +495,13 @@
         [wide, jax.ShapeDtypeStruct((heads, chunks, D, D), BF16), narrow],
         [tile16] * pair,
     )(codes, query_rows, key_rows, value_rows)
-    scaled, stats, pref = call(
+    scaled, stats, pref, sends[0] = call(
         functools.partial(scale_kernel, pieces),
         1,
-        [vmem, vmem],
-        [wide, sums, jax.ShapeDtypeStruct((1,), jnp.int32)],
-        out_specs=[vmem, vmem, smem],
-    )(upstream, gain)
+        [vmem] * 3,
+        [wide, sums, jax.ShapeDtypeStruct((1,), jnp.int32), jax.ShapeDtypeStruct(sends[0].shape, F32)],
+        out_specs=[vmem, vmem, smem, vmem],
+    )(upstream, gain, sends[0])
 
     far_maps, ext = far.forward(sends)
     if not far.fast:
@@ -548,8 +545,8 @@
         1,
         [vmem] * 3,
         [narrow],
-        grid=(tokens // ROWS,),
-        out_specs=[pl.BlockSpec((ROWS, width), lambda i: (i, 0))],
+        grid=(tokens // WIDE,),
+        out_specs=[pl.BlockSpec((WIDE, width), lambda i: (i, 0))],
     )(att, stats, gain)[0]
     key_in, readers = call(
         key_kernel, 4, [smem] + [vmem] * 3, [wide, jax.ShapeDtypeStruct((heads, chunks, D, D), BF16)], [tile16, tile32]
@@ -563,7 +560,7 @@
     done = []
     for offsets in turns:
         base, count = offsets[0], len(offsets)
-        block = pl.BlockSpec((WIDE, each * D), lambda j, i, pref, base=base: (i, (base + j) ^ pref[0]))
+        block = pl.BlockSpec((tokens, each * D), lambda j, pref, base=base: (0, (base + j) ^ pref[0]))
         done = call(
             functools.partial(outer_kernel, base, count, each),
             2 / len(turns),
@@ -571,7 +568,7 @@
             [narrow, narrow],
             grid_spec=pltpu.PrefetchScalarGridSpec(
                 num_scalar_prefetch=1,
-                grid=(count, tokens // WIDE),
+                grid=(count,),
                 in_specs=[vmem] * (4 + count) + [pl.BlockSpec(memory_space=pl.ANY)] * len(done),
                 out_specs=[block, block],
                 scratch_shapes=[pltpu.VMEM((count * each, D, D), BF16)],

time: 91.9 us -> 89.8 us (0.977)
  Pallas kernels: 40.6 us -> 38.6 us
    pallas_call x2, Pallas kernels: 6.59 us -> 5.47 us  [local(): call(functools.partial(outer_kernel, base, count, each), 2 / len(turns),...]
  transfers between devices with their start and end apart: 17 -> 17, of which waited for: 9 -> 9; matrix products, arithmetic and copies ran while one was open for 1% -> 0% of each run, Pallas kernels for 32% -> 32%
where the time goes in v2:
time: 89.8 us; the launch traced here: 89.6 us
  Pallas kernels  38.6 us (43%)
  waiting for transfers between devices  27.1 us (30%)
  starting transfers between devices  21.6 us (24%)
  local copies, waits for them, and re-layouts  0.95 us (1%)
    ppermute x17, waiting for transfers between devices, exchange(): return lax.ppermute(x, axis, [(i, i ^ distance) for i in range(count)])  27.1 us
    ppermute x17, starting transfers between devices, exchange(): return lax.ppermute(x, axis, [(i, i ^ distance) for i in range(count)])  21.6 us
    pallas_call x1, Pallas kernels, local(): call(key_kernel, 4, [smem] + [vmem] * 3, [wide, jax.ShapeDtypeStruct((hea...  6.81 us
    pallas_call x1, Pallas kernels, local(): call(functools.partial(query_kernel, pieces, each), 3, [smem] + [vmem] *...  6.02 us
    pallas_call x1, Pallas kernels, local(): call(functools.partial(inside_kernel, pair), 5, [smem, vmem, vmem, vmem],...  5.97 us
    pallas_call x2, Pallas kernels, local(): call(functools.partial(outer_kernel, base, count, each), 2 / len(turns),...  5.47 us
    pallas_call x1, Pallas kernels, local(): call(functools.partial(state_kernel, pieces, each, (first_far, far.bits))...  3.66 us
    pallas_call x2, Pallas kernels, local(): call(functools.partial(attend_kernel, offsets, pieces, each), 1, [vmem] *...  2.95 us
  transfers between devices with their start and end apart: 17, of which 9 were waited for; matrix products, arithmetic and copies ran while one was open for 0% of the time, Pallas kernels for 32%

profile of v2, /device:TPU:0, one launch (start us, length us, event | category | flops | bytes accessed | tf_op | source)
XLA Modules:
  0.0 89.6 jit_solution(4056901950702824760)
XLA Ops:
  0.7 3.7 %shard_map.94 = (f32[264,128]{1,0:T(8,128)}, f32[264,128]{1,0:T(8,128)}, f32[264,128]{1,0:T(8,128)}, f32[264,128]{1,0:T(8,128)}) custom-call(s32[1,8,20]{2,1,0:T(8,128)} %bitcast.238, bf16[1024,1024]{1,0:T(8,128)(2,1)} %k.9, bf16[1024,1024]{1,0:T(8,128)(2,1)} %v.9), custom_call_target="tpu_custom_call" | custom-call | flops 268435456 | bytes 8388608 | tf_op jit(solution)/shard_map/pallas_call | solution.py:462
  4.3 3.0 %collective-permute-start = (f32[264,128]{1,0:T(8,128)}, f32[264,128]{1,0:T(8,128)S(1)}, u32[]{:S(2)}, u32[]{:S(2)}) collective-permute-start(f32[264,128]{1,0:T(8,128)} %get-tuple-element.39), channel_id=1, source_target_pairs={{0,2},{2,0},{4,6},{6,4},{8,10},{10,8},{12,14},{14,12},{16,18},{18,... | collective-permute-start | bytes 405512 | tf_op jit(solution)/shard_map/ppermute | solution.py:337
  7.4 1.5 %collective-permute-start.1 = (f32[264,128]{1,0:T(8,128)}, f32[264,128]{1,0:T(8,128)S(1)}, u32[]{:S(2)}, u32[]{:S(2)}) collective-permute-start(f32[264,128]{1,0:T(8,128)} %get-tuple-element.40), channel_id=1, source_target_pairs={{0,4},{2,6},{4,0},{6,2},{8,12},{10,14},{12,8},{14,10},{16,20},{18,... | collective-permute-start | bytes 405512 | tf_op jit(solution)/shard_map/ppermute | solution.py:337
  11.7 3.9 %collective-permute-done.1 = f32[264,128]{1,0:T(8,128)S(1)} collective-permute-done((f32[264,128]{1,0:T(8,128)}, f32[264,128]{1,0:T(8,128)S(1)}, u32[]{:S(2)}, u32[]{:S(2)}) %collective-permute-start.1) | collective-permute-done | bytes 135200 | tf_op jit(solution)/shard_map/ppermute | solution.py:337
  15.6 1.6 %collective-permute-start.3 = (f32[256,128]{1,0:T(8,128)S(1)}, f32[256,128]{1,0:T(8,128)S(1)}, u32[]{:S(2)}, u32[]{:S(2)}) collective-permute-start(f32[256,128]{1,0:T(8,128)S(1)} %add_add_fusion), channel_id=1, source_target_pairs={{0,8},{2,10},{4,12},{6,14},{8,0},{10,2},{12,4},{14,6},{16,24},{18,... | collective-permute-start | bytes 393224 | tf_op jit(solution)/shard_map/ppermute | solution.py:337
  17.2 3.4 %collective-permute-done.3 = f32[256,128]{1,0:T(8,128)S(1)} collective-permute-done((f32[256,128]{1,0:T(8,128)S(1)}, f32[256,128]{1,0:T(8,128)S(1)}, u32[]{:S(2)}, u32[]{:S(2)}) %collective-permute-start.3) | collective-permute-done | bytes 131104 | tf_op jit(solution)/shard_map/ppermute | solution.py:337
  20.6 2.7 %collective-permute-start.4 = (f32[256,128]{1,0:T(8,128)S(1)}, f32[256,128]{1,0:T(8,128)S(1)}, u32[]{:S(2)}, u32[]{:S(2)}) collective-permute-start(f32[256,128]{1,0:T(8,128)S(1)} %add.227), channel_id=1, source_target_pairs={{0,16},{2,18},{4,20},{6,22},{8,24},{10,26},{12,28},{14,30},{16,0},... | collective-permute-start | bytes 393224 | tf_op jit(solution)/shard_map/ppermute | solution.py:337
  23.3 4.7 %collective-permute-done.4 = f32[256,128]{1,0:T(8,128)S(1)} collective-permute-done((f32[256,128]{1,0:T(8,128)S(1)}, f32[256,128]{1,0:T(8,128)S(1)}, u32[]{:S(2)}, u32[]{:S(2)}) %collective-permute-start.4) | collective-permute-done | bytes 131104 | tf_op jit(solution)/shard_map/ppermute | solution.py:337
  31.9 6.0 %shard_map.93 = (f32[1024,1024]{1,0:T(8,128)S(1)}, bf16[8,8,128,128]{3,2,1,0:T(8,128)(2,1)S(1)}, bf16[1024,1024]{1,0:T(8,128)(2,1)S(1)}) custom-call(s32[1,8,20]{2,1,0:T(8,128)S(1)} %bitcast.239, bf16[1024,1024]{1,0:T(8,128)(2,1)S(1)} %copy-done.2, bf16[1024,1024]{1,0:T(8,128)(2,1)S(1)} %copy-done, bf16[1024,1024]{1,0:T(8,128)(2,1)S(1)} %copy-done.1), custom_call_target="tpu_custom_call" | custom-call | flops 1342177280 | bytes 8388608 | tf_op jit(solution)/shard_map/pallas_call | solution.py:491
  39.3 1.6 %shard_map.97 = (f32[1024,1024]{1,0:T(8,128)S(1)}, f32[2,1024]{1,0:T(2,128)S(1)}) custom-call(bf16[1024,1024]{1,0:T(8,128)(2,1)S(1)} %copy-done.2, f32[1024,1024]{1,0:T(8,128)S(1)} %get-tuple-element.42.part, f32[1024,1024]{1,0:T(8,128)S(1)} %get-tuple-element.36.scaled, f32[2,1024]{1,0:T(2,128)S(1)} %get-tuple-element.43.stats_in, ...), custom_call_target="tpu_custom_call", output_to_operand_aliasing={{0}: (1, {})} | custom-call | flops 268435456 | bytes 8388608 | tf_op jit(solution)/shard_map/pallas_call | solution.py:512
  42.1 2.4 %shard_map.99 = (bf16[1024,1024]{1,0:T(8,128)(2,1)S(1)}, f32[1,256,128]{2,1,0:T(8,128)S(1)}, f32[1,256,128]{2,1,0:T(8,128)S(1)}, f32[1,256,128]{2,1,0:T(8,128)S(1)}, f32[1,256,128]{2,1,0:T(8,128)S(1)}) custom-call(bf16[1024,1024]{1,0:T(8,128)(2,1)S(1)} %copy-done.2, f32[1024,1024]{1,0:T(8,128)S(1)} %get-tuple-element.44.att, ...), custom_call_target="tpu_custom_call" | custom-call | flops 268435456 | bytes 8388608 | tf_op jit(solution)/shard_map/pallas_call | solution.py:523
  48.1 2.9 %collective-permute-done.9 = f32[1,256,128]{2,1,0:T(8,128)S(1)} collective-permute-done((f32[1,256,128]{2,1,0:T(8,128)S(1)}, f32[1,256,128]{2,1,0:T(8,128)S(1)}, u32[]{:S(2)}, u32[]{:S(2)}) %collective-permute-start.9) | collective-permute-done | bytes 131104 | tf_op jit(solution)/shard_map/ppermute | solution.py:337
  51.0 1.6 %collective-permute-done.10 = f32[1,256,128]{2,1,0:T(8,128)S(1)} collective-permute-done((f32[1,256,128]{2,1,0:T(8,128)S(1)}, f32[1,256,128]{2,1,0:T(8,128)S(1)}, u32[]{:S(2)}, u32[]{:S(2)}) %collective-permute-start.10) | collective-permute-done | bytes 131104 | tf_op jit(solution)/shard_map/ppermute | solution.py:337
  52.6 1.8 %collective-permute-done.11 = f32[1,256,128]{2,1,0:T(8,128)S(1)} collective-permute-done((f32[1,256,128]{2,1,0:T(8,128)S(1)}, f32[1,256,128]{2,1,0:T(8,128)S(1)}, u32[]{:S(2)}, u32[]{:S(2)}) %collective-permute-start.11) | collective-permute-done | bytes 131104 | tf_op jit(solution)/shard_map/ppermute | solution.py:337
  54.4 1.7 %collective-permute-start.12 = (f32[256,128]{1,0:T(8,128)S(1)}, f32[256,128]{1,0:T(8,128)S(1)}, u32[]{:S(2)}, u32[]{:S(2)}) collective-permute-start(f32[256,128]{1,0:T(8,128)S(1)} %fusion.13), channel_id=1, source_target_pairs={{0,16},{2,18},{4,20},{6,22},{8,24},{10,26},{12,28},{14,30},{16,0},... | collective-permute-start | bytes 393224 | tf_op jit(solution)/shard_map/ppermute | solution.py:337
  56.1 6.8 %collective-permute-done.12 = f32[256,128]{1,0:T(8,128)S(1)} collective-permute-done((f32[256,128]{1,0:T(8,128)S(1)}, f32[256,128]{1,0:T(8,128)S(1)}, u32[]{:S(2)}, u32[]{:S(2)}) %collective-permute-start.12) | collective-permute-done | bytes 131104 | tf_op jit(solution)/shard_map/ppermute | solution.py:337
  63.1 6.8 %shard_map.101 = (f32[1024,1024]{1,0:T(8,128)S(1)}, bf16[8,8,128,128]{3,2,1,0:T(8,128)(2,1)S(1)}) custom-call(s32[1,8,20]{2,1,0:T(8,128)S(1)} %bitcast.240, bf16[1024,1024]{1,0:T(8,128)(2,1)S(1)} %copy-done.2, bf16[1024,1024]{1,0:T(8,128)(2,1)S(1)} %copy-done.1, bf16[1024,1024]{1,0:T(8,128)(2,1)S(1)} %get-tuple-element.46.grad), custom_call_target="tpu_custom_call" | custom-call | flops 1073741824 | bytes 8388608 | tf_op jit(solution)/shard_map/pallas_call | solution.py:551
  70.1 1.6 %collective-permute-start.15 = (f32[256,128]{1,0:T(8,128)S(1)}, f32[256,128]{1,0:T(8,128)S(1)}, u32[]{:S(2)}, u32[]{:S(2)}) collective-permute-start(f32[256,128]{1,0:T(8,128)S(1)} %get-tuple-element.68), channel_id=1, source_target_pairs={{0,6},{2,4},{4,2},{6,0},{8,14},{10,12},{12,10},{14,8},{16,22},{18,... | collective-permute-start | bytes 393224 | tf_op jit(solution)/shard_map/ppermute | solution.py:337
  71.7 1.9 %collective-permute-start.14 = (f32[256,128]{1,0:T(8,128)S(1)}, f32[256,128]{1,0:T(8,128)S(1)}, u32[]{:S(2)}, u32[]{:S(2)}) collective-permute-start(f32[256,128]{1,0:T(8,128)S(1)} %fusion.28), channel_id=1, source_target_pairs={{0,4},{2,6},{4,0},{6,2},{8,12},{10,14},{12,8},{14,10},{16,20},{18,... | collective-permute-start | bytes 393224 | tf_op jit(solution)/shard_map/ppermute | solution.py:337
  73.6 2.8 %shard_map.102.value_in = f32[1024,1024]{1,0:T(8,128)S(1)} custom-call(bf16[1024,1024]{1,0:T(8,128)(2,1)S(1)} %copy-done, bf16[1024,1024]{1,0:T(8,128)(2,1)S(1)} %get-tuple-element.46.grad, bf16[1024,1024]{1,0:T(8,128)(2,1)S(1)} %get-tuple-element.50.att_t, bf16[8,8,128,128]{3,2,1,0:T(8,128)(2,1)S(1)} %get-tuple-element.51.readers), custom_call_target="tpu_custom_call" | custom-call | flops 536870912 | bytes 8388608 | tf_op jit(solution)/shard_map/pallas_call | solution.py:554
  76.5 1.7 %shard_map.98 = bf16[1024,1024]{1,0:T(8,128)(2,1)} custom-call(f32[1024,1024]{1,0:T(8,128)S(1)} %get-tuple-element.44.att, f32[2,1024]{1,0:T(2,128)S(1)} %add.245.stats, f32[1,1024]{1,0:T(1,128)S(1)} %bitcast.243), custom_call_target="tpu_custom_call" | custom-call | flops 268435456 | bytes 8388608 | tf_op jit(solution)/shard_map/pallas_call | solution.py:543
  78.1 6.0 %shard_map.100 = bf16[1024,1024]{1,0:T(8,128)(2,1)} custom-call(s32[1,8,20]{2,1,0:T(8,128)S(1)} %bitcast.241, bf16[1024,1024]{1,0:T(8,128)(2,1)S(1)} %copy-done, bf16[1024,1024]{1,0:T(8,128)(2,1)S(1)} %copy-done.1, bf16[1024,1024]{1,0:T(8,128)(2,1)S(1)} %get-tuple-element.46.grad, bf16[8,8,128,128]{3,2,1,0:T(8,128)(2,1)S(1)} %get-tuple-element.47.maps, ...), custom_call_target="tpu_custom_call" | custom-call | flops 805306368 | bytes 8388608 | tf_op jit(solution)/shard_map/pallas_call | solution.py:534
  84.2 2.8 %shard_map.103 = (bf16[1024,1024]{1,0:T(8,128)(2,1)}, bf16[1024,1024]{1,0:T(8,128)(2,1)}) custom-call(s32[1]{0:T(128)} %get-tuple-element.48.pref, bf16[1024,1024]{1,0:T(8,128)(2,1)S(1)} %copy-done, bf16[1024,1024]{1,0:T(8,128)(2,1)S(1)} %copy-done.1, f32[1024,1024]{1,0:T(8,128)S(1)} %get-tuple-element.49.key_in, f32[1024,1024]{1,0:T(8,128)S(1)} %shard_map.102.value_in, ...), custom_call_target="tpu_custom_call" | custom-call | flops 268435456 | bytes 8388608 | tf_op jit(solution)/shard_map/pallas_call | solution.py:564
  86.9 2.7 %shard_map.104 = (bf16[1024,1024]{1,0:T(8,128)(2,1)}, bf16[1024,1024]{1,0:T(8,128)(2,1)}) custom-call(s32[1]{0:T(128)} %get-tuple-element.48.pref, bf16[1024,1024]{1,0:T(8,128)(2,1)S(1)} %copy-done, bf16[1024,1024]{1,0:T(8,128)(2,1)S(1)} %copy-done.1, f32[1024,1024]{1,0:T(8,128)S(1)} %get-tuple-element.49.key_in, ...), custom_call_target="tpu_custom_call", output_to_operand_aliasing={{0}: (7, {}), {1}: (8, {})} | custom-call | flops 268435456 | bytes 8388608 | tf_op jit(solution)/shard_map/pallas_call | solution.py:564
  (53 shorter events, 13.3 us)
Async XLA Ops:
  0.6 8.3 %copy-start.3 = (bf16[1024,1024]{1,0:T(8,128)(2,1)S(1)}, bf16[1024,1024]{1,0:T(8,128)(2,1)}, u32[]{:S(2)}) copy-start(bf16[1024,1024]{1,0:T(8,128)(2,1)} %u) | copy-start | bytes 6291460
  0.6 8.3 %copy-start.6 = (f32[1024]{0:T(1024)S(1)}, f32[1024]{0:T(1024)}, u32[]{:S(2)}) copy-start(f32[1024]{0:T(1024)} %param.10) | copy-start | bytes 12292
  0.7 31.2 %copy-start.2 = (bf16[1024,1024]{1,0:T(8,128)(2,1)S(1)}, bf16[1024,1024]{1,0:T(8,128)(2,1)}, u32[]{:S(2)}) copy-start(bf16[1024,1024]{1,0:T(8,128)(2,1)} %q.9) | copy-start | bytes 6291460
  4.3 7.3 %collective-permute-start = (f32[264,128]{1,0:T(8,128)}, f32[264,128]{1,0:T(8,128)S(1)}, u32[]{:S(2)}, u32[]{:S(2)}) collective-permute-start(f32[264,128]{1,0:T(8,128)} %get-tuple-element.39), channel_id=1, source_target_pairs={{0,2},{2,0},{4,6},{6,4},{8,10},{10,8},{12,14},{14,12},{16,18},{18,... | collective-permute-start | bytes 405512 | tf_op jit(solution)/shard_map/ppermute | solution.py:337
  7.4 8.1 %collective-permute-start.1 = (f32[264,128]{1,0:T(8,128)}, f32[264,128]{1,0:T(8,128)S(1)}, u32[]{:S(2)}, u32[]{:S(2)}) collective-permute-start(f32[264,128]{1,0:T(8,128)} %get-tuple-element.40), channel_id=1, source_target_pairs={{0,4},{2,6},{4,0},{6,2},{8,12},{10,14},{12,8},{14,10},{16,20},{18,... | collective-permute-start | bytes 405512 | tf_op jit(solution)/shard_map/ppermute | solution.py:337
  8.9 6.6 %collective-permute-start.2 = (f32[264,128]{1,0:T(8,128)}, f32[264,128]{1,0:T(8,128)S(1)}, u32[]{:S(2)}, u32[]{:S(2)}) collective-permute-start(f32[264,128]{1,0:T(8,128)} %get-tuple-element.41), channel_id=1, source_target_pairs={{0,6},{2,4},{4,2},{6,0},{8,14},{10,12},{12,10},{14,8},{16,22},{18,... | collective-permute-start | bytes 405512 | tf_op jit(solution)/shard_map/ppermute | solution.py:337
  8.9 0.9 %copy-start.4 = (f32[264,128]{1,0:T(8,128)S(1)}, f32[264,128]{1,0:T(8,128)}, u32[]{:S(2)}) copy-start(f32[264,128]{1,0:T(8,128)} %get-tuple-element.35.send) | copy-start | bytes 405508
  9.8 22.1 %copy-start.1 = (bf16[1024,1024]{1,0:T(8,128)(2,1)S(1)}, bf16[1024,1024]{1,0:T(8,128)(2,1)}, u32[]{:S(2)}) copy-start(bf16[1024,1024]{1,0:T(8,128)(2,1)} %v.9) | copy-start | bytes 6291460
  10.6 21.3 %copy-start = (bf16[1024,1024]{1,0:T(8,128)(2,1)S(1)}, bf16[1024,1024]{1,0:T(8,128)(2,1)}, u32[]{:S(2)}) copy-start(bf16[1024,1024]{1,0:T(8,128)(2,1)} %k.9) | copy-start | bytes 6291460
  10.6 21.3 %copy-start.5 = (s32[1,20,8]{1,2,0:T(8,128)S(1)}, s32[1,20,8]{1,2,0:T(8,128)}, u32[]{:S(2)}) copy-start(s32[1,20,8]{1,2,0:T(8,128)} %param.9) | copy-start | bytes 1924
  15.6 5.0 %collective-permute-start.3 = (f32[256,128]{1,0:T(8,128)S(1)}, f32[256,128]{1,0:T(8,128)S(1)}, u32[]{:S(2)}, u32[]{:S(2)}) collective-permute-start(f32[256,128]{1,0:T(8,128)S(1)} %add_add_fusion), channel_id=1, source_target_pairs={{0,8},{2,10},{4,12},{6,14},{8,0},{10,2},{12,4},{14,6},{16,24},{18,... | collective-permute-start | bytes 393224 | tf_op jit(solution)/shard_map/ppermute | solution.py:337
  20.6 7.3 %collective-permute-start.4 = (f32[256,128]{1,0:T(8,128)S(1)}, f32[256,128]{1,0:T(8,128)S(1)}, u32[]{:S(2)}, u32[]{:S(2)}) collective-permute-start(f32[256,128]{1,0:T(8,128)S(1)} %add.227), channel_id=1, source_target_pairs={{0,16},{2,18},{4,20},{6,22},{8,24},{10,26},{12,28},{14,30},{16,0},... | collective-permute-start | bytes 393224 | tf_op jit(solution)/shard_map/ppermute | solution.py:337
  28.1 9.8 %collective-permute-start.5 = (f32[1,256,128]{2,1,0:T(8,128)S(1)}, f32[1,256,128]{2,1,0:T(8,128)S(1)}, u32[]{:S(2)}, u32[]{:S(2)}) collective-permute-start(f32[1,256,128]{2,1,0:T(8,128)S(1)} %bitcast.244), channel_id=1, source_target_pairs={{0,2},{2,0},{4,6},{6,4},{8,10},{10,8},{12,14},{14,12},{16,18},{18,... | collective-permute-start | bytes 393224 | tf_op jit(solution)/shard_map/ppermute | solution.py:337
  29.4 9.9 %collective-permute-start.6 = (f32[1,256,128]{2,1,0:T(8,128)S(1)}, f32[1,256,128]{2,1,0:T(8,128)S(1)}, u32[]{:S(2)}, u32[]{:S(2)}) collective-permute-start(f32[1,256,128]{2,1,0:T(8,128)S(1)} %bitcast.246), channel_id=1, source_target_pairs={{0,4},{2,6},{4,0},{6,2},{8,12},{10,14},{12,8},{14,10},{16,20},{18,... | collective-permute-start | bytes 393224 | tf_op jit(solution)/shard_map/ppermute | solution.py:337
  30.4 8.9 %collective-permute-start.7 = (f32[1,256,128]{2,1,0:T(8,128)S(1)}, f32[1,256,128]{2,1,0:T(8,128)S(1)}, u32[]{:S(2)}, u32[]{:S(2)}) collective-permute-start(f32[1,256,128]{2,1,0:T(8,128)S(1)} %bitcast.245), channel_id=1, source_target_pairs={{0,6},{2,4},{4,2},{6,0},{8,14},{10,12},{12,10},{14,8},{16,22},{18,... | collective-permute-start | bytes 393224 | tf_op jit(solution)/shard_map/ppermute | solution.py:337
  40.9 1.2 %collective-permute-start.8 = (f32[2,1024]{1,0:T(2,128)S(1)}, f32[2,1024]{1,0:T(2,128)S(1)}, u32[]{:S(2)}, u32[]{:S(2)}) collective-permute-start(f32[2,1024]{1,0:T(2,128)S(1)} %get-tuple-element.45), channel_id=1, source_target_pairs={{0,1},{1,0},{2,3},{3,2},{4,5},{5,4},{6,7},{7,6},{8,9},{9,8},{10,11... | collective-permute-start | bytes 24584 | tf_op jit(solution)/shard_map/ppermute | solution.py:337
  44.6 6.4 %collective-permute-start.9 = (f32[1,256,128]{2,1,0:T(8,128)S(1)}, f32[1,256,128]{2,1,0:T(8,128)S(1)}, u32[]{:S(2)}, u32[]{:S(2)}) collective-permute-start(f32[1,256,128]{2,1,0:T(8,128)S(1)} %get-tuple-element.53), channel_id=1, source_target_pairs={{0,2},{2,0},{4,6},{6,4},{8,10},{10,8},{12,14},{14,12},{16,18},{18,... | collective-permute-start | bytes 393224 | tf_op jit(solution)/shard_map/ppermute | solution.py:337
  45.7 6.8 %collective-permute-start.10 = (f32[1,256,128]{2,1,0:T(8,128)S(1)}, f32[1,256,128]{2,1,0:T(8,128)S(1)}, u32[]{:S(2)}, u32[]{:S(2)}) collective-permute-start(f32[1,256,128]{2,1,0:T(8,128)S(1)} %get-tuple-element.54), channel_id=1, source_target_pairs={{0,4},{2,6},{4,0},{6,2},{8,12},{10,14},{12,8},{14,10},{16,20},{18,... | collective-permute-start | bytes 393224 | tf_op jit(solution)/shard_map/ppermute | solution.py:337
  46.7 7.7 %collective-permute-start.11 = (f32[1,256,128]{2,1,0:T(8,128)S(1)}, f32[1,256,128]{2,1,0:T(8,128)S(1)}, u32[]{:S(2)}, u32[]{:S(2)}) collective-permute-start(f32[1,256,128]{2,1,0:T(8,128)S(1)} %get-tuple-element.55), channel_id=1, source_target_pairs={{0,6},{2,4},{4,2},{6,0},{8,14},{10,12},{12,10},{14,8},{16,22},{18,... | collective-permute-start | bytes 393224 | tf_op jit(solution)/shard_map/ppermute | solution.py:337
  54.4 8.5 %collective-permute-start.12 = (f32[256,128]{1,0:T(8,128)S(1)}, f32[256,128]{1,0:T(8,128)S(1)}, u32[]{:S(2)}, u32[]{:S(2)}) collective-permute-start(f32[256,128]{1,0:T(8,128)S(1)} %fusion.13), channel_id=1, source_target_pairs={{0,16},{2,18},{4,20},{6,22},{8,24},{10,26},{12,28},{14,30},{16,0},... | collective-permute-start | bytes 393224 | tf_op jit(solution)/shard_map/ppermute | solution.py:337
  63.0 6.9 %collective-permute-start.13 = (f32[256,128]{1,0:T(8,128)S(1)}, f32[256,128]{1,0:T(8,128)S(1)}, u32[]{:S(2)}, u32[]{:S(2)}) collective-permute-start(f32[256,128]{1,0:T(8,128)S(1)} %fusion.10), channel_id=1, source_target_pairs={{0,8},{2,10},{4,12},{6,14},{8,0},{10,2},{12,4},{14,6},{16,24},{18,... | collective-permute-start | bytes 393224 | tf_op jit(solution)/shard_map/ppermute | solution.py:337
  70.0 14.2 %collective-permute-start.16 = (f32[256,128]{1,0:T(8,128)S(1)}, f32[256,128]{1,0:T(8,128)S(1)}, u32[]{:S(2)}, u32[]{:S(2)}) collective-permute-start(f32[256,128]{1,0:T(8,128)S(1)} %get-tuple-element.66), channel_id=1, source_target_pairs={{0,2},{2,0},{4,6},{6,4},{8,10},{10,8},{12,14},{14,12},{16,18},{18,... | collective-permute-start | bytes 393224 | tf_op jit(solution)/shard_map/ppermute | solution.py:337
  70.1 16.9 %collective-permute-start.15 = (f32[256,128]{1,0:T(8,128)S(1)}, f32[256,128]{1,0:T(8,128)S(1)}, u32[]{:S(2)}, u32[]{:S(2)}) collective-permute-start(f32[256,128]{1,0:T(8,128)S(1)} %get-tuple-element.68), channel_id=1, source_target_pairs={{0,6},{2,4},{4,2},{6,0},{8,14},{10,12},{12,10},{14,8},{16,22},{18,... | collective-permute-start | bytes 393224 | tf_op jit(solution)/shard_map/ppermute | solution.py:337
  71.7 15.2 %collective-permute-start.14 = (f32[256,128]{1,0:T(8,128)S(1)}, f32[256,128]{1,0:T(8,128)S(1)}, u32[]{:S(2)}, u32[]{:S(2)}) collective-permute-start(f32[256,128]{1,0:T(8,128)S(1)} %fusion.28), channel_id=1, source_target_pairs={{0,4},{2,6},{4,0},{6,2},{8,12},{10,14},{12,8},{14,10},{16,20},{18,... | collective-permute-start | bytes 393224 | tf_op jit(solution)/shard_map/ppermute | solution.py:337

commit v3 on v2

--- a/solution.py
+++ b/solution.py
@@ -104,7 +104,7 @@
 
 def state_kernel(parts, each, far, codes_hbm, k_hbm, v_hbm, *refs):
     outs, (k, v, state, codes, sems, codes_sem) = refs[:parts], refs[parts:]
-    blocks = [slice(i, i + ROWS) for i in range(0, k.shape[0], ROWS)]
+    blocks = chunk_rows(k.shape[0])
     copies = []
     for n, r in enumerate(blocks):
         pair = [
@@ -177,6 +177,13 @@
         scaled[r, :] = u[r, :].astype(F32) * gain[...]
 
 
+def turn_kernel(q, turned):
+    @pl.loop(0, q.shape[1] // D)
+    def _(h):
+        for r in chunk_rows(q.shape[0]):
+            turned[col(h), r] = q[r, col(h)].T
+
+
 def sort_pieces(pieces, each, p, out):
     for m, piece in enumerate(pieces):
         for g in range(piece.shape[0]):
@@ -228,18 +235,18 @@
         beta_s[r, :] = jnp.broadcast_to(turned[:, 1:2], (CHUNK, CHUNK))
 
 
-def grad_kernel(pieces, each, features, q, att, scaled, stats, grad, *refs):
+def grad_kernel(pieces, each, features, q_turned, att, scaled, stats, grad, *refs):
     outs, (inv, beta, sums) = refs[:pieces], refs[pieces:]
     token_factors(stats, features, inv, beta)
-    groups = q.shape[0] // GROUP
-
-    for start in range(0, q.shape[0], ROWS):
+    groups = att.shape[0] // GROUP
+
+    for start in range(0, att.shape[0], ROWS):
         r = slice(start, start + ROWS)
-        for h in range(q.shape[1] // D):
+        for h in range(att.shape[1] // D):
             c = slice(h * D, (h + 1) * D)
             gr = (inv[r, :] * scaled[r, c] - att[r, c] * beta[r, :]).astype(BF16)
             grad[r, c] = gr
-            y = dot(q[r, c], gr, 0, 0)
+            y = dot(q_turned[c, r], gr, 1, 0)
             sums[h, start // GROUP] = y if start % GROUP == 0 else sums[h, start // GROUP] + y
 
     for m, out in enumerate(outs):
@@ -248,26 +255,29 @@
                 out[g, i * D : (i + 1) * D, :] = sums[(m ^ place(pieces)) * each + i, g]
 
 
-def query_kernel(pieces, each, codes, k, v, grad, maps, *refs):
+def query_kernel(pair, pieces, each, codes, k, v, grad, maps, *refs):
     far, (dq, reach, tiles, outer) = refs[:pieces], refs[pieces:]
-    h = pl.program_id(0)
-
-    @pl.when(h == 0)
+
+    @pl.when(pl.program_id(0) == 0)
     def _():
         sort_pieces(far, each, place(pieces), reach)
 
-    c = col(h)
     rows = chunk_rows(k.shape[0])
     per_group = GROUP // CHUNK
-    for i, r in enumerate(rows):
-        if i % per_group == 0:
-            w = tile_weights(codes, i // per_group, h)
-        to = (maps[h, i].astype(F32) + reach[h, i // per_group]).astype(BF16)
-        y = dot(grad[r, c], cat(v[r, c], to, 0), 1, 1)
-        tiles[r, :] = (w * y[:, :D]).astype(BF16)
-        outer[r, :] = y[:, D:]
-    for r in rows:
-        dq[r, :] = (dot(tiles[r, :], k[r, c], 1, 0) + outer[r, :]).astype(BF16)
+    heads = [pl.program_id(0) * pair + n for n in range(pair)]
+    for n, h in enumerate(heads):
+        c = col(h)
+        for i, r in enumerate(rows):
+            if i % per_group == 0:
+                w = tile_weights(codes, i // per_group, h)
+            to = (maps[h, i].astype(F32) + reach[h, i // per_group]).astype(BF16)
+            y = dot(grad[r, c], cat(v[r, c], to, 0), 1, 1)
+            tiles[n, r, :] = (w * y[:, :D]).astype(BF16)
+            outer[n, r, :] = y[:, D:]
+    for n, h in enumerate(heads):
+        c = col(h)
+        for r in rows:
+            dq[r, n * D : (n + 1) * D] = (dot(tiles[n, r, :], k[r, c], 1, 0) + outer[n, r, :]).astype(BF16)
 
 
 def normed_kernel(features, att, stats, gain, normed):
@@ -280,24 +290,30 @@
             normed[n * CHUNK : (n + 1) * CHUNK, c] = (att[b, c] * inv * gain[:, c]).astype(BF16)
 
 
-def key_kernel(codes, q, v, grad, key_in, readers, tiles, outer):
+def key_kernel(pair, codes, q, v, grad, key_in, readers, tiles, outer):
     rows = chunk_rows(q.shape[0])
     per_group = GROUP // CHUNK
 
-    @pl.loop(0, q.shape[1] // D)
-    def _(h):
-        c = col(h)
-        sums = chunk_maps([dot(q[r, c], grad[r, c], 0, 0) for r in rows], codes, h, reverse=True)
-        for i in range(len(rows)):
-            readers[h, i] = bf16_map(sums[i])
-        for i, r in enumerate(rows):
-            if i % per_group == 0:
-                w = tile_weights(codes, i // per_group, h, transposed=True)
-            y = dot(v[r, c], cat(grad[r, c], readers[h, i], 0), 1, 1)
-            tiles[r, :] = (w * y[:, :D]).astype(BF16)
-            outer[r, :] = y[:, D:]
-        for r in rows:
-            key_in[r, c] = dot(tiles[r, :], q[r, c], 1, 0) + outer[r, :]
+    @pl.loop(0, q.shape[1] // D // pair)
+    def _(step):
+        heads = [step * pair + n for n in range(pair)]
+        for h in heads:
+            c = col(h)
+            sums = chunk_maps([dot(q[r, c], grad[r, c], 0, 0) for r in rows], codes, h, reverse=True)
+            for i in range(len(rows)):
+                readers[h, i] = bf16_map(sums[i])
+        for n, h in enumerate(heads):
+            c = col(h)
+            for i, r in enumerate(rows):
+                if i % per_group == 0:
+                    w = tile_weights(codes, i // per_group, h, transposed=True)
+                y = dot(v[r, c], cat(grad[r, c], readers[h, i], 0), 1, 1)
+                tiles[n, r, :] = (w * y[:, :D]).astype(BF16)
+                outer[n, r, :] = y[:, D:]
+        for n, h in enumerate(heads):
+            c = col(h)
+            for r in rows:
+                key_in[r, c] = dot(tiles[n, r, :], q[r, c], 1, 0) + outer[n, r, :]
 
 
 def value_kernel(k, grad, att_t, readers, value_in):
@@ -440,9 +456,13 @@
     wide = jax.ShapeDtypeStruct((tokens, width), F32)
     narrow = jax.ShapeDtypeStruct((tokens, width), BF16)
     sums = jax.ShapeDtypeStruct((2, tokens), F32)
-    turns = [(0, 1), (2, 3)] if pieces == 4 else [tuple(range(pieces))]
+    together = [tuple(range(pieces))]
+    up_turns = [(0, 1), (2,), (3,)] if pieces == 4 else together
+    down_turns = [(0,), (1,), (2, 3)] if pieces == 4 else together
     tile16 = pltpu.VMEM((tokens, D), BF16)
     tile32 = pltpu.VMEM((tokens, D), F32)
+    tiles16 = pltpu.VMEM((pair, tokens, D), BF16)
+    tiles32 = pltpu.VMEM((pair, tokens, D), F32)
     unit = tokens * D * D * heads
 
     def call(kernel, units, ins, outs, scratch=(), limit=12, **kw):
@@ -466,7 +486,7 @@
             [jax.ShapeDtypeStruct((far.rows + far.extra, D), F32)] * pieces,
             [pltpu.VMEM((tokens, width), BF16)] * 2
             + [pltpu.VMEM((heads, D, D), F32), pltpu.SMEM(codes.shape, jnp.int32)]
-            + [pltpu.SemaphoreType.DMA((2, tokens // ROWS)), pltpu.SemaphoreType.DMA],
+            + [pltpu.SemaphoreType.DMA((2, tokens // CHUNK)), pltpu.SemaphoreType.DMA],
             limit=58,
         )(codes, key_rows, value_rows)
         sends = list(sends)
@@ -488,6 +508,7 @@
             sends.append(jnp.concatenate([piece, jnp.broadcast_to(w, (far.extra, D))], 0))
 
     upstream, sends[1] = lax.optimization_barrier((upstream, sends[1]))
+    q_turned = call(turn_kernel, 1, [vmem], [jax.ShapeDtypeStruct((width, tokens), BF16)])(query_rows)[0]
     part, maps, att_t = call(
         functools.partial(inside_kernel, pair),
         5,
@@ -508,7 +529,7 @@
         far_maps = [far.gather_pieces(far_maps)]
 
     att = part
-    for offsets in turns:
+    for offsets in up_turns:
         att, stats = call(
             functools.partial(attend_kernel, offsets, pieces, each),
             1,
@@ -526,19 +547,19 @@
         [vmem] * 4,
         [narrow] + [jax.ShapeDtypeStruct((groups, each * D, D), F32)] * pieces,
         [tile32, tile32, pltpu.VMEM((heads, groups, D, D), F32)],
-    )(query_rows, att, scaled, stats)
+    )(q_turned, att, scaled, stats)
 
     if not far.fast:
         map_grads = far.split_pieces(map_grads[0])
 
     query_gradient = call(
-        functools.partial(query_kernel, pieces, each),
+        functools.partial(query_kernel, pair, pieces, each),
         3,
         [smem] + [vmem] * (4 + pieces),
         [narrow],
-        [pltpu.VMEM((heads, groups, D, D), F32), tile16, tile32],
-        grid=(heads,),
-        out_specs=[pl.BlockSpec((tokens, D), lambda h: (0, h))],
+        [pltpu.VMEM((heads, groups, D, D), F32), tiles16, tiles32],
+        grid=(heads // pair,),
+        out_specs=[pl.BlockSpec((tokens, pair * D), lambda h: (0, h))],
     )(codes, key_rows, value_rows, grad, maps, *far_maps)[0]
     normed = call(
         functools.partial(normed_kernel, features),
@@ -549,7 +570,11 @@
         out_specs=[pl.BlockSpec((WIDE, width), lambda i: (i, 0))],
     )(att, stats, gain)[0]
     key_in, readers = call(
-        key_kernel, 4, [smem] + [vmem] * 3, [wide, jax.ShapeDtypeStruct((heads, chunks, D, D), BF16)], [tile16, tile32]
+        functools.partial(key_kernel, pair),
+        4,
+        [smem] + [vmem] * 3,
+        [wide, jax.ShapeDtypeStruct((heads, chunks, D, D), BF16)],
+        [tiles16, tiles32],
     )(codes, query_rows, value_rows, grad)
     value_in = call(value_kernel, 2, [vmem] * 4, [wide])(key_rows, grad, att_t, readers)[0]
 
@@ -558,12 +583,12 @@
         state_grads = [far.gather_pieces(state_grads)]
 
     done = []
-    for offsets in turns:
+    for offsets in down_turns:
         base, count = offsets[0], len(offsets)
         block = pl.BlockSpec((tokens, each * D), lambda j, pref, base=base: (0, (base + j) ^ pref[0]))
         done = call(
             functools.partial(outer_kernel, base, count, each),
-            2 / len(turns),
+            2 / len(down_turns),
             None,
             [narrow, narrow],
             grid_spec=pltpu.PrefetchScalarGridSpec(

time: 89.8 us -> 88.3 us (0.983)
  Pallas kernels: 38.6 us -> 37.5 us
    pallas_call x4 -> x6, Pallas kernels: 18.3 us -> 17.3 us  [the longest x3 7 us: local(): call(functools.partial(outer_kernel, base, count, each), 2 / len(down_tur...]
    pallas_call x2 -> x3, Pallas kernels: 2.95 us -> 3.63 us  [local(): call(functools.partial(attend_kernel, offsets, pieces, each), 1, [vmem] *...]
  transfers between devices with their start and end apart: 17 -> 17, of which waited for: 9 -> 10; matrix products, arithmetic and copies ran while one was open for 0% -> 0% of each run, Pallas kernels for 32% -> 32%
where the time goes in v3:
time: 88.3 us; the launch traced here: 88.1 us
  Pallas kernels  37.5 us (42%)
  waiting for transfers between devices  26.7 us (30%)
  starting transfers between devices  21.7 us (25%)
  local copies, waits for them, and re-layouts  0.95 us (1%)
    ppermute x17, waiting for transfers between devices, exchange(): return lax.ppermute(x, axis, [(i, i ^ distance) for i in range(count)])  26.7 us
    ppermute x17, starting transfers between devices, exchange(): return lax.ppermute(x, axis, [(i, i ^ distance) for i in range(count)])  21.7 us
    pallas_call x3, Pallas kernels, local(): call(functools.partial(outer_kernel, base, count, each), 2 / len(down_tur...  7 us
    pallas_call x1, Pallas kernels, local(): call(functools.partial(inside_kernel, pair), 5, [smem, vmem, vmem, vmem],...  5.99 us
    pallas_call x1, Pallas kernels, local(): call(functools.partial(key_kernel, pair), 4, [smem] + [vmem] * 3, [wide,...  4.84 us
    pallas_call x1, Pallas kernels, local(): call(functools.partial(query_kernel, pair, pieces, each), 3, [smem] + [vm...  4.45 us
    pallas_call x3, Pallas kernels, local(): call(functools.partial(attend_kernel, offsets, pieces, each), 1, [vmem] *...  3.63 us
    pallas_call x1, Pallas kernels, local(): call(functools.partial(state_kernel, pieces, each, (first_far, far.bits))...  3.5 us
  transfers between devices with their start and end apart: 17, of which 10 were waited for; matrix products, arithmetic and copies ran while one was open for 0% of the time, Pallas kernels for 32%

profile of v3, /device:TPU:0, one launch (start us, length us, event | category | flops | bytes accessed | tf_op | source)
XLA Modules:
  0.0 88.1 jit_solution(3685763182726207676)
XLA Ops:
  0.7 3.5 %shard_map.94 = (f32[264,128]{1,0:T(8,128)}, f32[264,128]{1,0:T(8,128)}, f32[264,128]{1,0:T(8,128)}, f32[264,128]{1,0:T(8,128)}) custom-call(s32[1,8,20]{2,1,0:T(8,128)} %bitcast.238, bf16[1024,1024]{1,0:T(8,128)(2,1)} %k.11, bf16[1024,1024]{1,0:T(8,128)(2,1)} %v.11), custom_call_target="tpu_custom_call" | custom-call | flops 268435456 | bytes 8388608 | tf_op jit(solution)/shard_map/pallas_call | solution.py:482
  4.2 3.0 %collective-permute-start = (f32[264,128]{1,0:T(8,128)}, f32[264,128]{1,0:T(8,128)S(1)}, u32[]{:S(2)}, u32[]{:S(2)}) collective-permute-start(f32[264,128]{1,0:T(8,128)} %get-tuple-element.43), channel_id=1, source_target_pairs={{0,2},{2,0},{4,6},{6,4},{8,10},{10,8},{12,14},{14,12},{16,18},{18,... | collective-permute-start | bytes 405512 | tf_op jit(solution)/shard_map/ppermute | solution.py:353
  7.2 1.5 %collective-permute-start.1 = (f32[264,128]{1,0:T(8,128)}, f32[264,128]{1,0:T(8,128)S(1)}, u32[]{:S(2)}, u32[]{:S(2)}) collective-permute-start(f32[264,128]{1,0:T(8,128)} %get-tuple-element.44), channel_id=1, source_target_pairs={{0,4},{2,6},{4,0},{6,2},{8,12},{10,14},{12,8},{14,10},{16,20},{18,... | collective-permute-start | bytes 405512 | tf_op jit(solution)/shard_map/ppermute | solution.py:353
  11.5 3.9 %collective-permute-done.1 = f32[264,128]{1,0:T(8,128)S(1)} collective-permute-done((f32[264,128]{1,0:T(8,128)}, f32[264,128]{1,0:T(8,128)S(1)}, u32[]{:S(2)}, u32[]{:S(2)}) %collective-permute-start.1) | collective-permute-done | bytes 135200 | tf_op jit(solution)/shard_map/ppermute | solution.py:353
  15.4 1.6 %collective-permute-start.3 = (f32[256,128]{1,0:T(8,128)S(1)}, f32[256,128]{1,0:T(8,128)S(1)}, u32[]{:S(2)}, u32[]{:S(2)}) collective-permute-start(f32[256,128]{1,0:T(8,128)S(1)} %add_add_fusion), channel_id=1, source_target_pairs={{0,8},{2,10},{4,12},{6,14},{8,0},{10,2},{12,4},{14,6},{16,24},{18,... | collective-permute-start | bytes 393224 | tf_op jit(solution)/shard_map/ppermute | solution.py:353
  17.0 3.4 %collective-permute-done.3 = f32[256,128]{1,0:T(8,128)S(1)} collective-permute-done((f32[256,128]{1,0:T(8,128)S(1)}, f32[256,128]{1,0:T(8,128)S(1)}, u32[]{:S(2)}, u32[]{:S(2)}) %collective-permute-start.3) | collective-permute-done | bytes 131104 | tf_op jit(solution)/shard_map/ppermute | solution.py:353
  20.4 2.7 %collective-permute-start.4 = (f32[256,128]{1,0:T(8,128)S(1)}, f32[256,128]{1,0:T(8,128)S(1)}, u32[]{:S(2)}, u32[]{:S(2)}) collective-permute-start(f32[256,128]{1,0:T(8,128)S(1)} %add.227), channel_id=1, source_target_pairs={{0,16},{2,18},{4,20},{6,22},{8,24},{10,26},{12,28},{14,30},{16,0},... | collective-permute-start | bytes 393224 | tf_op jit(solution)/shard_map/ppermute | solution.py:353
  23.1 4.7 %collective-permute-done.4 = f32[256,128]{1,0:T(8,128)S(1)} collective-permute-done((f32[256,128]{1,0:T(8,128)S(1)}, f32[256,128]{1,0:T(8,128)S(1)}, u32[]{:S(2)}, u32[]{:S(2)}) %collective-permute-start.4) | collective-permute-done | bytes 131104 | tf_op jit(solution)/shard_map/ppermute | solution.py:353
  31.7 6.0 %shard_map.93 = (f32[1024,1024]{1,0:T(8,128)S(1)}, bf16[8,8,128,128]{3,2,1,0:T(8,128)(2,1)S(1)}, bf16[1024,1024]{1,0:T(8,128)(2,1)S(1)}) custom-call(s32[1,8,20]{2,1,0:T(8,128)S(1)} %bitcast.239, bf16[1024,1024]{1,0:T(8,128)(2,1)S(1)} %copy-done.2, bf16[1024,1024]{1,0:T(8,128)(2,1)S(1)} %copy-done, bf16[1024,1024]{1,0:T(8,128)(2,1)S(1)} %copy-done.1), custom_call_target="tpu_custom_call" | custom-call | flops 1342177280 | bytes 8388608 | tf_op jit(solution)/shard_map/pallas_call | solution.py:512
  42.7 1.8 %shard_map.101 = (bf16[1024,1024]{1,0:T(8,128)(2,1)S(1)}, f32[1,256,128]{2,1,0:T(8,128)S(1)}, f32[1,256,128]{2,1,0:T(8,128)S(1)}, f32[1,256,128]{2,1,0:T(8,128)S(1)}, f32[1,256,128]{2,1,0:T(8,128)S(1)}) custom-call(bf16[1024,1024]{1,0:T(8,128)(2,1)S(1)} %shard_map.100.q_turned, f32[1024,1024]{1,0:T(8,128)S(1)} %get-tuple-element.50.att, ...), custom_call_target="tpu_custom_call" | custom-call | flops 268435456 | bytes 8388608 | tf_op jit(solution)/shard_map/pallas_call | solution.py:544
  48.1 2.9 %collective-permute-done.9 = f32[1,256,128]{2,1,0:T(8,128)S(1)} collective-permute-done((f32[1,256,128]{2,1,0:T(8,128)S(1)}, f32[1,256,128]{2,1,0:T(8,128)S(1)}, u32[]{:S(2)}, u32[]{:S(2)}) %collective-permute-start.9) | collective-permute-done | bytes 131104 | tf_op jit(solution)/shard_map/ppermute | solution.py:353
  50.9 1.8 %collective-permute-done.10 = f32[1,256,128]{2,1,0:T(8,128)S(1)} collective-permute-done((f32[1,256,128]{2,1,0:T(8,128)S(1)}, f32[1,256,128]{2,1,0:T(8,128)S(1)}, u32[]{:S(2)}, u32[]{:S(2)}) %collective-permute-start.10) | collective-permute-done | bytes 131104 | tf_op jit(solution)/shard_map/ppermute | solution.py:353
  52.7 1.8 %collective-permute-done.11 = f32[1,256,128]{2,1,0:T(8,128)S(1)} collective-permute-done((f32[1,256,128]{2,1,0:T(8,128)S(1)}, f32[1,256,128]{2,1,0:T(8,128)S(1)}, u32[]{:S(2)}, u32[]{:S(2)}) %collective-permute-start.11) | collective-permute-done | bytes 131104 | tf_op jit(solution)/shard_map/ppermute | solution.py:353
  54.6 1.7 %collective-permute-start.12 = (f32[256,128]{1,0:T(8,128)S(1)}, f32[256,128]{1,0:T(8,128)S(1)}, u32[]{:S(2)}, u32[]{:S(2)}) collective-permute-start(f32[256,128]{1,0:T(8,128)S(1)} %fusion.13), channel_id=1, source_target_pairs={{0,16},{2,18},{4,20},{6,22},{8,24},{10,26},{12,28},{14,30},{16,0},... | collective-permute-start | bytes 393224 | tf_op jit(solution)/shard_map/ppermute | solution.py:353
  56.2 7.0 %collective-permute-done.12 = f32[256,128]{1,0:T(8,128)S(1)} collective-permute-done((f32[256,128]{1,0:T(8,128)S(1)}, f32[256,128]{1,0:T(8,128)S(1)}, u32[]{:S(2)}, u32[]{:S(2)}) %collective-permute-start.12) | collective-permute-done | bytes 131104 | tf_op jit(solution)/shard_map/ppermute | solution.py:353
  63.4 4.8 %shard_map.103 = (f32[1024,1024]{1,0:T(8,128)S(1)}, bf16[8,8,128,128]{3,2,1,0:T(8,128)(2,1)S(1)}) custom-call(s32[1,8,20]{2,1,0:T(8,128)S(1)} %bitcast.240, bf16[1024,1024]{1,0:T(8,128)(2,1)S(1)} %copy-done.2, bf16[1024,1024]{1,0:T(8,128)(2,1)S(1)} %copy-done.1, bf16[1024,1024]{1,0:T(8,128)(2,1)S(1)} %get-tuple-element.52.grad), custom_call_target="tpu_custom_call" | custom-call | flops 1073741824 | bytes 8388608 | tf_op jit(solution)/shard_map/pallas_call | solution.py:572
  68.5 2.9 %shard_map.104.value_in = f32[1024,1024]{1,0:T(8,128)S(1)} custom-call(bf16[1024,1024]{1,0:T(8,128)(2,1)S(1)} %copy-done, bf16[1024,1024]{1,0:T(8,128)(2,1)S(1)} %get-tuple-element.52.grad, bf16[1024,1024]{1,0:T(8,128)(2,1)S(1)} %get-tuple-element.56.att_t, bf16[8,8,128,128]{3,2,1,0:T(8,128)(2,1)S(1)} %get-tuple-element.57.readers), custom_call_target="tpu_custom_call" | custom-call | flops 536870912 | bytes 8388608 | tf_op jit(solution)/shard_map/pallas_call | solution.py:579
  71.4 1.7 %collective-permute-start.15 = (f32[256,128]{1,0:T(8,128)S(1)}, f32[256,128]{1,0:T(8,128)S(1)}, u32[]{:S(2)}, u32[]{:S(2)}) collective-permute-start(f32[256,128]{1,0:T(8,128)S(1)} %get-tuple-element.76), channel_id=1, source_target_pairs={{0,6},{2,4},{4,2},{6,0},{8,14},{10,12},{12,10},{14,8},{16,22},{18,... | collective-permute-start | bytes 393224 | tf_op jit(solution)/shard_map/ppermute | solution.py:353
  73.1 1.9 %collective-permute-start.14 = (f32[256,128]{1,0:T(8,128)S(1)}, f32[256,128]{1,0:T(8,128)S(1)}, u32[]{:S(2)}, u32[]{:S(2)}) collective-permute-start(f32[256,128]{1,0:T(8,128)S(1)} %fusion.28), channel_id=1, source_target_pairs={{0,4},{2,6},{4,0},{6,2},{8,12},{10,14},{12,8},{14,10},{16,20},{18,... | collective-permute-start | bytes 393224 | tf_op jit(solution)/shard_map/ppermute | solution.py:353
  75.0 1.6 %shard_map.99 = bf16[1024,1024]{1,0:T(8,128)(2,1)} custom-call(f32[1024,1024]{1,0:T(8,128)S(1)} %get-tuple-element.50.att, f32[2,1024]{1,0:T(2,128)S(1)} %add.245.stats, f32[1,1024]{1,0:T(1,128)S(1)} %bitcast.243), custom_call_target="tpu_custom_call" | custom-call | flops 268435456 | bytes 8388608 | tf_op jit(solution)/shard_map/pallas_call | solution.py:564
  76.7 4.5 %shard_map.102 = bf16[1024,1024]{1,0:T(8,128)(2,1)} custom-call(s32[1,8,20]{2,1,0:T(8,128)S(1)} %bitcast.241, bf16[1024,1024]{1,0:T(8,128)(2,1)S(1)} %copy-done, bf16[1024,1024]{1,0:T(8,128)(2,1)S(1)} %copy-done.1, bf16[1024,1024]{1,0:T(8,128)(2,1)S(1)} %get-tuple-element.52.grad, bf16[8,8,128,128]{3,2,1,0:T(8,128)(2,1)S(1)} %get-tuple-element.53.maps, ...), custom_call_target="tpu_custom_call" | custom-call | flops 805306368 | bytes 8388608 | tf_op jit(solution)/shard_map/pallas_call | solution.py:555
  81.1 2.2 %shard_map.105 = (bf16[1024,1024]{1,0:T(8,128)(2,1)}, bf16[1024,1024]{1,0:T(8,128)(2,1)}) custom-call(s32[1]{0:T(128)} %get-tuple-element.54.pref, bf16[1024,1024]{1,0:T(8,128)(2,1)S(1)} %copy-done, bf16[1024,1024]{1,0:T(8,128)(2,1)S(1)} %copy-done.1, f32[1024,1024]{1,0:T(8,128)S(1)} %get-tuple-element.55.key_in, f32[1024,1024]{1,0:T(8,128)S(1)} %shard_map.104.value_in, ...), custom_call_target="tpu_custom_call" | custom-call | flops 178956976 | bytes 8388608 | tf_op jit(solution)/shard_map/pallas_call | solution.py:589
  83.3 2.1 %shard_map.106 = (bf16[1024,1024]{1,0:T(8,128)(2,1)}, bf16[1024,1024]{1,0:T(8,128)(2,1)}) custom-call(s32[1]{0:T(128)} %get-tuple-element.54.pref, bf16[1024,1024]{1,0:T(8,128)(2,1)S(1)} %copy-done, bf16[1024,1024]{1,0:T(8,128)(2,1)S(1)} %copy-done.1, f32[1024,1024]{1,0:T(8,128)S(1)} %get-tuple-element.55.key_in, ...), custom_call_target="tpu_custom_call", output_to_operand_aliasing={{0}: (6, {}), {1}: (7, {})} | custom-call | flops 178956976 | bytes 8388608 | tf_op jit(solution)/shard_map/pallas_call | solution.py:589
  85.4 2.7 %shard_map.107 = (bf16[1024,1024]{1,0:T(8,128)(2,1)}, bf16[1024,1024]{1,0:T(8,128)(2,1)}) custom-call(s32[1]{0:T(128)} %get-tuple-element.54.pref, bf16[1024,1024]{1,0:T(8,128)(2,1)S(1)} %copy-done, bf16[1024,1024]{1,0:T(8,128)(2,1)S(1)} %copy-done.1, f32[1024,1024]{1,0:T(8,128)S(1)} %get-tuple-element.55.key_in, ...), custom_call_target="tpu_custom_call", output_to_operand_aliasing={{0}: (7, {}), {1}: (8, {})} | custom-call | flops 178956976 | bytes 8388608 | tf_op jit(solution)/shard_map/pallas_call | solution.py:589
  (56 shorter events, 15.6 us)
Async XLA Ops:
  0.6 8.1 %copy-start.3 = (bf16[1024,1024]{1,0:T(8,128)(2,1)S(1)}, bf16[1024,1024]{1,0:T(8,128)(2,1)}, u32[]{:S(2)}) copy-start(bf16[1024,1024]{1,0:T(8,128)(2,1)} %u) | copy-start | bytes 6291460
  0.6 8.1 %copy-start.6 = (f32[1024]{0:T(1024)S(1)}, f32[1024]{0:T(1024)}, u32[]{:S(2)}) copy-start(f32[1024]{0:T(1024)} %param.10) | copy-start | bytes 12292
  0.7 31.1 %copy-start.2 = (bf16[1024,1024]{1,0:T(8,128)(2,1)S(1)}, bf16[1024,1024]{1,0:T(8,128)(2,1)}, u32[]{:S(2)}) copy-start(bf16[1024,1024]{1,0:T(8,128)(2,1)} %q.11) | copy-start | bytes 6291460
  4.2 7.3 %collective-permute-start = (f32[264,128]{1,0:T(8,128)}, f32[264,128]{1,0:T(8,128)S(1)}, u32[]{:S(2)}, u32[]{:S(2)}) collective-permute-start(f32[264,128]{1,0:T(8,128)} %get-tuple-element.43), channel_id=1, source_target_pairs={{0,2},{2,0},{4,6},{6,4},{8,10},{10,8},{12,14},{14,12},{16,18},{18,... | collective-permute-start | bytes 405512 | tf_op jit(solution)/shard_map/ppermute | solution.py:353
  7.2 8.2 %collective-permute-start.1 = (f32[264,128]{1,0:T(8,128)}, f32[264,128]{1,0:T(8,128)S(1)}, u32[]{:S(2)}, u32[]{:S(2)}) collective-permute-start(f32[264,128]{1,0:T(8,128)} %get-tuple-element.44), channel_id=1, source_target_pairs={{0,4},{2,6},{4,0},{6,2},{8,12},{10,14},{12,8},{14,10},{16,20},{18,... | collective-permute-start | bytes 405512 | tf_op jit(solution)/shard_map/ppermute | solution.py:353
  8.7 6.6 %collective-permute-start.2 = (f32[264,128]{1,0:T(8,128)}, f32[264,128]{1,0:T(8,128)S(1)}, u32[]{:S(2)}, u32[]{:S(2)}) collective-permute-start(f32[264,128]{1,0:T(8,128)} %get-tuple-element.45), channel_id=1, source_target_pairs={{0,6},{2,4},{4,2},{6,0},{8,14},{10,12},{12,10},{14,8},{16,22},{18,... | collective-permute-start | bytes 405512 | tf_op jit(solution)/shard_map/ppermute | solution.py:353
  8.7 0.9 %copy-start.4 = (f32[264,128]{1,0:T(8,128)S(1)}, f32[264,128]{1,0:T(8,128)}, u32[]{:S(2)}) copy-start(f32[264,128]{1,0:T(8,128)} %get-tuple-element.39.send) | copy-start | bytes 405508
  9.7 22.1 %copy-start.1 = (bf16[1024,1024]{1,0:T(8,128)(2,1)S(1)}, bf16[1024,1024]{1,0:T(8,128)(2,1)}, u32[]{:S(2)}) copy-start(bf16[1024,1024]{1,0:T(8,128)(2,1)} %v.11) | copy-start | bytes 6291460
  10.5 21.3 %copy-start = (bf16[1024,1024]{1,0:T(8,128)(2,1)S(1)}, bf16[1024,1024]{1,0:T(8,128)(2,1)}, u32[]{:S(2)}) copy-start(bf16[1024,1024]{1,0:T(8,128)(2,1)} %k.11) | copy-start | bytes 6291460
  10.5 21.3 %copy-start.5 = (s32[1,20,8]{1,2,0:T(8,128)S(1)}, s32[1,20,8]{1,2,0:T(8,128)}, u32[]{:S(2)}) copy-start(s32[1,20,8]{1,2,0:T(8,128)} %param.9) | copy-start | bytes 1924
  15.4 5.0 %collective-permute-start.3 = (f32[256,128]{1,0:T(8,128)S(1)}, f32[256,128]{1,0:T(8,128)S(1)}, u32[]{:S(2)}, u32[]{:S(2)}) collective-permute-start(f32[256,128]{1,0:T(8,128)S(1)} %add_add_fusion), channel_id=1, source_target_pairs={{0,8},{2,10},{4,12},{6,14},{8,0},{10,2},{12,4},{14,6},{16,24},{18,... | collective-permute-start | bytes 393224 | tf_op jit(solution)/shard_map/ppermute | solution.py:353
  20.4 7.3 %collective-permute-start.4 = (f32[256,128]{1,0:T(8,128)S(1)}, f32[256,128]{1,0:T(8,128)S(1)}, u32[]{:S(2)}, u32[]{:S(2)}) collective-permute-start(f32[256,128]{1,0:T(8,128)S(1)} %add.227), channel_id=1, source_target_pairs={{0,16},{2,18},{4,20},{6,22},{8,24},{10,26},{12,28},{14,30},{16,0},... | collective-permute-start | bytes 393224 | tf_op jit(solution)/shard_map/ppermute | solution.py:353
  27.9 9.9 %collective-permute-start.5 = (f32[1,256,128]{2,1,0:T(8,128)S(1)}, f32[1,256,128]{2,1,0:T(8,128)S(1)}, u32[]{:S(2)}, u32[]{:S(2)}) collective-permute-start(f32[1,256,128]{2,1,0:T(8,128)S(1)} %bitcast.245), channel_id=1, source_target_pairs={{0,2},{2,0},{4,6},{6,4},{8,10},{10,8},{12,14},{14,12},{16,18},{18,... | collective-permute-start | bytes 393224 | tf_op jit(solution)/shard_map/ppermute | solution.py:353
  29.3 9.9 %collective-permute-start.6 = (f32[1,256,128]{2,1,0:T(8,128)S(1)}, f32[1,256,128]{2,1,0:T(8,128)S(1)}, u32[]{:S(2)}, u32[]{:S(2)}) collective-permute-start(f32[1,256,128]{2,1,0:T(8,128)S(1)} %bitcast.246), channel_id=1, source_target_pairs={{0,4},{2,6},{4,0},{6,2},{8,12},{10,14},{12,8},{14,10},{16,20},{18,... | collective-permute-start | bytes 393224 | tf_op jit(solution)/shard_map/ppermute | solution.py:353
  30.2 10.0 %collective-permute-start.7 = (f32[1,256,128]{2,1,0:T(8,128)S(1)}, f32[1,256,128]{2,1,0:T(8,128)S(1)}, u32[]{:S(2)}, u32[]{:S(2)}) collective-permute-start(f32[1,256,128]{2,1,0:T(8,128)S(1)} %bitcast.244), channel_id=1, source_target_pairs={{0,6},{2,4},{4,2},{6,0},{8,14},{10,12},{12,10},{14,8},{16,22},{18,... | collective-permute-start | bytes 393224 | tf_op jit(solution)/shard_map/ppermute | solution.py:353
  41.4 1.2 %collective-permute-start.8 = (f32[2,1024]{1,0:T(2,128)S(1)}, f32[2,1024]{1,0:T(2,128)S(1)}, u32[]{:S(2)}, u32[]{:S(2)}) collective-permute-start(f32[2,1024]{1,0:T(2,128)S(1)} %get-tuple-element.51), channel_id=1, source_target_pairs={{0,1},{1,0},{2,3},{3,2},{4,5},{5,4},{6,7},{7,6},{8,9},{9,8},{10,11... | collective-permute-start | bytes 24584 | tf_op jit(solution)/shard_map/ppermute | solution.py:353
  44.5 6.4 %collective-permute-start.9 = (f32[1,256,128]{2,1,0:T(8,128)S(1)}, f32[1,256,128]{2,1,0:T(8,128)S(1)}, u32[]{:S(2)}, u32[]{:S(2)}) collective-permute-start(f32[1,256,128]{2,1,0:T(8,128)S(1)} %get-tuple-element.59), channel_id=1, source_target_pairs={{0,2},{2,0},{4,6},{6,4},{8,10},{10,8},{12,14},{14,12},{16,18},{18,... | collective-permute-start | bytes 393224 | tf_op jit(solution)/shard_map/ppermute | solution.py:353
  45.7 7.0 %collective-permute-start.10 = (f32[1,256,128]{2,1,0:T(8,128)S(1)}, f32[1,256,128]{2,1,0:T(8,128)S(1)}, u32[]{:S(2)}, u32[]{:S(2)}) collective-permute-start(f32[1,256,128]{2,1,0:T(8,128)S(1)} %get-tuple-element.60), channel_id=1, source_target_pairs={{0,4},{2,6},{4,0},{6,2},{8,12},{10,14},{12,8},{14,10},{16,20},{18,... | collective-permute-start | bytes 393224 | tf_op jit(solution)/shard_map/ppermute | solution.py:353
  46.6 7.9 %collective-permute-start.11 = (f32[1,256,128]{2,1,0:T(8,128)S(1)}, f32[1,256,128]{2,1,0:T(8,128)S(1)}, u32[]{:S(2)}, u32[]{:S(2)}) collective-permute-start(f32[1,256,128]{2,1,0:T(8,128)S(1)} %get-tuple-element.61), channel_id=1, source_target_pairs={{0,6},{2,4},{4,2},{6,0},{8,14},{10,12},{12,10},{14,8},{16,22},{18,... | collective-permute-start | bytes 393224 | tf_op jit(solution)/shard_map/ppermute | solution.py:353
  54.6 8.7 %collective-permute-start.12 = (f32[256,128]{1,0:T(8,128)S(1)}, f32[256,128]{1,0:T(8,128)S(1)}, u32[]{:S(2)}, u32[]{:S(2)}) collective-permute-start(f32[256,128]{1,0:T(8,128)S(1)} %fusion.13), channel_id=1, source_target_pairs={{0,16},{2,18},{4,20},{6,22},{8,24},{10,26},{12,28},{14,30},{16,0},... | collective-permute-start | bytes 393224 | tf_op jit(solution)/shard_map/ppermute | solution.py:353
  63.3 5.1 %collective-permute-start.13 = (f32[256,128]{1,0:T(8,128)S(1)}, f32[256,128]{1,0:T(8,128)S(1)}, u32[]{:S(2)}, u32[]{:S(2)}) collective-permute-start(f32[256,128]{1,0:T(8,128)S(1)} %fusion.10), channel_id=1, source_target_pairs={{0,8},{2,10},{4,12},{6,14},{8,0},{10,2},{12,4},{14,6},{16,24},{18,... | collective-permute-start | bytes 393224 | tf_op jit(solution)/shard_map/ppermute | solution.py:353
  68.5 14.8 %collective-permute-start.16 = (f32[256,128]{1,0:T(8,128)S(1)}, f32[256,128]{1,0:T(8,128)S(1)}, u32[]{:S(2)}, u32[]{:S(2)}) collective-permute-start(f32[256,128]{1,0:T(8,128)S(1)} %get-tuple-element.75), channel_id=1, source_target_pairs={{0,2},{2,0},{4,6},{6,4},{8,10},{10,8},{12,14},{14,12},{16,18},{18,... | collective-permute-start | bytes 393224 | tf_op jit(solution)/shard_map/ppermute | solution.py:353
  71.4 14.0 %collective-permute-start.15 = (f32[256,128]{1,0:T(8,128)S(1)}, f32[256,128]{1,0:T(8,128)S(1)}, u32[]{:S(2)}, u32[]{:S(2)}) collective-permute-start(f32[256,128]{1,0:T(8,128)S(1)} %get-tuple-element.76), channel_id=1, source_target_pairs={{0,6},{2,4},{4,2},{6,0},{8,14},{10,12},{12,10},{14,8},{16,22},{18,... | collective-permute-start | bytes 393224 | tf_op jit(solution)/shard_map/ppermute | solution.py:353
  73.1 12.3 %collective-permute-start.14 = (f32[256,128]{1,0:T(8,128)S(1)}, f32[256,128]{1,0:T(8,128)S(1)}, u32[]{:S(2)}, u32[]{:S(2)}) collective-permute-start(f32[256,128]{1,0:T(8,128)S(1)} %fusion.28), channel_id=1, source_target_pairs={{0,4},{2,6},{4,0},{6,2},{8,12},{10,14},{12,8},{14,10},{16,20},{18,... | collective-permute-start | bytes 393224 | tf_op jit(solution)/shard_map/ppermute | solution.py:353

commit v4 on v3

--- a/solution.py
+++ b/solution.py
@@ -202,14 +202,12 @@
     def attend(heads):
         cols = [slice(h * D, (h + 1) * D) for h in heads]
 
-        @pl.loop(0, q.shape[0] // WIDE)
-        def _(step):
-            r = pl.ds(pl.multiple_of(step * WIDE, WIDE), WIDE)
-            g = (step * WIDE) // GROUP
+        for start in range(0, q.shape[0], WIDE):
+            r = slice(start, start + WIDE)
             for n, c in enumerate(cols):
-                att[r, c] = part[r, c] + dot(q[r, c], maps[n, g], 1, 0)
-            for block in range(WIDE // CHUNK):
-                b = pl.ds(pl.multiple_of(step * WIDE + block * CHUNK, CHUNK), CHUNK)
+                att[r, c] = part[r, c] + dot(q[r, c], maps[n, start // GROUP], 1, 0)
+            for begin in range(start, start + WIDE, CHUNK):
+                b = slice(begin, begin + CHUNK)
                 squares = dots = None
                 for n, c in enumerate(cols):
                     a = att[b, c]

time: 88.3 us -> 87.3 us (0.989)
  Pallas kernels: 37.5 us -> 36.5 us
    pallas_call x3, Pallas kernels: 3.63 us -> 2.62 us  [local(): call(functools.partial(attend_kernel, offsets, pieces, each), 1, [vmem] *...]
where the time goes in v4:
time: 87.3 us; the launch traced here: 87.1 us
  Pallas kernels  36.5 us (42%)
  waiting for transfers between devices  26.7 us (31%)
  starting transfers between devices  21.7 us (25%)
  local copies, waits for them, and re-layouts  0.95 us (1%)
    ppermute x17, waiting for transfers between devices, exchange(): return lax.ppermute(x, axis, [(i, i ^ distance) for i in range(count)])  26.7 us
    ppermute x17, starting transfers between devices, exchange(): return lax.ppermute(x, axis, [(i, i ^ distance) for i in range(count)])  21.7 us
    pallas_call x3, Pallas kernels, local(): call(functools.partial(outer_kernel, base, count, each), 2 / len(down_tur...  7.01 us
    pallas_call x1, Pallas kernels, local(): call(functools.partial(inside_kernel, pair), 5, [smem, vmem, vmem, vmem],...  5.99 us
    pallas_call x1, Pallas kernels, local(): call(functools.partial(key_kernel, pair), 4, [smem] + [vmem] * 3, [wide,...  4.83 us
    pallas_call x1, Pallas kernels, local(): call(functools.partial(query_kernel, pair, pieces, each), 3, [smem] + [vm...  4.46 us
    pallas_call x1, Pallas kernels, local(): call(functools.partial(state_kernel, pieces, each, (first_far, far.bits))...  3.5 us
    pallas_call x1, Pallas kernels, local(): call(value_kernel, 2, [vmem] * 4, [wide])(key_rows, grad, att_t, readers)[0]  2.85 us
  transfers between devices with their start and end apart: 17, of which 10 were waited for; matrix products, arithmetic and copies ran while one was open for 0% of the time, Pallas kernels for 32%

profile of v4, /device:TPU:0, one launch (start us, length us, event | category | flops | bytes accessed | tf_op | source)
XLA Modules:
  0.0 87.1 jit_solution(9084012547332059487)
XLA Ops:
  0.7 3.5 %shard_map.94 = (f32[264,128]{1,0:T(8,128)}, f32[264,128]{1,0:T(8,128)}, f32[264,128]{1,0:T(8,128)}, f32[264,128]{1,0:T(8,128)}) custom-call(s32[1,8,20]{2,1,0:T(8,128)} %bitcast.238, bf16[1024,1024]{1,0:T(8,128)(2,1)} %k.11, bf16[1024,1024]{1,0:T(8,128)(2,1)} %v.11), custom_call_target="tpu_custom_call" | custom-call | flops 268435456 | bytes 8388608 | tf_op jit(solution)/shard_map/pallas_call | solution.py:480
  4.2 3.0 %collective-permute-start = (f32[264,128]{1,0:T(8,128)}, f32[264,128]{1,0:T(8,128)S(1)}, u32[]{:S(2)}, u32[]{:S(2)}) collective-permute-start(f32[264,128]{1,0:T(8,128)} %get-tuple-element.43), channel_id=1, source_target_pairs={{0,2},{2,0},{4,6},{6,4},{8,10},{10,8},{12,14},{14,12},{16,18},{18,... | collective-permute-start | bytes 405512 | tf_op jit(solution)/shard_map/ppermute | solution.py:351
  7.2 1.5 %collective-permute-start.1 = (f32[264,128]{1,0:T(8,128)}, f32[264,128]{1,0:T(8,128)S(1)}, u32[]{:S(2)}, u32[]{:S(2)}) collective-permute-start(f32[264,128]{1,0:T(8,128)} %get-tuple-element.44), channel_id=1, source_target_pairs={{0,4},{2,6},{4,0},{6,2},{8,12},{10,14},{12,8},{14,10},{16,20},{18,... | collective-permute-start | bytes 405512 | tf_op jit(solution)/shard_map/ppermute | solution.py:351
  11.5 3.9 %collective-permute-done.1 = f32[264,128]{1,0:T(8,128)S(1)} collective-permute-done((f32[264,128]{1,0:T(8,128)}, f32[264,128]{1,0:T(8,128)S(1)}, u32[]{:S(2)}, u32[]{:S(2)}) %collective-permute-start.1) | collective-permute-done | bytes 135200 | tf_op jit(solution)/shard_map/ppermute | solution.py:351
  15.4 1.6 %collective-permute-start.3 = (f32[256,128]{1,0:T(8,128)S(1)}, f32[256,128]{1,0:T(8,128)S(1)}, u32[]{:S(2)}, u32[]{:S(2)}) collective-permute-start(f32[256,128]{1,0:T(8,128)S(1)} %add_add_fusion), channel_id=1, source_target_pairs={{0,8},{2,10},{4,12},{6,14},{8,0},{10,2},{12,4},{14,6},{16,24},{18,... | collective-permute-start | bytes 393224 | tf_op jit(solution)/shard_map/ppermute | solution.py:351
  17.0 3.4 %collective-permute-done.3 = f32[256,128]{1,0:T(8,128)S(1)} collective-permute-done((f32[256,128]{1,0:T(8,128)S(1)}, f32[256,128]{1,0:T(8,128)S(1)}, u32[]{:S(2)}, u32[]{:S(2)}) %collective-permute-start.3) | collective-permute-done | bytes 131104 | tf_op jit(solution)/shard_map/ppermute | solution.py:351
  20.4 2.7 %collective-permute-start.4 = (f32[256,128]{1,0:T(8,128)S(1)}, f32[256,128]{1,0:T(8,128)S(1)}, u32[]{:S(2)}, u32[]{:S(2)}) collective-permute-start(f32[256,128]{1,0:T(8,128)S(1)} %add.227), channel_id=1, source_target_pairs={{0,16},{2,18},{4,20},{6,22},{8,24},{10,26},{12,28},{14,30},{16,0},... | collective-permute-start | bytes 393224 | tf_op jit(solution)/shard_map/ppermute | solution.py:351
  23.1 4.7 %collective-permute-done.4 = f32[256,128]{1,0:T(8,128)S(1)} collective-permute-done((f32[256,128]{1,0:T(8,128)S(1)}, f32[256,128]{1,0:T(8,128)S(1)}, u32[]{:S(2)}, u32[]{:S(2)}) %collective-permute-start.4) | collective-permute-done | bytes 131104 | tf_op jit(solution)/shard_map/ppermute | solution.py:351
  31.7 6.0 %shard_map.93 = (f32[1024,1024]{1,0:T(8,128)S(1)}, bf16[8,8,128,128]{3,2,1,0:T(8,128)(2,1)S(1)}, bf16[1024,1024]{1,0:T(8,128)(2,1)S(1)}) custom-call(s32[1,8,20]{2,1,0:T(8,128)S(1)} %bitcast.239, bf16[1024,1024]{1,0:T(8,128)(2,1)S(1)} %copy-done.2, bf16[1024,1024]{1,0:T(8,128)(2,1)S(1)} %copy-done, bf16[1024,1024]{1,0:T(8,128)(2,1)S(1)} %copy-done.1), custom_call_target="tpu_custom_call" | custom-call | flops 1342177280 | bytes 8388608 | tf_op jit(solution)/shard_map/pallas_call | solution.py:510
  41.7 1.8 %shard_map.101 = (bf16[1024,1024]{1,0:T(8,128)(2,1)S(1)}, f32[1,256,128]{2,1,0:T(8,128)S(1)}, f32[1,256,128]{2,1,0:T(8,128)S(1)}, f32[1,256,128]{2,1,0:T(8,128)S(1)}, f32[1,256,128]{2,1,0:T(8,128)S(1)}) custom-call(bf16[1024,1024]{1,0:T(8,128)(2,1)S(1)} %shard_map.100.q_turned, f32[1024,1024]{1,0:T(8,128)S(1)} %get-tuple-element.50.att, ...), custom_call_target="tpu_custom_call" | custom-call | flops 268435456 | bytes 8388608 | tf_op jit(solution)/shard_map/pallas_call | solution.py:542
  47.1 2.9 %collective-permute-done.9 = f32[1,256,128]{2,1,0:T(8,128)S(1)} collective-permute-done((f32[1,256,128]{2,1,0:T(8,128)S(1)}, f32[1,256,128]{2,1,0:T(8,128)S(1)}, u32[]{:S(2)}, u32[]{:S(2)}) %collective-permute-start.9) | collective-permute-done | bytes 131104 | tf_op jit(solution)/shard_map/ppermute | solution.py:351
  49.9 1.8 %collective-permute-done.10 = f32[1,256,128]{2,1,0:T(8,128)S(1)} collective-permute-done((f32[1,256,128]{2,1,0:T(8,128)S(1)}, f32[1,256,128]{2,1,0:T(8,128)S(1)}, u32[]{:S(2)}, u32[]{:S(2)}) %collective-permute-start.10) | collective-permute-done | bytes 131104 | tf_op jit(solution)/shard_map/ppermute | solution.py:351
  51.7 1.8 %collective-permute-done.11 = f32[1,256,128]{2,1,0:T(8,128)S(1)} collective-permute-done((f32[1,256,128]{2,1,0:T(8,128)S(1)}, f32[1,256,128]{2,1,0:T(8,128)S(1)}, u32[]{:S(2)}, u32[]{:S(2)}) %collective-permute-start.11) | collective-permute-done | bytes 131104 | tf_op jit(solution)/shard_map/ppermute | solution.py:351
  53.5 1.7 %collective-permute-start.12 = (f32[256,128]{1,0:T(8,128)S(1)}, f32[256,128]{1,0:T(8,128)S(1)}, u32[]{:S(2)}, u32[]{:S(2)}) collective-permute-start(f32[256,128]{1,0:T(8,128)S(1)} %fusion.13), channel_id=1, source_target_pairs={{0,16},{2,18},{4,20},{6,22},{8,24},{10,26},{12,28},{14,30},{16,0},... | collective-permute-start | bytes 393224 | tf_op jit(solution)/shard_map/ppermute | solution.py:351
  55.2 7.0 %collective-permute-done.12 = f32[256,128]{1,0:T(8,128)S(1)} collective-permute-done((f32[256,128]{1,0:T(8,128)S(1)}, f32[256,128]{1,0:T(8,128)S(1)}, u32[]{:S(2)}, u32[]{:S(2)}) %collective-permute-start.12) | collective-permute-done | bytes 131104 | tf_op jit(solution)/shard_map/ppermute | solution.py:351
  62.4 4.8 %shard_map.103 = (f32[1024,1024]{1,0:T(8,128)S(1)}, bf16[8,8,128,128]{3,2,1,0:T(8,128)(2,1)S(1)}) custom-call(s32[1,8,20]{2,1,0:T(8,128)S(1)} %bitcast.240, bf16[1024,1024]{1,0:T(8,128)(2,1)S(1)} %copy-done.2, bf16[1024,1024]{1,0:T(8,128)(2,1)S(1)} %copy-done.1, bf16[1024,1024]{1,0:T(8,128)(2,1)S(1)} %get-tuple-element.52.grad), custom_call_target="tpu_custom_call" | custom-call | flops 1073741824 | bytes 8388608 | tf_op jit(solution)/shard_map/pallas_call | solution.py:570
  67.5 2.9 %shard_map.104.value_in = f32[1024,1024]{1,0:T(8,128)S(1)} custom-call(bf16[1024,1024]{1,0:T(8,128)(2,1)S(1)} %copy-done, bf16[1024,1024]{1,0:T(8,128)(2,1)S(1)} %get-tuple-element.52.grad, bf16[1024,1024]{1,0:T(8,128)(2,1)S(1)} %get-tuple-element.56.att_t, bf16[8,8,128,128]{3,2,1,0:T(8,128)(2,1)S(1)} %get-tuple-element.57.readers), custom_call_target="tpu_custom_call" | custom-call | flops 536870912 | bytes 8388608 | tf_op jit(solution)/shard_map/pallas_call | solution.py:577
  70.4 1.7 %collective-permute-start.15 = (f32[256,128]{1,0:T(8,128)S(1)}, f32[256,128]{1,0:T(8,128)S(1)}, u32[]{:S(2)}, u32[]{:S(2)}) collective-permute-start(f32[256,128]{1,0:T(8,128)S(1)} %get-tuple-element.76), channel_id=1, source_target_pairs={{0,6},{2,4},{4,2},{6,0},{8,14},{10,12},{12,10},{14,8},{16,22},{18,... | collective-permute-start | bytes 393224 | tf_op jit(solution)/shard_map/ppermute | solution.py:351
  72.1 1.9 %collective-permute-start.14 = (f32[256,128]{1,0:T(8,128)S(1)}, f32[256,128]{1,0:T(8,128)S(1)}, u32[]{:S(2)}, u32[]{:S(2)}) collective-permute-start(f32[256,128]{1,0:T(8,128)S(1)} %fusion.28), channel_id=1, source_target_pairs={{0,4},{2,6},{4,0},{6,2},{8,12},{10,14},{12,8},{14,10},{16,20},{18,... | collective-permute-start | bytes 393224 | tf_op jit(solution)/shard_map/ppermute | solution.py:351
  74.0 1.6 %shard_map.99 = bf16[1024,1024]{1,0:T(8,128)(2,1)} custom-call(f32[1024,1024]{1,0:T(8,128)S(1)} %get-tuple-element.50.att, f32[2,1024]{1,0:T(2,128)S(1)} %add.245.stats, f32[1,1024]{1,0:T(1,128)S(1)} %bitcast.243), custom_call_target="tpu_custom_call" | custom-call | flops 268435456 | bytes 8388608 | tf_op jit(solution)/shard_map/pallas_call | solution.py:562
  75.6 4.5 %shard_map.102 = bf16[1024,1024]{1,0:T(8,128)(2,1)} custom-call(s32[1,8,20]{2,1,0:T(8,128)S(1)} %bitcast.241, bf16[1024,1024]{1,0:T(8,128)(2,1)S(1)} %copy-done, bf16[1024,1024]{1,0:T(8,128)(2,1)S(1)} %copy-done.1, bf16[1024,1024]{1,0:T(8,128)(2,1)S(1)} %get-tuple-element.52.grad, bf16[8,8,128,128]{3,2,1,0:T(8,128)(2,1)S(1)} %get-tuple-element.53.maps, ...), custom_call_target="tpu_custom_call" | custom-call | flops 805306368 | bytes 8388608 | tf_op jit(solution)/shard_map/pallas_call | solution.py:553
  80.1 2.2 %shard_map.105 = (bf16[1024,1024]{1,0:T(8,128)(2,1)}, bf16[1024,1024]{1,0:T(8,128)(2,1)}) custom-call(s32[1]{0:T(128)} %get-tuple-element.54.pref, bf16[1024,1024]{1,0:T(8,128)(2,1)S(1)} %copy-done, bf16[1024,1024]{1,0:T(8,128)(2,1)S(1)} %copy-done.1, f32[1024,1024]{1,0:T(8,128)S(1)} %get-tuple-element.55.key_in, f32[1024,1024]{1,0:T(8,128)S(1)} %shard_map.104.value_in, ...), custom_call_target="tpu_custom_call" | custom-call | flops 178956976 | bytes 8388608 | tf_op jit(solution)/shard_map/pallas_call | solution.py:587
  82.3 2.1 %shard_map.106 = (bf16[1024,1024]{1,0:T(8,128)(2,1)}, bf16[1024,1024]{1,0:T(8,128)(2,1)}) custom-call(s32[1]{0:T(128)} %get-tuple-element.54.pref, bf16[1024,1024]{1,0:T(8,128)(2,1)S(1)} %copy-done, bf16[1024,1024]{1,0:T(8,128)(2,1)S(1)} %copy-done.1, f32[1024,1024]{1,0:T(8,128)S(1)} %get-tuple-element.55.key_in, ...), custom_call_target="tpu_custom_call", output_to_operand_aliasing={{0}: (6, {}), {1}: (7, {})} | custom-call | flops 178956976 | bytes 8388608 | tf_op jit(solution)/shard_map/pallas_call | solution.py:587
  84.4 2.7 %shard_map.107 = (bf16[1024,1024]{1,0:T(8,128)(2,1)}, bf16[1024,1024]{1,0:T(8,128)(2,1)}) custom-call(s32[1]{0:T(128)} %get-tuple-element.54.pref, bf16[1024,1024]{1,0:T(8,128)(2,1)S(1)} %copy-done, bf16[1024,1024]{1,0:T(8,128)(2,1)S(1)} %copy-done.1, f32[1024,1024]{1,0:T(8,128)S(1)} %get-tuple-element.55.key_in, ...), custom_call_target="tpu_custom_call", output_to_operand_aliasing={{0}: (7, {}), {1}: (8, {})} | custom-call | flops 178956976 | bytes 8388608 | tf_op jit(solution)/shard_map/pallas_call | solution.py:587
  (56 shorter events, 14.6 us)
Async XLA Ops:
  0.6 8.1 %copy-start.3 = (bf16[1024,1024]{1,0:T(8,128)(2,1)S(1)}, bf16[1024,1024]{1,0:T(8,128)(2,1)}, u32[]{:S(2)}) copy-start(bf16[1024,1024]{1,0:T(8,128)(2,1)} %u) | copy-start | bytes 6291460
  0.6 8.1 %copy-start.6 = (f32[1024]{0:T(1024)S(1)}, f32[1024]{0:T(1024)}, u32[]{:S(2)}) copy-start(f32[1024]{0:T(1024)} %param.10) | copy-start | bytes 12292
  0.7 31.1 %copy-start.2 = (bf16[1024,1024]{1,0:T(8,128)(2,1)S(1)}, bf16[1024,1024]{1,0:T(8,128)(2,1)}, u32[]{:S(2)}) copy-start(bf16[1024,1024]{1,0:T(8,128)(2,1)} %q.11) | copy-start | bytes 6291460
  4.2 7.3 %collective-permute-start = (f32[264,128]{1,0:T(8,128)}, f32[264,128]{1,0:T(8,128)S(1)}, u32[]{:S(2)}, u32[]{:S(2)}) collective-permute-start(f32[264,128]{1,0:T(8,128)} %get-tuple-element.43), channel_id=1, source_target_pairs={{0,2},{2,0},{4,6},{6,4},{8,10},{10,8},{12,14},{14,12},{16,18},{18,... | collective-permute-start | bytes 405512 | tf_op jit(solution)/shard_map/ppermute | solution.py:351
  7.2 8.2 %collective-permute-start.1 = (f32[264,128]{1,0:T(8,128)}, f32[264,128]{1,0:T(8,128)S(1)}, u32[]{:S(2)}, u32[]{:S(2)}) collective-permute-start(f32[264,128]{1,0:T(8,128)} %get-tuple-element.44), channel_id=1, source_target_pairs={{0,4},{2,6},{4,0},{6,2},{8,12},{10,14},{12,8},{14,10},{16,20},{18,... | collective-permute-start | bytes 405512 | tf_op jit(solution)/shard_map/ppermute | solution.py:351
  8.7 6.6 %collective-permute-start.2 = (f32[264,128]{1,0:T(8,128)}, f32[264,128]{1,0:T(8,128)S(1)}, u32[]{:S(2)}, u32[]{:S(2)}) collective-permute-start(f32[264,128]{1,0:T(8,128)} %get-tuple-element.45), channel_id=1, source_target_pairs={{0,6},{2,4},{4,2},{6,0},{8,14},{10,12},{12,10},{14,8},{16,22},{18,... | collective-permute-start | bytes 405512 | tf_op jit(solution)/shard_map/ppermute | solution.py:351
  8.7 0.9 %copy-start.4 = (f32[264,128]{1,0:T(8,128)S(1)}, f32[264,128]{1,0:T(8,128)}, u32[]{:S(2)}) copy-start(f32[264,128]{1,0:T(8,128)} %get-tuple-element.39.send) | copy-start | bytes 405508
  9.7 22.1 %copy-start.1 = (bf16[1024,1024]{1,0:T(8,128)(2,1)S(1)}, bf16[1024,1024]{1,0:T(8,128)(2,1)}, u32[]{:S(2)}) copy-start(bf16[1024,1024]{1,0:T(8,128)(2,1)} %v.11) | copy-start | bytes 6291460
  10.5 21.3 %copy-start = (bf16[1024,1024]{1,0:T(8,128)(2,1)S(1)}, bf16[1024,1024]{1,0:T(8,128)(2,1)}, u32[]{:S(2)}) copy-start(bf16[1024,1024]{1,0:T(8,128)(2,1)} %k.11) | copy-start | bytes 6291460
  10.5 21.3 %copy-start.5 = (s32[1,20,8]{1,2,0:T(8,128)S(1)}, s32[1,20,8]{1,2,0:T(8,128)}, u32[]{:S(2)}) copy-start(s32[1,20,8]{1,2,0:T(8,128)} %param.9) | copy-start | bytes 1924
  15.4 5.0 %collective-permute-start.3 = (f32[256,128]{1,0:T(8,128)S(1)}, f32[256,128]{1,0:T(8,128)S(1)}, u32[]{:S(2)}, u32[]{:S(2)}) collective-permute-start(f32[256,128]{1,0:T(8,128)S(1)} %add_add_fusion), channel_id=1, source_target_pairs={{0,8},{2,10},{4,12},{6,14},{8,0},{10,2},{12,4},{14,6},{16,24},{18,... | collective-permute-start | bytes 393224 | tf_op jit(solution)/shard_map/ppermute | solution.py:351
  20.4 7.3 %collective-permute-start.4 = (f32[256,128]{1,0:T(8,128)S(1)}, f32[256,128]{1,0:T(8,128)S(1)}, u32[]{:S(2)}, u32[]{:S(2)}) collective-permute-start(f32[256,128]{1,0:T(8,128)S(1)} %add.227), channel_id=1, source_target_pairs={{0,16},{2,18},{4,20},{6,22},{8,24},{10,26},{12,28},{14,30},{16,0},... | collective-permute-start | bytes 393224 | tf_op jit(solution)/shard_map/ppermute | solution.py:351
  27.9 9.9 %collective-permute-start.5 = (f32[1,256,128]{2,1,0:T(8,128)S(1)}, f32[1,256,128]{2,1,0:T(8,128)S(1)}, u32[]{:S(2)}, u32[]{:S(2)}) collective-permute-start(f32[1,256,128]{2,1,0:T(8,128)S(1)} %bitcast.245), channel_id=1, source_target_pairs={{0,2},{2,0},{4,6},{6,4},{8,10},{10,8},{12,14},{14,12},{16,18},{18,... | collective-permute-start | bytes 393224 | tf_op jit(solution)/shard_map/ppermute | solution.py:351
  29.3 9.6 %collective-permute-start.6 = (f32[1,256,128]{2,1,0:T(8,128)S(1)}, f32[1,256,128]{2,1,0:T(8,128)S(1)}, u32[]{:S(2)}, u32[]{:S(2)}) collective-permute-start(f32[1,256,128]{2,1,0:T(8,128)S(1)} %bitcast.246), channel_id=1, source_target_pairs={{0,4},{2,6},{4,0},{6,2},{8,12},{10,14},{12,8},{14,10},{16,20},{18,... | collective-permute-start | bytes 393224 | tf_op jit(solution)/shard_map/ppermute | solution.py:351
  30.2 9.4 %collective-permute-start.7 = (f32[1,256,128]{2,1,0:T(8,128)S(1)}, f32[1,256,128]{2,1,0:T(8,128)S(1)}, u32[]{:S(2)}, u32[]{:S(2)}) collective-permute-start(f32[1,256,128]{2,1,0:T(8,128)S(1)} %bitcast.244), channel_id=1, source_target_pairs={{0,6},{2,4},{4,2},{6,0},{8,14},{10,12},{12,10},{14,8},{16,22},{18,... | collective-permute-start | bytes 393224 | tf_op jit(solution)/shard_map/ppermute | solution.py:351
  40.4 1.2 %collective-permute-start.8 = (f32[2,1024]{1,0:T(2,128)S(1)}, f32[2,1024]{1,0:T(2,128)S(1)}, u32[]{:S(2)}, u32[]{:S(2)}) collective-permute-start(f32[2,1024]{1,0:T(2,128)S(1)} %get-tuple-element.51), channel_id=1, source_target_pairs={{0,1},{1,0},{2,3},{3,2},{4,5},{5,4},{6,7},{7,6},{8,9},{9,8},{10,11... | collective-permute-start | bytes 24584 | tf_op jit(solution)/shard_map/ppermute | solution.py:351
  43.5 6.4 %collective-permute-start.9 = (f32[1,256,128]{2,1,0:T(8,128)S(1)}, f32[1,256,128]{2,1,0:T(8,128)S(1)}, u32[]{:S(2)}, u32[]{:S(2)}) collective-permute-start(f32[1,256,128]{2,1,0:T(8,128)S(1)} %get-tuple-element.59), channel_id=1, source_target_pairs={{0,2},{2,0},{4,6},{6,4},{8,10},{10,8},{12,14},{14,12},{16,18},{18,... | collective-permute-start | bytes 393224 | tf_op jit(solution)/shard_map/ppermute | solution.py:351
  44.7 7.0 %collective-permute-start.10 = (f32[1,256,128]{2,1,0:T(8,128)S(1)}, f32[1,256,128]{2,1,0:T(8,128)S(1)}, u32[]{:S(2)}, u32[]{:S(2)}) collective-permute-start(f32[1,256,128]{2,1,0:T(8,128)S(1)} %get-tuple-element.60), channel_id=1, source_target_pairs={{0,4},{2,6},{4,0},{6,2},{8,12},{10,14},{12,8},{14,10},{16,20},{18,... | collective-permute-start | bytes 393224 | tf_op jit(solution)/shard_map/ppermute | solution.py:351
  45.6 7.9 %collective-permute-start.11 = (f32[1,256,128]{2,1,0:T(8,128)S(1)}, f32[1,256,128]{2,1,0:T(8,128)S(1)}, u32[]{:S(2)}, u32[]{:S(2)}) collective-permute-start(f32[1,256,128]{2,1,0:T(8,128)S(1)} %get-tuple-element.61), channel_id=1, source_target_pairs={{0,6},{2,4},{4,2},{6,0},{8,14},{10,12},{12,10},{14,8},{16,22},{18,... | collective-permute-start | bytes 393224 | tf_op jit(solution)/shard_map/ppermute | solution.py:351
  53.5 8.7 %collective-permute-start.12 = (f32[256,128]{1,0:T(8,128)S(1)}, f32[256,128]{1,0:T(8,128)S(1)}, u32[]{:S(2)}, u32[]{:S(2)}) collective-permute-start(f32[256,128]{1,0:T(8,128)S(1)} %fusion.13), channel_id=1, source_target_pairs={{0,16},{2,18},{4,20},{6,22},{8,24},{10,26},{12,28},{14,30},{16,0},... | collective-permute-start | bytes 393224 | tf_op jit(solution)/shard_map/ppermute | solution.py:351
  62.3 5.1 %collective-permute-start.13 = (f32[256,128]{1,0:T(8,128)S(1)}, f32[256,128]{1,0:T(8,128)S(1)}, u32[]{:S(2)}, u32[]{:S(2)}) collective-permute-start(f32[256,128]{1,0:T(8,128)S(1)} %fusion.10), channel_id=1, source_target_pairs={{0,8},{2,10},{4,12},{6,14},{8,0},{10,2},{12,4},{14,6},{16,24},{18,... | collective-permute-start | bytes 393224 | tf_op jit(solution)/shard_map/ppermute | solution.py:351
  67.5 14.8 %collective-permute-start.16 = (f32[256,128]{1,0:T(8,128)S(1)}, f32[256,128]{1,0:T(8,128)S(1)}, u32[]{:S(2)}, u32[]{:S(2)}) collective-permute-start(f32[256,128]{1,0:T(8,128)S(1)} %get-tuple-element.75), channel_id=1, source_target_pairs={{0,2},{2,0},{4,6},{6,4},{8,10},{10,8},{12,14},{14,12},{16,18},{18,... | collective-permute-start | bytes 393224 | tf_op jit(solution)/shard_map/ppermute | solution.py:351
  70.4 14.0 %collective-permute-start.15 = (f32[256,128]{1,0:T(8,128)S(1)}, f32[256,128]{1,0:T(8,128)S(1)}, u32[]{:S(2)}, u32[]{:S(2)}) collective-permute-start(f32[256,128]{1,0:T(8,128)S(1)} %get-tuple-element.76), channel_id=1, source_target_pairs={{0,6},{2,4},{4,2},{6,0},{8,14},{10,12},{12,10},{14,8},{16,22},{18,... | collective-permute-start | bytes 393224 | tf_op jit(solution)/shard_map/ppermute | solution.py:351
  72.1 12.3 %collective-permute-start.14 = (f32[256,128]{1,0:T(8,128)S(1)}, f32[256,128]{1,0:T(8,128)S(1)}, u32[]{:S(2)}, u32[]{:S(2)}) collective-permute-start(f32[256,128]{1,0:T(8,128)S(1)} %fusion.28), channel_id=1, source_target_pairs={{0,4},{2,6},{4,0},{6,2},{8,12},{10,14},{12,8},{14,10},{16,20},{18,... | collective-permute-start | bytes 393224 | tf_op jit(solution)/shard_map/ppermute | solution.py:351
